TPU v7x, 32 devices: a whole 2x2x4 slice. The times are simulated.
32 devices in a mesh: band: 8 (over z, x), lon: 4 (over y, core).
Axes of the slice: x: 2, y: 2, z: 4, core: 2. Of those that a mesh axis runs over, the one named last changes fastest.
Arguments:
- loads: float32 [2, 2, 32, 4096], P(None, None, 'band', 'lon'), may hold values from -6 to 6
- legendre: bfloat16 [1024, 1024, 32], P('band', 'lon'), may hold values from -1 to 1
- love: float32 [2, 2, 1024], P(None, None, 'lon'), may hold values from -4 to 4
- cycle_weight: float32 [32], replicated, may hold values from 0.25 to 1
- order_list: int32 [1024], replicated, may hold values from 0 to 1023, as said below
- cycle_order: int32 [32], replicated, may hold values from 0 to 31, each once
Outputs:
- sea_response: float32 [2, 2, 32, 4096], P(None, None, 'band', 'lon')
Inputs may be any that keep to these rules, and one draw needn't show every extreme that they name: `order_list`: entries b * 128 to b * 128 + 127 are the orders held by band index b; every order appears once, and the orders of every band index have the same sum. Row j of the grid holds cycle pair cycle_order[j].
All inputs are finite; a program needn't handle non-finite values.
Results may differ from a plain program's by a relative error of at most 0.0041.
Values may be sent and summed in bfloat16 or wider, within the bound.
No kernel may reach another device: no remote copies, remote signals or barrier semaphores. Data moves between devices by JAX's collectives and lax.ppermute only.
A program may use at most 64 MiB of HBM per device.

v0:
```python
import math

import jax
import jax.numpy as jnp
from jax import lax
from jax.sharding import PartitionSpec as P


def cycle_basis(order_ids, positions, total):
    phase = positions[:, None] * order_ids[None, :] % total
    angle = phase.astype(jnp.float32) * (2.0 * math.pi / total)
    scale = 1.0 / math.sqrt(total)
    return (jnp.cos(angle) * scale, jnp.sin(angle) * scale)


def per_device(loads, legendre, love, cycle_weight, order_list, cycle_order):
    highest = lax.Precision.HIGHEST
    owners = lax.axis_size("band")
    lon_count = lax.axis_size("lon")
    band_index = lax.axis_index("band")
    lon_index = lax.axis_index("lon")
    cycle_pairs = loads.shape[2]
    points = loads.shape[3]
    total = points * lon_count
    orders = order_list.shape[0]
    per_owner = legendre.shape[0]
    degree_count = legendre.shape[1]
    northern = legendre.shape[2]
    quarter = per_owner // lon_count
    positions = lon_index * points + jnp.arange(points, dtype=jnp.int32)
    cosine, sine = cycle_basis(order_list, positions, total)
    my_cycles = lax.dynamic_slice_in_dim(cycle_order, band_index * cycle_pairs, cycle_pairs)
    picker = my_cycles[:, None] == jnp.arange(northern, dtype=jnp.int32)[None, :]
    weights = jnp.sum(jnp.where(picker, cycle_weight[None, :], 0.0), axis=1)
    forward = jnp.stack([cosine, -sine], axis=1)
    spectrum = jnp.einsum("fhjx,xrm->fhjrm", loads, forward, precision=highest)
    spectrum = spectrum.reshape(2, 2, cycle_pairs, 2, owners, per_owner)
    summed = lax.psum_scatter(spectrum, "lon", scatter_dimension=5, tiled=True)
    cycle_scale = weights[None, :, None, None, None]
    symmetric = ((summed[:, 0] + summed[:, 1]) * cycle_scale).astype(jnp.bfloat16)
    antisym = ((summed[:, 0] - summed[:, 1]) * cycle_scale).astype(jnp.bfloat16)
    folded = jnp.stack([symmetric, antisym], axis=1)
    slot_width = folded.shape[5]
    outgoing = jnp.transpose(folded, (4, 5, 0, 1, 3, 2)).reshape(owners, slot_width, 8, cycle_pairs)
    arrived = lax.all_to_all(outgoing, "band", split_axis=0, concat_axis=3, tiled=True).reshape(
        slot_width, 8, northern
    )
    columns = lax.all_gather(arrived, "lon", axis=0, tiled=True)
    inverse_rows = jnp.argsort(cycle_order)
    columns_sorted = jnp.take(columns, inverse_rows, axis=2)
    my_orders = lax.dynamic_slice_in_dim(order_list, band_index * per_owner, per_owner)
    degrees = lon_index * degree_count + jnp.arange(degree_count, dtype=jnp.int32)
    analysed = jnp.einsum(
        "olk,ock->ocl", legendre, columns_sorted, preferred_element_type=jnp.float32
    )
    analysed = analysed.reshape(per_owner, 2, 2, 2, degree_count)
    even = (degrees[None, :] - my_orders[:, None]) % 2 == 0
    valid = degrees[None, :] >= my_orders[:, None]
    selected = jnp.where(even[:, None, None, :], analysed[:, :, 0], analysed[:, :, 1])
    selected = selected * valid[:, None, None, :].astype(jnp.float32)
    response = jnp.einsum("gfl,ofrl->ogrl", love, selected, precision=highest).astype(jnp.bfloat16)
    even_part = jnp.where((even & valid)[:, None, None, :], response, jnp.zeros_like(response))
    odd_part = jnp.where((~even & valid)[:, None, None, :], response, jnp.zeros_like(response))
    stacked = jnp.stack([even_part, odd_part], axis=2).reshape(per_owner, 8, degree_count)
    partial_sorted = jnp.einsum(
        "olk,ocl->ock", legendre, stacked, preferred_element_type=jnp.float32
    )
    partial_value = jnp.take(partial_sorted, cycle_order, axis=2)
    reduced = lax.psum_scatter(partial_value, "lon", scatter_dimension=0, tiled=True)
    returned = lax.all_to_all(reduced, "band", split_axis=2, concat_axis=0, tiled=True)
    gathered = lax.all_gather(returned[None], "lon", axis=0, tiled=True).reshape(
        orders, 8, cycle_pairs
    )
    slot_ids = jnp.transpose(order_list.reshape(owners, lon_count, quarter), (1, 0, 2)).reshape(
        orders
    )
    cosine_back, sine_back = cycle_basis(slot_ids, positions, total)
    pieces = gathered.reshape(orders, 2, 2, 2, cycle_pairs)
    cycle_values = jnp.stack(
        [pieces[:, :, 0] + pieces[:, :, 1], pieces[:, :, 0] - pieces[:, :, 1]], axis=2
    )
    factor = jnp.where(slot_ids == 0, 1.0, 2.0).astype(jnp.float32)
    inverse = jnp.stack([cosine_back.T, -sine_back.T], axis=0)
    scaled = cycle_values * factor[:, None, None, None, None]
    return jnp.einsum("sghrp,rsx->ghpx", scaled, inverse, precision=highest)


def solution(mesh):
    return jax.shard_map(
        per_device,
        mesh=mesh,
        in_specs=(
            P(None, None, "band", "lon"),
            P("band", "lon", None),
            P(None, None, "lon"),
            P(),
            P(),
            P(),
        ),
        out_specs=P(None, None, "band", "lon"),
        check_vma=False,
    )
```

profile of v0, /device:TPU:0, one launch (start us, length us, event | category | flops | bytes accessed | tf_op | source)
XLA Modules:
  0.0 154.0 jit_solution(11945288678279143153)
XLA Ops:
  6.6 17.9 %cosine_multiply_fusion.1 = (f32[1024,1,1024]{2,0,1:T(8,128)S(1)}, f32[1024,1,1024]{2,0,1:T(8,128)S(1)}) fusion(s32[1024]{0:T(1024)} %param.10, s32[1024]{0:T(1024)S(1)} %iota_add_fusion), kind=kLoop, calls=%fused_computation.29 | loop fusion | flops 17825792 | bytes 8396800 | tf_op jit(solution)/shard_map/mul | solution.py:13
  24.5 5.1 %fusion.13 = f32[2,2,4,2,1024]{4,2,1,0,3:T(4,128)S(1)} fusion(f32[1024,1,1024]{2,0,1:T(8,128)S(1)} %get-tuple-element.18, f32[1024,1,1024]{2,0,1:T(8,128)S(1)} %get-tuple-element.17, f32[2,2,4,1024]{3,2,1,0:T(4,128)S(1)} %copy-done.1), kind=kOutput, calls=%fused_computation.32 | convolution fusion | flops 404750336 | bytes 8585216 | tf_op jit(solution)/shard_map/fhjx,xrm->fhjrm/dot_general | solution.py:36
  29.6 0.0 copy-start.6
  29.7 0.0 copy-start.2
  29.7 0.1 reshape.474
  29.7 1.9 %copy.68 = f32[2,2,4,2,8,128]{4,2,3,1,0,5:T(4,128)} copy(f32[2,2,4,2,8,128]{5,4,2,1,0,3:T(8,128)S(1)} %reshape.474) | data formatting | bytes 262144
  31.6 4.6 %reshape.504 = f32[128,256]{1,0:T(8,128)} reshape(f32[128,2,2,2,4,8]{5,4,3,2,1,0:T(4,128)} %bitcast.86) | data formatting | bytes 262144
  36.3 0.0 reduce-scatter.7.cloned.1.call-update
  36.3 1.6 %sort.17 = (s32[32]{0:T(128)}, s32[32]{0:T(128)S(1)}) sort(s32[32]{0:T(128)S(1)} %copy-done.5, s32[32]{0:T(128)S(1)} %iota.19), dimensions={0}, to_apply=%region_0.1 | sort | flops 160 | bytes 512 | tf_op jit(solution)/shard_map/jit(argsort)/sort | solution.py:49
  37.9 0.6 compare_and_fusion.2
  38.5 0.5 compare_and_fusion.3
  39.0 0.1 dynamic_slice.7
  39.1 0.2 select_reduce_fusion
  39.3 0.1 dynamic_slice.6
  39.4 0.8 compare_and_fusion.1
  40.2 18.6 %reduce-scatter.7.cloned.1.call-done = f32[32,256]{1,0:T(8,128)} async-done(((f32[128,256]{1,0:T(8,128)}), f32[32,256]{1,0:T(8,128)}) %reduce-scatter.7.cloned.1.call-update) | async-done | bytes 32784
  58.9 1.4 reshape.505
  60.3 0.2 copy.73
  60.5 0.2 copy.74
  60.6 0.1 multiply_convert_fusion.1
  60.8 0.7 reshape.508
  61.5 5.5 %all-to-all-start = ((bf16[8,2,512]{2,1,0:T(2,128)(2,1)}), bf16[8,2,512]{2,1,0:T(2,128)(2,1)S(1)}, u32[]{:S(2)}, u32[]{:S(2)}) async-start(bf16[8,2,512]{2,1,0:T(2,128)(2,1)} %reshape.508), calls=%async_computation | async-start | bytes 32768 | tf_op jit(solution)/shard_map/all_to_all | solution.py:45
  67.0 0.0 reduce-scatter.9.cloned.1.call-start
  67.1 0.1 reshape.479
  67.1 0.2 copy.63
  67.3 0.1 reshape.480
  67.4 6.2 %all-to-all-done = bf16[8,2,512]{2,1,0:T(2,128)(2,1)S(1)} async-done(((bf16[8,2,512]{2,1,0:T(2,128)(2,1)}), bf16[8,2,512]{2,1,0:T(2,128)(2,1)S(1)}, u32[]{:S(2)}, u32[]{:S(2)}) %all-to-all-start) | async-done | bytes 16416 | tf_op jit(solution)/shard_map/all_to_all | solution.py:45
  73.6 0.1 reshape.509
  73.7 0.1 copy.50
  73.8 5.8 %all_gather.6 = bf16[128,8,32]{2,1,0:T(8,128)(2,1)S(1)} all-gather(bf16[32,8,32]{2,1,0:T(8,128)(2,1)S(1)} %copy.50), channel_id=1, replica_groups=mesh['band'=8,'lon'=4] {'lon'}, dimensions={0}, use_global_device_ids=true | all-gather | bytes 81920 | tf_op jit(solution)/shard_map/all_gather | solution.py:48
  79.6 0.2 copy.51
  79.8 0.6 gather_fusion
  80.4 0.8 select_bitcast_fusion.1
  81.2 0.2 copy.52
  81.4 1.4 fusion.36
  82.8 1.8 %reshape.477 = f32[128,2,2,2,256]{4,3,2,1,0:T(2,128)S(1)} reshape(f32[128,8,256]{2,1,0:T(8,128)} %fusion.36) | data formatting | bytes 2097152 | tf_op jit(solution)/shard_map/reshape | solution.py:56
  84.6 1.3 fusion.32
  86.0 1.4 copy.75
  87.3 1.4 copy.76
  88.7 3.7 %fusion.21 = (bf16[128,2,1,2,256]{0,1,3,4,2:T(2,128)(2,1)S(1)}, bf16[128,2,1,2,256]{0,1,3,4,2:T(2,128)(2,1)S(1)}) fusion(pred[128,256]{0,1:T(8,128)(4,1)} %get-tuple-element.21, pred[128,256]{0,1:T(8,128)(4,1)} %get-tuple-element.22, f32[2,2,256,1]{1,0,3,2:T(2,128)S(1)} %copy.63, f32[128,2,1,2,256]{0,1,3,4,2:T(2,128)S(1)} %copy.76, ...), kind=kOutput, calls=%fused_computation.43 | convolution fusion | flops 3801088 | bytes 1806336 | tf_op jit(solution)/shard_map/gfl,ofrl->ogrl/dot_general | solution.py:61
  92.4 0.7 pad_maximum_fusion
  93.1 0.4 copy.56
  93.5 0.6 fusion.18
  94.2 0.2 copy.58
  94.4 0.6 gather_fusion.1
  95.0 0.1 select_bitcast_fusion
  95.1 2.8 %copy.70 = f32[128,8,32]{1,2,0:T(8,128)} copy(f32[128,8,32]{0,1,2:T(8,128)S(1)} %select_bitcast_fusion) | data formatting | bytes 262144
  97.9 3.4 %reshape.506 = f32[128,256]{1,0:T(8,128)} reshape(f32[128,32,8]{2,1,0:T(8,128)} %bitcast.87) | data formatting | bytes 262144
  101.4 0.0 reduce-scatter.9.cloned.1.call-update
  101.4 19.1 %cosine_multiply_fusion = (f32[1,1024,1024]{2,1,0:T(8,128)}, f32[1,1024,1024]{2,1,0:T(8,128)}) fusion(s32[1024]{0:T(1024)S(1)} %reshape.480, s32[1024]{0:T(1024)S(1)} %iota_add_fusion), kind=kLoop, calls=%fused_computation.27 | loop fusion | flops 17825792 | bytes 8396800 | tf_op jit(solution)/shard_map/mul | solution.py:13
  120.5 1.1 reshape.507
  121.6 0.3 copy.71
  121.9 0.7 reshape.510
  122.6 3.3 %all-to-all-start.1 = ((f32[8,1,1024]{2,1,0:T(1,128)}), f32[8,1,1024]{2,1,0:T(1,128)S(1)}, u32[]{:S(2)}, u32[]{:S(2)}) async-start(f32[8,1,1024]{2,1,0:T(1,128)} %reshape.510), calls=%async_computation.1 | async-start | bytes 65536 | tf_op jit(solution)/shard_map/all_to_all | solution.py:70
  126.0 6.6 %all-to-all-done.1 = f32[8,1,1024]{2,1,0:T(1,128)S(1)} async-done(((f32[8,1,1024]{2,1,0:T(1,128)}), f32[8,1,1024]{2,1,0:T(1,128)S(1)}, u32[]{:S(2)}, u32[]{:S(2)}) %all-to-all-start.1) | async-done | bytes 32800 | tf_op jit(solution)/shard_map/all_to_all | solution.py:70
  132.6 0.5 broadcast.549
  133.1 0.7 reduce
  133.8 0.1 reshape.511
  133.9 0.1 copy.59
  134.0 0.1 broadcast_in_dim.95
  134.1 5.4 %all_gather.7 = f32[4,256,8,4]{1,2,3,0:T(8,128)S(1)} all-gather(f32[1,256,8,4]{1,2,3,0:T(8,128)S(1)} %broadcast_in_dim.95), channel_id=1, replica_groups=mesh['band'=8,'lon'=4] {'lon'}, dimensions={0}, use_global_device_ids=true | all-gather | bytes 163840 | tf_op jit(solution)/shard_map/all_gather | solution.py:71
  139.5 0.1 copy.60
  139.6 0.1 reshape_reshape.3
  139.7 7.4 %fusion.14 = f32[2,2,4,1024]{3,2,1,0:T(4,128)} fusion(f32[1,1024,1024]{2,1,0:T(8,128)} %get-tuple-element.20, f32[1,1024,1024]{2,1,0:T(8,128)} %get-tuple-element.19, f32[1024,2,1,2,4]{0,4,3,2,1:T(4,128)S(1)} %get-tuple-element.16, f32[1024,2,1,2,4]{0,4,3,2,1:T(4,128)S(1)} %get-tuple-element.15, f32[1024]{0:T(1024)S(1)} %compare_select_fusion), kind=kOutput, calls=%fused_computation.33 | convolution fusion | flops 404815872 | bytes 8589312 | tf_op jit(solution)/shard_map/sghrp,rsx->ghpx/dot_general | solution.py:85
  (28 shorter events, 0.2 us)
Async XLA Ops:
  6.5 74.9 %copy-start = (bf16[128,256,32]{1,2,0:T(8,128)(2,1)S(1)}, bf16[128,256,32]{1,2,0:T(8,128)(2,1)}, u32[]{:S(2)}) copy-start(bf16[128,256,32]{1,2,0:T(8,128)(2,1)} %param.7) | copy-start | bytes 6291460
  6.5 52.3 %reduce-scatter.7.cloned.1.call-start = ((), (), s32[]{:S(2)}) async-start(), calls=%async_computation.4 | async-start | bytes 163840
  6.5 17.9 %copy-start.1 = (f32[2,2,4,1024]{3,2,1,0:T(4,128)S(1)}, f32[2,2,4,1024]{3,2,1,0:T(4,128)}, u32[]{:S(2)}) copy-start(f32[2,2,4,1024]{3,2,1,0:T(4,128)} %param.6) | copy-start | bytes 196612
  29.6 6.7 %copy-start.5 = (s32[32]{0:T(128)S(1)}, s32[32]{0:T(128)}, u32[]{:S(2)}) copy-start(s32[32]{0:T(128)} %param.11) | copy-start | bytes 388
  29.6 9.5 %copy-start.6 = (f32[32]{0:T(128)S(1)}, f32[32]{0:T(128)}, u32[]{:S(2)}) copy-start(f32[32]{0:T(128)} %param.9) | copy-start | bytes 388
  29.7 9.7 %copy-start.2 = (s32[1024]{0:T(1024)S(1)}, s32[1024]{0:T(1024)}, u32[]{:S(2)}) copy-start(s32[1024]{0:T(1024)} %param.10) | copy-start | bytes 12292
  29.7 37.5 %copy-start.3 = (f32[2,2,256]{2,1,0:T(2,128)S(1)}, f32[2,2,256]{2,1,0:T(2,128)}, u32[]{:S(2)}) copy-start(f32[2,2,256]{2,1,0:T(2,128)} %param.8) | copy-start | bytes 12292
  61.5 12.1 %all-to-all-start = ((bf16[8,2,512]{2,1,0:T(2,128)(2,1)}), bf16[8,2,512]{2,1,0:T(2,128)(2,1)S(1)}, u32[]{:S(2)}, u32[]{:S(2)}) async-start(bf16[8,2,512]{2,1,0:T(2,128)(2,1)} %reshape.508), calls=%async_computation | async-start | bytes 32768 | tf_op jit(solution)/shard_map/all_to_all | solution.py:45
  67.0 53.5 %reduce-scatter.9.cloned.1.call-start = ((), (), s32[]{:S(2)}) async-start(), calls=%async_computation.5 | async-start | bytes 163840
  92.4 2.6 %copy-start.4 = (pred[32]{0:T(512)(128)(4,1)S(1)}, pred[32]{0:T(512)(128)(4,1)}, u32[]{:S(2)}) copy-start(pred[32]{0:T(512)(128)(4,1)} %compare_and_fusion.3) | copy-start | bytes 100
  122.6 10.0 %all-to-all-start.1 = ((f32[8,1,1024]{2,1,0:T(1,128)}), f32[8,1,1024]{2,1,0:T(1,128)S(1)}, u32[]{:S(2)}, u32[]{:S(2)}) async-start(f32[8,1,1024]{2,1,0:T(1,128)} %reshape.510), calls=%async_computation.1 | async-start | bytes 65536 | tf_op jit(solution)/shard_map/all_to_all | solution.py:70
Sparse Core Ops, SparseCore 0:
  36.4 22.3 reduce-scatter.6
  101.5 16.0 reduce-scatter.8
where the time goes:
time: 155 us; the launch traced here: 154 us
  other arithmetic  43.2 us (28%)
  waiting for transfers between devices  31.5 us (20%)
  local copies, waits for them, and re-layouts  27.3 us (18%)
  matrix products  18.2 us (12%)
  between operations  13.7 us (9%)
  blocking collectives  11.2 us (7%)
  starting transfers between devices  8.9 us (6%)
    mul x2, other arithmetic, cycle_basis(): return (jnp.cos(angle) * scale, jnp.sin(angle) * scale)  37 us
    unnamed x30, local copies, waits for them, and re-layouts  20.5 us
    unnamed x4, waiting for transfers between devices  18.7 us
    dot_general x1, matrix products, per_device(): return jnp.einsum('sghrp,rsx->ghpx', scaled, inverse, precision=highest)  7.41 us
    all_to_all x1, waiting for transfers between devices, per_device(): lax.all_to_all(reduced, 'band', split_axis=2, concat_axis=0, tiled=True)  6.61 us
    all_to_all x1, waiting for transfers between devices, per_device(): lax.all_to_all(outgoing, 'band', split_axis=0, concat_axis=3, tiled=True)  6.17 us
    all_gather x1, blocking collectives, per_device(): columns = lax.all_gather(arrived, 'lon', axis=0, tiled=True)  5.78 us
    all_to_all x1, starting transfers between devices, per_device(): lax.all_to_all(outgoing, 'band', split_axis=0, concat_axis=3, tiled=True)  5.52 us
  transfers between devices with their start and end apart: 4, of which 3 were waited for; matrix products, arithmetic and copies ran while one was open for 15% of the time, Pallas kernels for 0%

commit v1 on v0

--- a/solution.py
+++ b/solution.py
@@ -1,9 +1,337 @@
+import functools
 import math
 
 import jax
 import jax.numpy as jnp
 from jax import lax
+from jax.experimental import pallas as pl
+from jax.experimental.pallas import tpu as pltpu
 from jax.sharding import PartitionSpec as P
+
+LANES = 128
+ROWS = 8
+NT = (((1,), (1,)), ((), ()))
+
+
+def iota(shape, axis):
+    return lax.broadcasted_iota(jnp.int32, shape, axis)
+
+
+def turn(phase, total):
+    shift = (total // 4).bit_length() - 1
+    quadrant = (phase + total // 8) >> shift
+    x = (phase - (quadrant << shift)).astype(jnp.float32) * (2.0 * math.pi / total)
+    z = x * x
+    s = ((-1.9515295891e-4 * z + 8.3321608736e-3) * z - 1.6666654611e-1) * z * x + x
+    c = ((2.443315711809948e-5 * z - 1.388731625493765e-3) * z + 4.166664568298827e-2) * z * z
+    c = c - 0.5 * z + 1.0
+    odd = (quadrant & 1) == 1
+    cosine = jnp.where(odd, s, c)
+    sine = jnp.where(odd, c, s)
+    cosine = jnp.where(((quadrant + 1) & 2) == 2, -cosine, cosine)
+    sine = jnp.where((quadrant & 2) == 2, -sine, sine)
+    return cosine, sine
+
+
+def split(x):
+    high = x.astype(jnp.bfloat16)
+    return high, (x - high.astype(jnp.float32)).astype(jnp.bfloat16)
+
+
+def dot(a, b):
+    return jnp.dot(a, b, preferred_element_type=jnp.float32)
+
+
+def dot_nt(a, b):
+    return lax.dot_general(a, b, NT, preferred_element_type=jnp.float32)
+
+
+def analyse_grid(lon_count, owners, total, orders_ref, weight_ref, cycle_ref, loads_ref, out_ref, points_ref, mid_ref):
+    cycles = loads_ref.shape[3]
+    blocks = loads_ref.shape[4] // LANES
+    per_owner = orders_ref.shape[1]
+    quarter = per_owner // lon_count
+    pieces = LANES // quarter
+    tiles = owners // pieces
+    band, lon = lax.axis_index("band"), lax.axis_index("lon")
+
+    mine = pltpu.roll(orders_ref[...], (LANES - quarter * lon) % LANES, 1)
+    slot = iota((1, LANES), 1) // quarter
+    shifted = [mine if i == 0 else pltpu.roll(mine, quarter * i, 1) for i in range(pieces)]
+    rows = []
+    for t in range(tiles):
+        row = shifted[0][t * pieces : t * pieces + 1]
+        for i in range(1, pieces):
+            row = jnp.where(slot == i, shifted[i][t * pieces + i : t * pieces + i + 1], row)
+        rows.append(row)
+    orders = jnp.concatenate(rows, axis=1)
+    width = orders.shape[1]
+
+    for q in range(lon_count):
+        for a in range(blocks):
+            for f in range(2):
+                north = loads_ref[q, f, 0, :, a * LANES : (a + 1) * LANES]
+                south = loads_ref[q, f, 1, :, a * LANES : (a + 1) * LANES]
+                at = ((q * blocks + a) * 2 + f) * 2 * cycles
+                points_ref[at : at + 2 * cycles] = jnp.concatenate([north + south, north - south], axis=0)
+    high, low = split(points_ref[...])
+    cos_b, sin_b = turn((iota((LANES, width), 0) * orders) & (total - 1), total)
+    cos_high, cos_low = split(cos_b)
+    sin_high, sin_low = split(sin_b)
+    basis_high = jnp.concatenate([cos_high, sin_high], axis=1)
+    basis_low = jnp.concatenate([cos_low, sin_low], axis=1)
+    mid_ref[...] = dot(
+        jnp.concatenate([high, low, high], axis=1),
+        jnp.concatenate([basis_high, basis_high, basis_low], axis=0),
+    )
+    count = lon_count * blocks
+    cos_a, sin_a = turn((iota((count, width), 0) * LANES * orders) & (total - 1), total)
+
+    step = 2 * cycles
+    sums = [[jnp.zeros((step, width), jnp.float32) for _ in range(2)] for _ in range(2)]
+    for a in range(count):
+        ca, sa = cos_a[a : a + 1], sin_a[a : a + 1]
+        for f in range(2):
+            at = (a * 2 + f) * step
+            tc = mid_ref[at : at + step, :width]
+            ts = mid_ref[at : at + step, width:]
+            sums[f][0] = sums[f][0] + (ca * tc - sa * ts)
+            sums[f][1] = sums[f][1] - (sa * tc + ca * ts)
+
+    sub = iota((step, 1), 0) % cycles
+    weight = jnp.zeros((step, 1), jnp.float32)
+    for j in range(cycles):
+        weight = jnp.where(sub == j, weight_ref[cycle_ref[band * cycles + j]], weight)
+    scale = 1.0 / math.sqrt(total)
+    sums = [[(sums[f][c] * scale) * weight for c in range(2)] for f in range(2)]
+    for owner in range(owners):
+        t, i = owner // pieces, owner % pieces
+        block = None
+        for e in range(4):
+            piece = sums[e // 2][e % 2][:, t * LANES : (t + 1) * LANES]
+            move = (e - i) * quarter % LANES
+            piece = pltpu.roll(piece, move, 1) if move else piece
+            block = piece if block is None else jnp.where(slot == e, piece, block)
+        block = block.astype(out_ref.dtype)
+        for q in range(lon_count):
+            out_ref[owner * lon_count + q] = block
+
+
+def spectral(lon_count, owners, orders_ref, cycle_ref, folded_ref, legendre_ref, love_ref, out_ref, spread_ref, kept_ref):
+    per_owner = orders_ref.shape[1]
+    quarter = per_owner // lon_count
+    degrees = legendre_ref.shape[1]
+    cycles = folded_ref.shape[1] // 2
+    northern = owners * cycles
+    group = degrees // northern
+    wide = group * northern
+    band, lon = lax.axis_index("band"), lax.axis_index("lon")
+    lane = iota((1, LANES), 1)
+
+    def cycle_lanes(repeat):
+        place = (lane // (repeat * cycles)) * cycles + lane % cycles
+        row = jnp.full((1, LANES), -1, jnp.int32)
+        for i in range(northern):
+            row = jnp.where(place == i, cycle_ref[i], row)
+        return row
+
+    parity_lane = (lane // cycles) % 2
+    arrived = cycle_lanes(2)
+    found = iota((northern, LANES), 0) == arrived
+    pick = []
+    for p in range(2):
+        one = jnp.where(found & (parity_lane == p), 1.0, 0.0)
+        pick += [one] * group
+    pick = jnp.concatenate(pick, axis=0).astype(jnp.bfloat16)
+
+    pad = jnp.zeros((LANES - 2 * northern, LANES), jnp.float32)
+    for q in range(lon_count):
+        pieces = [folded_ref[b * lon_count + q].astype(jnp.float32) for b in range(owners)]
+        turned = jnp.transpose(jnp.concatenate(pieces + [pad], axis=0)).astype(jnp.bfloat16)
+        spread_ref[q] = dot_nt(turned, pick)
+
+    own = orders_ref[pl.ds(band, 1), :].astype(jnp.float32)
+    order_rows = jnp.transpose(jnp.broadcast_to(own, (LANES, per_owner))).astype(jnp.int32)
+    degree = lon * degrees + iota((ROWS, degrees), 1)
+    diagonal = iota((ROWS, wide), 0) == iota((ROWS, wide), 1) // northern
+    love = [[love_ref[g, f : f + 1, :] for f in range(2)] for g in range(2)]
+
+    for q in range(lon_count):
+        for pair in range(quarter // (2 * group)):
+            halves = []
+            for half in range(2):
+                first = (pair * 2 + half) * group
+                left = []
+                for f in range(2):
+                    for p in range(2):
+                        for c in range(2):
+                            at = (f * 2 + c) * quarter + first
+                            left.append(
+                                jnp.where(diagonal, spread_ref[q, at : at + group, p * wide : (p + 1) * wide], 0.0)
+                            )
+                left = jnp.concatenate(left, axis=0).astype(jnp.bfloat16)
+                start = (q * quarter + first) * northern
+                table = legendre_ref[start : start + wide]
+                analysed = dot(left, table)
+                order = order_rows[q * quarter + first : q * quarter + first + group]
+                gap = degree - jnp.concatenate([order] * (degrees // LANES), axis=1)
+                valid = gap >= 0
+                keep = [valid & ((gap & 1) == p) for p in range(2)]
+                mixed = []
+                for g in range(2):
+                    for p in range(2):
+                        for c in range(2):
+                            lo = (p * 2 + c) * group
+                            hi = ((2 + p) * 2 + c) * group
+                            value = love[g][0] * analysed[lo : lo + group] + love[g][1] * analysed[hi : hi + group]
+                            mixed.append(jnp.where(keep[p], value, 0.0))
+                mixed = jnp.concatenate(mixed, axis=0).astype(jnp.bfloat16)
+                halves.append(dot_nt(mixed, table))
+            at = q * quarter + pair * 2 * group
+            for g in range(2):
+                for c in range(2):
+                    rows = []
+                    for half in range(2):
+                        even = halves[half][(g * 4 + c) * group : (g * 4 + c + 1) * group]
+                        odd = halves[half][(g * 4 + 2 + c) * group : (g * 4 + 3 + c) * group]
+                        rows.append((even, odd))
+                    for h in range(2):
+                        both = [even + odd if h == 0 else even - odd for even, odd in rows]
+                        both = [jnp.where(diagonal, value, 0.0) for value in both]
+                        kept_ref[g * 2 + h, c * per_owner + at : c * per_owner + at + 2 * group, :] = jnp.concatenate(
+                            both, axis=0
+                        ).astype(jnp.bfloat16)
+
+    leaving = cycle_lanes(4).astype(jnp.float32)
+    cycle_rows = jnp.transpose(jnp.broadcast_to(leaving, (LANES, LANES))).astype(jnp.int32)
+    cycle_rows = jnp.concatenate([cycle_rows] * (wide // LANES), axis=1)
+    found = cycle_rows == iota((LANES, wide), 1) % northern
+    part = (iota((LANES, wide), 0) // cycles) % 4
+    total = None
+    for i in range(4):
+        pick = jnp.where(found & (part == i), 1.0, 0.0).astype(jnp.bfloat16)
+        term = dot_nt(pick, kept_ref[i])
+        total = term if total is None else total + term
+    total = total.astype(out_ref.dtype)
+    for b in range(owners):
+        for q in range(lon_count):
+            out_ref[b * lon_count + q] = total[b * 4 * cycles : (b + 1) * 4 * cycles]
+
+
+def synthesise_grid(lon_count, owners, total, orders_ref, values_ref, out_ref, left_ref, right_ref):
+    per_owner = orders_ref.shape[1]
+    rows = values_ref.shape[1]
+    cycles = out_ref.shape[2]
+    blocks = out_ref.shape[3] // LANES
+    lon = lax.axis_index("lon")
+    scale = 1.0 / math.sqrt(total)
+    count = owners * per_owner
+    for b in range(owners):
+        order = orders_ref[b : b + 1, :]
+        value = values_ref[b * lon_count].astype(jnp.float32)
+        for q in range(1, lon_count):
+            value = value + values_ref[b * lon_count + q].astype(jnp.float32)
+        factor = jnp.where(order == 0, scale, 2.0 * scale)
+        re = value[:, :per_owner] * factor
+        im = value[:, per_owner:] * factor
+        step = iota((blocks, per_owner), 0) + lon * blocks
+        cos_a, sin_a = turn((step * LANES * order) & (total - 1), total)
+        cos_b, sin_b = turn((iota((LANES, per_owner), 0) * order) & (total - 1), total)
+        at = b * per_owner
+        for c, table in ((0, cos_b), (1, sin_b)):
+            high, low = split(table)
+            right_ref[0, :, c * count + at : c * count + at + per_owner] = high
+            right_ref[1, :, c * count + at : c * count + at + per_owner] = low
+        for a in range(blocks):
+            ca, sa = cos_a[a : a + 1], sin_a[a : a + 1]
+            for c, term in ((0, ca * re - sa * im), (1, -(sa * re + ca * im))):
+                high, low = split(term)
+                left_ref[0, a * rows : (a + 1) * rows, c * count + at : c * count + at + per_owner] = high
+                left_ref[1, a * rows : (a + 1) * rows, c * count + at : c * count + at + per_owner] = low
+    grid = dot_nt(left_ref[0], right_ref[0])
+    grid = grid + dot_nt(left_ref[1], right_ref[0])
+    grid = grid + dot_nt(left_ref[0], right_ref[1])
+    for a in range(blocks):
+        for g in range(2):
+            for h in range(2):
+                at = a * rows + (g * 2 + h) * cycles
+                out_ref[g, h, :, a * LANES : (a + 1) * LANES] = grid[at : at + cycles]
+
+
+def fits(owners, lon_count, cycles, points, per_owner, degrees):
+    northern = owners * cycles
+    total = points * lon_count
+    return (
+        per_owner == LANES
+        and 4 * per_owner == lon_count * LANES
+        and 2 * cycles == ROWS
+        and 4 * northern == LANES
+        and ROWS * northern == degrees
+        and degrees % LANES == 0
+        and owners == ROWS
+        and points % LANES == 0
+        and total & (total - 1) == 0
+        and owners * per_owner * LANES < 1 << 24
+    )
+
+
+def per_device_kernels(loads, legendre, love, cycle_weight, order_list, cycle_order):
+    owners = lax.axis_size("band")
+    lon_count = lax.axis_size("lon")
+    cycles, points = loads.shape[2], loads.shape[3]
+    per_owner, degrees, northern = legendre.shape
+    total = points * lon_count
+    devices = owners * lon_count
+    blocks = points // LANES
+    everyone = ("band", "lon")
+    vmem = pl.BlockSpec(memory_space=pltpu.VMEM)
+    smem = pl.BlockSpec(memory_space=pltpu.SMEM)
+    table = order_list.reshape(owners, per_owner)
+
+    whole = lax.all_gather(loads, "lon", axis=0)
+    count = lon_count * blocks * 4 * cycles
+    width = 2 * owners * per_owner // lon_count
+    folded = pl.pallas_call(
+        functools.partial(analyse_grid, lon_count, owners, total),
+        out_shape=jax.ShapeDtypeStruct((devices, 2 * cycles, LANES), jnp.bfloat16),
+        in_specs=[vmem, smem, smem, vmem],
+        out_specs=vmem,
+        scratch_shapes=[pltpu.VMEM((count, LANES), jnp.float32), pltpu.VMEM((count, width), jnp.float32)],
+        name="analyse_grid",
+    )(table, cycle_weight, cycle_order, whole)
+    arrived = lax.all_to_all(folded, everyone, split_axis=0, concat_axis=0, tiled=True)
+
+    rows = jnp.transpose(legendre, (0, 2, 1)).reshape(per_owner * northern, degrees)
+    values = pl.pallas_call(
+        functools.partial(spectral, lon_count, owners),
+        out_shape=jax.ShapeDtypeStruct((devices, 4 * cycles, 2 * per_owner), jnp.bfloat16),
+        in_specs=[vmem, smem, vmem, vmem, vmem],
+        out_specs=vmem,
+        scratch_shapes=[
+            pltpu.VMEM((lon_count, LANES, 2 * degrees), jnp.float32),
+            pltpu.VMEM((4, 2 * per_owner, degrees), jnp.bfloat16),
+        ],
+        name="spectral",
+    )(table, cycle_order, arrived, rows, love)
+    returned = lax.all_to_all(values, everyone, split_axis=0, concat_axis=0, tiled=True)
+
+    return pl.pallas_call(
+        functools.partial(synthesise_grid, lon_count, owners, total),
+        out_shape=jax.ShapeDtypeStruct(loads.shape, jnp.float32),
+        in_specs=[vmem, vmem],
+        out_specs=vmem,
+        scratch_shapes=[
+            pltpu.VMEM((2, 4 * cycles * blocks, 2 * owners * per_owner), jnp.bfloat16),
+            pltpu.VMEM((2, LANES, 2 * owners * per_owner), jnp.bfloat16),
+        ],
+        name="synthesise_grid",
+    )(table, returned)
+
+
+def per_device(loads, legendre, love, cycle_weight, order_list, cycle_order):
+    sizes = (lax.axis_size("band"), lax.axis_size("lon"), loads.shape[2], loads.shape[3], legendre.shape[0], legendre.shape[1])
+    form = per_device_kernels if fits(*sizes) else per_device_plain
+    return form(loads, legendre, love, cycle_weight, order_list, cycle_order)
 
 
 def cycle_basis(order_ids, positions, total):
@@ -13,7 +341,7 @@
     return (jnp.cos(angle) * scale, jnp.sin(angle) * scale)
 
 
-def per_device(loads, legendre, love, cycle_weight, order_list, cycle_order):
+def per_device_plain(loads, legendre, love, cycle_weight, order_list, cycle_order):
     highest = lax.Precision.HIGHEST
     owners = lax.axis_size("band")
     lon_count = lax.axis_size("lon")

time: 155 us -> 45.8 us (0.30)
  other arithmetic: 43.2 us -> 0 us
  waiting for transfers between devices: 31.5 us -> 0 us
  local copies, waits for them, and re-layouts: 27.3 us -> 0 us
  blocking collectives: 11.2 us -> 35.1 us
  matrix products: 18.2 us -> 0 us
  between operations: 13.7 us -> 0.01 us
  Pallas kernels: 0 us -> 10.4 us
  starting transfers between devices: 8.9 us -> 0 us
    mul x2 -> x0, other arithmetic: 37 us -> none  [cycle_basis(): return (jnp.cos(angle) * scale, jnp.sin(angle) * scale)]
    all_to_all x0 -> x2, blocking collectives: none -> 26.3 us  [the longest x1 13.8 us: per_device_kernels(): lax.all_to_all(values, everyone, split_axis=0, concat_axis=0, tiled=True)]
    unnamed x30 -> x0, local copies, waits for them, and re-layouts: 20.5 us -> none
    unnamed x4 -> x0, waiting for transfers between devices: 18.7 us -> none
    dot_general x5 -> x0, matrix products: 18.2 us -> none  [the longest x1 7.41 us: per_device(): return jnp.einsum('sghrp,rsx->ghpx', scaled, inverse, precision=highest)]
    all_to_all x2 -> x0, waiting for transfers between devices: 12.8 us -> none  [the longest x1 6.61 us: per_device(): lax.all_to_all(reduced, 'band', split_axis=2, concat_axis=0, tiled=True)]
    pallas_call x0 -> x3, Pallas kernels: none -> 10.4 us  [the longest x1 4.6 us: per_device_kernels(): pl.pallas_call(functools.partial(spectral, lon_count, owners), out_shape=...]
    all_to_all x2 -> x0, starting transfers between devices: 8.86 us -> none  [the longest x1 5.52 us: per_device(): lax.all_to_all(outgoing, 'band', split_axis=0, concat_axis=3, tiled=True)]
  transfers between devices with their start and end apart: 4 -> 0, of which waited for: 3 -> 0; matrix products, arithmetic and copies ran while one was open for 15% -> 0% of each run, Pallas kernels for 0% -> 0%
where the time goes in v1:
time: 45.8 us; the launch traced here: 45.5 us
  blocking collectives  35.1 us (77%)
  Pallas kernels  10.4 us (23%)
    all_to_all x1, blocking collectives, per_device_kernels(): lax.all_to_all(values, everyone, split_axis=0, concat_axis=0, tiled=True)  13.8 us
    all_to_all x1, blocking collectives, per_device_kernels(): lax.all_to_all(folded, everyone, split_axis=0, concat_axis=0, tiled=True)  12.4 us
    all_gather x1, blocking collectives, per_device_kernels(): whole = lax.all_gather(loads, 'lon', axis=0)  8.85 us
    pallas_call x1, Pallas kernels, per_device_kernels(): pl.pallas_call(functools.partial(spectral, lon_count, owners), out_shape=...  4.6 us
    pallas_call x1, Pallas kernels, per_device_kernels(): pl.pallas_call(functools.partial(synthesise_grid, lon_count, owners, tota...  3.31 us
    pallas_call x1, Pallas kernels, per_device_kernels(): pl.pallas_call(functools.partial(analyse_grid, lon_count, owners, total),...  2.45 us

profile of v1, /device:TPU:0, one launch (start us, length us, event | category | flops | bytes accessed | tf_op | source)
XLA Modules:
  0.0 45.5 jit_solution(3465681907413413144)
XLA Ops:
  0.0 8.8 %all-gather = f32[8,2,4,1024]{3,2,1,0:T(4,128)} all-gather(f32[2,2,4,1024]{3,2,1,0:T(4,128)} %param.6), channel_id=2, replica_groups=mesh['band'=8,'lon'=4] {'lon'}, dimensions={0}, use_global_device_ids=true | all-gather | bytes 327680 | tf_op jit(solution)/shard_map/all_gather | solution.py:291
  8.8 2.5 %analyse_grid.1 = bf16[32,8,128]{2,1,0:T(8,128)(2,1)} custom-call(s32[8,128]{1,0:T(8,128)} %bitcast.7, f32[32]{0:T(128)} %weight_ref.1, s32[32]{0:T(128)} %cycle_ref.3, f32[4,2,2,4,1024]{4,3,2,1,0:T(4,128)} %bitcast.6), custom_call_target="tpu_custom_call" | custom-call | tf_op jit(solution)/shard_map/analyse_grid/pallas_call | solution.py:294
  11.3 12.4 %all_to_all.10.folded_ref = bf16[32,8,128]{2,1,0:T(8,128)(2,1)} all-to-all(bf16[32,8,128]{2,1,0:T(8,128)(2,1)} %analyse_grid.1), channel_id=1, replica_groups=mesh['band'=8,'lon'=4] {'band','lon'}, dimensions={0} | all-to-all | bytes 131072 | tf_op jit(solution)/shard_map/all_to_all | solution.py:302
  23.7 4.6 %spectral.1 = bf16[32,16,256]{2,1,0:T(8,128)(2,1)} custom-call(s32[8,128]{1,0:T(8,128)} %bitcast.8, s32[32]{0:T(128)} %cycle_ref.3, bf16[32,8,128]{2,1,0:T(8,128)(2,1)} %all_to_all.10.folded_ref, bf16[4096,256]{1,0:T(8,128)(2,1)} %bitcast.5, f32[2,2,256]{2,1,0:T(2,128)} %love_ref.1), custom_call_target="tpu_custom_call" | custom-call | tf_op jit(solution)/shard_map/spectral/pallas_call | solution.py:305
  28.3 13.8 %all_to_all.11.values_ref = bf16[32,16,256]{2,1,0:T(8,128)(2,1)} all-to-all(bf16[32,16,256]{2,1,0:T(8,128)(2,1)} %spectral.1), channel_id=1, replica_groups=mesh['band'=8,'lon'=4] {'band','lon'}, dimensions={0} | all-to-all | bytes 524288 | tf_op jit(solution)/shard_map/all_to_all | solution.py:316
  42.2 3.3 %synthesise_grid.1 = f32[2,2,4,1024]{3,2,1,0:T(4,128)} custom-call(s32[8,128]{1,0:T(8,128)} %bitcast.9, bf16[32,16,256]{2,1,0:T(8,128)(2,1)} %all_to_all.11.values_ref), custom_call_target="tpu_custom_call" | custom-call | tf_op jit(solution)/shard_map/synthesise_grid/pallas_call | solution.py:318

commit v2 on v1

--- a/solution.py
+++ b/solution.py
@@ -10,6 +10,7 @@
 
 LANES = 128
 ROWS = 8
+VMEM_LIMIT = 12 << 20
 NT = (((1,), (1,)), ((), ()))
 
 
@@ -46,51 +47,30 @@
     return lax.dot_general(a, b, NT, preferred_element_type=jnp.float32)
 
 
-def analyse_grid(lon_count, owners, total, orders_ref, weight_ref, cycle_ref, loads_ref, out_ref, points_ref, mid_ref):
-    cycles = loads_ref.shape[3]
-    blocks = loads_ref.shape[4] // LANES
-    per_owner = orders_ref.shape[1]
-    quarter = per_owner // lon_count
+def analyse_grid(right_ref, turn_ref, weight_ref, *refs):
+    parts, out_ref, points_ref, mid_ref = refs[:-3], refs[-3], refs[-2], refs[-1]
+    lon_count = len(parts)
+    cycles = parts[0].shape[2]
+    blocks = parts[0].shape[3] // LANES
+    owners = out_ref.shape[0] // lon_count
+    count, width = turn_ref.shape[1:]
+    quarter = width // owners
     pieces = LANES // quarter
-    tiles = owners // pieces
-    band, lon = lax.axis_index("band"), lax.axis_index("lon")
-
-    mine = pltpu.roll(orders_ref[...], (LANES - quarter * lon) % LANES, 1)
-    slot = iota((1, LANES), 1) // quarter
-    shifted = [mine if i == 0 else pltpu.roll(mine, quarter * i, 1) for i in range(pieces)]
-    rows = []
-    for t in range(tiles):
-        row = shifted[0][t * pieces : t * pieces + 1]
-        for i in range(1, pieces):
-            row = jnp.where(slot == i, shifted[i][t * pieces + i : t * pieces + i + 1], row)
-        rows.append(row)
-    orders = jnp.concatenate(rows, axis=1)
-    width = orders.shape[1]
-
-    for q in range(lon_count):
+    step = 2 * cycles
+
+    for q, part in enumerate(parts):
         for a in range(blocks):
             for f in range(2):
-                north = loads_ref[q, f, 0, :, a * LANES : (a + 1) * LANES]
-                south = loads_ref[q, f, 1, :, a * LANES : (a + 1) * LANES]
-                at = ((q * blocks + a) * 2 + f) * 2 * cycles
-                points_ref[at : at + 2 * cycles] = jnp.concatenate([north + south, north - south], axis=0)
+                north = part[f, 0, :, a * LANES : (a + 1) * LANES]
+                south = part[f, 1, :, a * LANES : (a + 1) * LANES]
+                at = ((q * blocks + a) * 2 + f) * step
+                points_ref[at : at + step] = jnp.concatenate([north + south, north - south], axis=0)
     high, low = split(points_ref[...])
-    cos_b, sin_b = turn((iota((LANES, width), 0) * orders) & (total - 1), total)
-    cos_high, cos_low = split(cos_b)
-    sin_high, sin_low = split(sin_b)
-    basis_high = jnp.concatenate([cos_high, sin_high], axis=1)
-    basis_low = jnp.concatenate([cos_low, sin_low], axis=1)
-    mid_ref[...] = dot(
-        jnp.concatenate([high, low, high], axis=1),
-        jnp.concatenate([basis_high, basis_high, basis_low], axis=0),
-    )
-    count = lon_count * blocks
-    cos_a, sin_a = turn((iota((count, width), 0) * LANES * orders) & (total - 1), total)
-
-    step = 2 * cycles
+    mid_ref[...] = dot(jnp.concatenate([high, low, high], axis=1), right_ref[...])
+
     sums = [[jnp.zeros((step, width), jnp.float32) for _ in range(2)] for _ in range(2)]
     for a in range(count):
-        ca, sa = cos_a[a : a + 1], sin_a[a : a + 1]
+        ca, sa = turn_ref[0, a : a + 1], turn_ref[1, a : a + 1]
         for f in range(2):
             at = (a * 2 + f) * step
             tc = mid_ref[at : at + step, :width]
@@ -98,12 +78,8 @@
             sums[f][0] = sums[f][0] + (ca * tc - sa * ts)
             sums[f][1] = sums[f][1] - (sa * tc + ca * ts)
 
-    sub = iota((step, 1), 0) % cycles
-    weight = jnp.zeros((step, 1), jnp.float32)
-    for j in range(cycles):
-        weight = jnp.where(sub == j, weight_ref[cycle_ref[band * cycles + j]], weight)
-    scale = 1.0 / math.sqrt(total)
-    sums = [[(sums[f][c] * scale) * weight for c in range(2)] for f in range(2)]
+    slot = iota((1, LANES), 1) // quarter
+    weight = weight_ref[...]
     for owner in range(owners):
         t, i = owner // pieces, owner % pieces
         block = None
@@ -112,37 +88,99 @@
             move = (e - i) * quarter % LANES
             piece = pltpu.roll(piece, move, 1) if move else piece
             block = piece if block is None else jnp.where(slot == e, piece, block)
-        block = block.astype(out_ref.dtype)
+        block = (block * weight).astype(out_ref.dtype)
         for q in range(lon_count):
             out_ref[owner * lon_count + q] = block
 
 
-def spectral(lon_count, owners, orders_ref, cycle_ref, folded_ref, legendre_ref, love_ref, out_ref, spread_ref, kept_ref):
-    per_owner = orders_ref.shape[1]
+def tables(lon_count, cycles, degrees, blocks, total, orders_ref, weight_ref, cycle_ref, *out_refs):
+    right_ref, first_ref, column_ref, pick_ref, put_ref, rows_ref, turn_ref, basis_ref = out_refs
+    owners, per_owner = orders_ref.shape
+    quarter = per_owner // lon_count
+    pieces = LANES // quarter
+    northern = owners * cycles
+    group = degrees // northern
+    wide = group * northern
+    band, lon = lax.axis_index("band"), lax.axis_index("lon")
+    lane = iota((1, LANES), 1)
+
+    mine = pltpu.roll(orders_ref[...], (LANES - quarter * lon) % LANES, 1)
+    slot = lane // quarter
+    shifted = [mine if i == 0 else pltpu.roll(mine, quarter * i, 1) for i in range(pieces)]
+    rows = []
+    for t in range(owners // pieces):
+        row = shifted[0][t * pieces : t * pieces + 1]
+        for i in range(1, pieces):
+            row = jnp.where(slot == i, shifted[i][t * pieces + i : t * pieces + i + 1], row)
+        rows.append(row)
+    orders = jnp.concatenate(rows, axis=1)
+    width = orders.shape[1]
+    for c, table in enumerate(turn((iota((LANES, width), 0) * orders) & (total - 1), total)):
+        high, low = split(table)
+        for k, value in enumerate((high, high, low)):
+            right_ref[k * LANES : (k + 1) * LANES, c * width : (c + 1) * width] = value
+    for k in range(lon_count):
+        origin = (lon + lon_count - k) % lon_count
+        step = iota((blocks, width), 0) + origin * blocks
+        for c, table in enumerate(turn((step * LANES * orders) & (total - 1), total)):
+            first_ref[c, k * blocks : (k + 1) * blocks] = table
+    sub = iota((2 * cycles, LANES), 0) % cycles
+    weight = jnp.zeros((2 * cycles, LANES), jnp.float32)
+    for j in range(cycles):
+        weight = jnp.where(sub == j, weight_ref[cycle_ref[band * cycles + j]], weight)
+    column_ref[...] = weight * (1.0 / math.sqrt(total))
+
+    def cycle_lanes(repeat):
+        place = (lane // (repeat * cycles)) * cycles + lane % cycles
+        row = jnp.full((1, LANES), -1, jnp.int32)
+        for i in range(northern):
+            row = jnp.where(place == i, cycle_ref[i], row)
+        return row
+
+    parity_lane = (lane // cycles) % 2
+    found = iota((northern, LANES), 0) == cycle_lanes(2)
+    for p in range(2):
+        one = jnp.where(found & (parity_lane == p), 1.0, 0.0)
+        pick_ref[p * wide : (p + 1) * wide] = jnp.concatenate([one] * group, axis=0).astype(jnp.bfloat16)
+
+    leaving = cycle_lanes(4).astype(jnp.float32)
+    cycle_rows = jnp.transpose(jnp.broadcast_to(leaving, (LANES, LANES))).astype(jnp.int32)
+    found = cycle_rows == iota((LANES, LANES), 1) % northern
+    part = (iota((LANES, LANES), 0) // cycles) % 4
+    for i in range(4):
+        put = jnp.where(found & (part == i), 1.0, 0.0)
+        put_ref[i] = jnp.concatenate([put] * (wide // LANES), axis=1).astype(jnp.bfloat16)
+
+    own = orders_ref[pl.ds(band, 1), :].astype(jnp.float32)
+    rows_ref[...] = jnp.transpose(jnp.broadcast_to(own, (LANES, per_owner))).astype(jnp.int32)
+
+    scale = 1.0 / math.sqrt(total)
+    count = owners * per_owner
+    for b in range(owners):
+        order = orders_ref[b : b + 1, :]
+        factor = jnp.where(order == 0, scale, 2.0 * scale)
+        step = iota((blocks, per_owner), 0) + lon * blocks
+        cos_a, sin_a = turn((step * LANES * order) & (total - 1), total)
+        turn_ref[0, b] = cos_a * factor
+        turn_ref[1, b] = sin_a * factor
+        cos_b, sin_b = turn((iota((LANES, per_owner), 0) * order) & (total - 1), total)
+        for c, table in ((0, cos_b), (1, sin_b)):
+            high, low = split(table)
+            at = c * count + b * per_owner
+            basis_ref[0, :, at : at + per_owner] = high
+            basis_ref[1, :, at : at + per_owner] = low
+
+
+def spectral(lon_count, owners, pick_ref, put_ref, rows_ref, folded_ref, legendre_ref, love_ref, out_ref, spread_ref, kept_ref):
+    per_owner = rows_ref.shape[0]
     quarter = per_owner // lon_count
     degrees = legendre_ref.shape[1]
     cycles = folded_ref.shape[1] // 2
     northern = owners * cycles
     group = degrees // northern
     wide = group * northern
-    band, lon = lax.axis_index("band"), lax.axis_index("lon")
-    lane = iota((1, LANES), 1)
-
-    def cycle_lanes(repeat):
-        place = (lane // (repeat * cycles)) * cycles + lane % cycles
-        row = jnp.full((1, LANES), -1, jnp.int32)
-        for i in range(northern):
-            row = jnp.where(place == i, cycle_ref[i], row)
-        return row
-
-    parity_lane = (lane // cycles) % 2
-    arrived = cycle_lanes(2)
-    found = iota((northern, LANES), 0) == arrived
-    pick = []
-    for p in range(2):
-        one = jnp.where(found & (parity_lane == p), 1.0, 0.0)
-        pick += [one] * group
-    pick = jnp.concatenate(pick, axis=0).astype(jnp.bfloat16)
+    lon = lax.axis_index("lon")
+    pick = pick_ref[...]
 
     pad = jnp.zeros((LANES - 2 * northern, LANES), jnp.float32)
     for q in range(lon_count):
@@ -150,8 +188,6 @@
         turned = jnp.transpose(jnp.concatenate(pieces + [pad], axis=0)).astype(jnp.bfloat16)
         spread_ref[q] = dot_nt(turned, pick)
 
-    own = orders_ref[pl.ds(band, 1), :].astype(jnp.float32)
-    order_rows = jnp.transpose(jnp.broadcast_to(own, (LANES, per_owner))).astype(jnp.int32)
     degree = lon * degrees + iota((ROWS, degrees), 1)
     diagonal = iota((ROWS, wide), 0) == iota((ROWS, wide), 1) // northern
     love = [[love_ref[g, f : f + 1, :] for f in range(2)] for g in range(2)]
@@ -173,7 +209,7 @@
                 start = (q * quarter + first) * northern
                 table = legendre_ref[start : start + wide]
                 analysed = dot(left, table)
-                order = order_rows[q * quarter + first : q * quarter + first + group]
+                order = rows_ref[q * quarter + first : q * quarter + first + group]
                 gap = degree - jnp.concatenate([order] * (degrees // LANES), axis=1)
                 valid = gap >= 0
                 keep = [valid & ((gap & 1) == p) for p in range(2)]
@@ -202,15 +238,9 @@
                             both, axis=0
                         ).astype(jnp.bfloat16)
 
-    leaving = cycle_lanes(4).astype(jnp.float32)
-    cycle_rows = jnp.transpose(jnp.broadcast_to(leaving, (LANES, LANES))).astype(jnp.int32)
-    cycle_rows = jnp.concatenate([cycle_rows] * (wide // LANES), axis=1)
-    found = cycle_rows == iota((LANES, wide), 1) % northern
-    part = (iota((LANES, wide), 0) // cycles) % 4
     total = None
     for i in range(4):
-        pick = jnp.where(found & (part == i), 1.0, 0.0).astype(jnp.bfloat16)
-        term = dot_nt(pick, kept_ref[i])
+        term = dot_nt(put_ref[i], kept_ref[i])
         total = term if total is None else total + term
     total = total.astype(out_ref.dtype)
     for b in range(owners):
@@ -218,39 +248,26 @@
             out_ref[b * lon_count + q] = total[b * 4 * cycles : (b + 1) * 4 * cycles]
 
 
-def synthesise_grid(lon_count, owners, total, orders_ref, values_ref, out_ref, left_ref, right_ref):
-    per_owner = orders_ref.shape[1]
+def synthesise_grid(lon_count, turn_ref, basis_ref, values_ref, out_ref, left_ref):
+    owners, blocks, per_owner = turn_ref.shape[1:]
     rows = values_ref.shape[1]
     cycles = out_ref.shape[2]
-    blocks = out_ref.shape[3] // LANES
-    lon = lax.axis_index("lon")
-    scale = 1.0 / math.sqrt(total)
     count = owners * per_owner
     for b in range(owners):
-        order = orders_ref[b : b + 1, :]
         value = values_ref[b * lon_count].astype(jnp.float32)
         for q in range(1, lon_count):
             value = value + values_ref[b * lon_count + q].astype(jnp.float32)
-        factor = jnp.where(order == 0, scale, 2.0 * scale)
-        re = value[:, :per_owner] * factor
-        im = value[:, per_owner:] * factor
-        step = iota((blocks, per_owner), 0) + lon * blocks
-        cos_a, sin_a = turn((step * LANES * order) & (total - 1), total)
-        cos_b, sin_b = turn((iota((LANES, per_owner), 0) * order) & (total - 1), total)
+        re, im = value[:, :per_owner], value[:, per_owner:]
         at = b * per_owner
-        for c, table in ((0, cos_b), (1, sin_b)):
-            high, low = split(table)
-            right_ref[0, :, c * count + at : c * count + at + per_owner] = high
-            right_ref[1, :, c * count + at : c * count + at + per_owner] = low
         for a in range(blocks):
-            ca, sa = cos_a[a : a + 1], sin_a[a : a + 1]
+            ca, sa = turn_ref[0, b, a : a + 1], turn_ref[1, b, a : a + 1]
             for c, term in ((0, ca * re - sa * im), (1, -(sa * re + ca * im))):
                 high, low = split(term)
                 left_ref[0, a * rows : (a + 1) * rows, c * count + at : c * count + at + per_owner] = high
                 left_ref[1, a * rows : (a + 1) * rows, c * count + at : c * count + at + per_owner] = low
-    grid = dot_nt(left_ref[0], right_ref[0])
-    grid = grid + dot_nt(left_ref[1], right_ref[0])
-    grid = grid + dot_nt(left_ref[0], right_ref[1])
+    grid = dot_nt(left_ref[0], basis_ref[0])
+    grid = grid + dot_nt(left_ref[1], basis_ref[0])
+    grid = grid + dot_nt(left_ref[0], basis_ref[1])
     for a in range(blocks):
         for g in range(2):
             for h in range(2):
@@ -288,44 +305,71 @@
     smem = pl.BlockSpec(memory_space=pltpu.SMEM)
     table = order_list.reshape(owners, per_owner)
 
-    whole = lax.all_gather(loads, "lon", axis=0)
-    count = lon_count * blocks * 4 * cycles
-    width = 2 * owners * per_owner // lon_count
-    folded = pl.pallas_call(
-        functools.partial(analyse_grid, lon_count, owners, total),
-        out_shape=jax.ShapeDtypeStruct((devices, 2 * cycles, LANES), jnp.bfloat16),
-        in_specs=[vmem, smem, smem, vmem],
-        out_specs=vmem,
-        scratch_shapes=[pltpu.VMEM((count, LANES), jnp.float32), pltpu.VMEM((count, width), jnp.float32)],
-        name="analyse_grid",
-    )(table, cycle_weight, cycle_order, whole)
+    def kernel(body, out_shape, in_specs, scratch_shapes, flops):
+        return pl.pallas_call(
+            body,
+            out_shape=out_shape,
+            in_specs=in_specs,
+            out_specs=jax.tree.map(lambda _: vmem, out_shape),
+            scratch_shapes=scratch_shapes,
+            compiler_params=pltpu.CompilerParams(vmem_limit_bytes=VMEM_LIMIT),
+            cost_estimate=pl.CostEstimate(flops=flops, bytes_accessed=1 << 20, transcendentals=0),
+            name=getattr(body, "func", body).__name__,
+        )
+
+    parts = [loads]
+    for k in range(1, lon_count):
+        parts.append(lax.ppermute(loads, "lon", [(i, (i + k) % lon_count) for i in range(lon_count)]))
+    count = lon_count * blocks
+    width = owners * per_owner // lon_count
+    right, first, column, pick, put, order_rows, turns, basis = kernel(
+        functools.partial(tables, lon_count, cycles, degrees, blocks, total),
+        (
+            jax.ShapeDtypeStruct((3 * LANES, 2 * width), jnp.bfloat16),
+            jax.ShapeDtypeStruct((2, count, width), jnp.float32),
+            jax.ShapeDtypeStruct((2 * cycles, LANES), jnp.float32),
+            jax.ShapeDtypeStruct((2 * degrees, LANES), jnp.bfloat16),
+            jax.ShapeDtypeStruct((4, LANES, degrees), jnp.bfloat16),
+            jax.ShapeDtypeStruct((per_owner, LANES), jnp.int32),
+            jax.ShapeDtypeStruct((2, owners, blocks, per_owner), jnp.float32),
+            jax.ShapeDtypeStruct((2, LANES, 2 * owners * per_owner), jnp.bfloat16),
+        ),
+        [vmem, smem, smem],
+        [],
+        1 << 31,
+    )(table, cycle_weight, cycle_order)
+    folded = kernel(
+        analyse_grid,
+        jax.ShapeDtypeStruct((devices, 2 * cycles, LANES), jnp.bfloat16),
+        [vmem] * (3 + lon_count),
+        [
+            pltpu.VMEM((count * 4 * cycles, LANES), jnp.float32),
+            pltpu.VMEM((count * 4 * cycles, 2 * width), jnp.float32),
+        ],
+        1 << 31,
+    )(right, first, column, *parts)
     arrived = lax.all_to_all(folded, everyone, split_axis=0, concat_axis=0, tiled=True)
 
     rows = jnp.transpose(legendre, (0, 2, 1)).reshape(per_owner * northern, degrees)
-    values = pl.pallas_call(
+    values = kernel(
         functools.partial(spectral, lon_count, owners),
-        out_shape=jax.ShapeDtypeStruct((devices, 4 * cycles, 2 * per_owner), jnp.bfloat16),
-        in_specs=[vmem, smem, vmem, vmem, vmem],
-        out_specs=vmem,
-        scratch_shapes=[
+        jax.ShapeDtypeStruct((devices, 4 * cycles, 2 * per_owner), jnp.bfloat16),
+        [vmem] * 6,
+        [
             pltpu.VMEM((lon_count, LANES, 2 * degrees), jnp.float32),
             pltpu.VMEM((4, 2 * per_owner, degrees), jnp.bfloat16),
         ],
-        name="spectral",
-    )(table, cycle_order, arrived, rows, love)
+        1 << 32,
+    )(pick, put, order_rows, arrived, rows, love)
     returned = lax.all_to_all(values, everyone, split_axis=0, concat_axis=0, tiled=True)
 
-    return pl.pallas_call(
-        functools.partial(synthesise_grid, lon_count, owners, total),
-        out_shape=jax.ShapeDtypeStruct(loads.shape, jnp.float32),
-        in_specs=[vmem, vmem],
-        out_specs=vmem,
-        scratch_shapes=[
-            pltpu.VMEM((2, 4 * cycles * blocks, 2 * owners * per_owner), jnp.bfloat16),
-            pltpu.VMEM((2, LANES, 2 * owners * per_owner), jnp.bfloat16),
-        ],
-        name="synthesise_grid",
-    )(table, returned)
+    return kernel(
+        functools.partial(synthesise_grid, lon_count),
+        jax.ShapeDtypeStruct(loads.shape, jnp.float32),
+        [vmem] * 3,
+        [pltpu.VMEM((2, 4 * cycles * blocks, 2 * owners * per_owner), jnp.bfloat16)],
+        1 << 31,
+    )(turns, basis, returned)
 
 
 def per_device(loads, legendre, love, cycle_weight, order_list, cycle_order):

time: 45.8 us -> 37.5 us (0.82)
  blocking collectives: 35.1 us -> 24.4 us
  starting transfers between devices: 0 us -> 4.46 us
  Pallas kernels: 10.4 us -> 6.32 us
  local copies, waits for them, and re-layouts: 0 us -> 2.01 us
    all_gather x1 -> x0, blocking collectives: 8.85 us -> none  [per_device_kernels(): whole = lax.all_gather(loads, 'lon', axis=0)]
    ppermute x0 -> x3, starting transfers between devices: none -> 4.46 us  [per_device_kernels(): lax.ppermute(loads, 'lon', [(i, (i + k) % lon_count) for i in range(lon_c...]
    pallas_call x3 -> x4, Pallas kernels: 10.4 us -> 6.32 us  [the longest x1 2.25 us: per_device_kernels(): kernel(functools.partial(spectral, lon_count, owners), jax.ShapeDtypeStru...]
    unnamed x0 -> x12, local copies, waits for them, and re-layouts: none -> 2.01 us
    all_to_all x1, blocking collectives: 13.8 us -> 12.3 us  [per_device_kernels(): lax.all_to_all(values, everyone, split_axis=0, concat_axis=0, tiled=True)]
  transfers between devices with their start and end apart: 0 -> 3, of which waited for: 0 -> 0; matrix products, arithmetic and copies ran while one was open for 0% -> 0% of each run, Pallas kernels for 0% -> 6%
where the time goes in v2:
time: 37.5 us; the launch traced here: 37.3 us
  blocking collectives  24.4 us (65%)
  Pallas kernels  6.32 us (17%)
  starting transfers between devices  4.46 us (12%)
  local copies, waits for them, and re-layouts  2.01 us (5%)
    all_to_all x1, blocking collectives, per_device_kernels(): lax.all_to_all(values, everyone, split_axis=0, concat_axis=0, tiled=True)  12.3 us
    all_to_all x1, blocking collectives, per_device_kernels(): lax.all_to_all(folded, everyone, split_axis=0, concat_axis=0, tiled=True)  12.1 us
    ppermute x3, starting transfers between devices, per_device_kernels(): lax.ppermute(loads, 'lon', [(i, (i + k) % lon_count) for i in range(lon_c...  4.46 us
    pallas_call x1, Pallas kernels, per_device_kernels(): kernel(functools.partial(spectral, lon_count, owners), jax.ShapeDtypeStru...  2.25 us
    pallas_call x1, Pallas kernels, per_device_kernels(): kernel(functools.partial(tables, lon_count, cycles, degrees, blocks, tota...  2.09 us
    unnamed x12, local copies, waits for them, and re-layouts  2.01 us
    pallas_call x1, Pallas kernels, per_device_kernels(): kernel(functools.partial(synthesise_grid, lon_count), jax.ShapeDtypeStruc...  1.42 us
  transfers between devices with their start and end apart: 3, of which 0 were waited for; matrix products, arithmetic and copies ran while one was open for 0% of the time, Pallas kernels for 6%

profile of v2, /device:TPU:0, one launch (start us, length us, event | category | flops | bytes accessed | tf_op | source)
XLA Modules:
  0.0 37.3 jit_solution(15412342974734416079)
XLA Ops:
  0.0 0.5 %collective-permute-start = (f32[2,2,4,1024]{3,2,1,0:T(4,128)}, f32[2,2,4,1024]{3,2,1,0:T(4,128)S(1)}, u32[]{:S(2)}, u32[]{:S(2)}) collective-permute-start(f32[2,2,4,1024]{3,2,1,0:T(4,128)} %refs_0_.1), channel_id=1, source_target_pairs={{0,1},{1,2},{2,3},{3,0},{4,5},{5,6},{6,7},{7,4},{8,9},{9,10},{10,1... | collective-permute-start | bytes 196616 | tf_op jit(solution)/shard_map/ppermute | solution.py:322
  0.5 2.5 %collective-permute-start.1 = (f32[2,2,4,1024]{3,2,1,0:T(4,128)}, f32[2,2,4,1024]{3,2,1,0:T(4,128)S(1)}, u32[]{:S(2)}, u32[]{:S(2)}) collective-permute-start(f32[2,2,4,1024]{3,2,1,0:T(4,128)} %refs_0_.1), channel_id=1, source_target_pairs={{0,2},{1,3},{2,0},{3,1},{4,6},{5,7},{6,4},{7,5},{8,10},{9,11},{10,... | collective-permute-start | bytes 196616 | tf_op jit(solution)/shard_map/ppermute | solution.py:322
  3.0 1.5 %collective-permute-start.2 = (f32[2,2,4,1024]{3,2,1,0:T(4,128)}, f32[2,2,4,1024]{3,2,1,0:T(4,128)S(1)}, u32[]{:S(2)}, u32[]{:S(2)}) collective-permute-start(f32[2,2,4,1024]{3,2,1,0:T(4,128)} %refs_0_.1), channel_id=1, source_target_pairs={{0,3},{1,0},{2,1},{3,2},{4,7},{5,4},{6,5},{7,6},{8,11},{9,8},{10,9... | collective-permute-start | bytes 196616 | tf_op jit(solution)/shard_map/ppermute | solution.py:322
  4.5 0.0 copy-start.2
  4.5 0.7 %copy-done.2 = s32[1024]{0:T(1024)S(1)} copy-done((s32[1024]{0:T(1024)S(1)}, s32[1024]{0:T(1024)}, u32[]{:S(2)}) %copy-start.2) | copy-done | bytes 4120
  5.2 0.0 copy-start.4
  5.2 0.7 %copy-done.4 = f32[32]{0:T(128)S(1)} copy-done((f32[32]{0:T(128)S(1)}, f32[32]{0:T(128)}, u32[]{:S(2)}) %copy-start.4) | copy-done | bytes 152
  5.8 0.0 copy-start.5
  5.8 0.7 %copy-done.5 = s32[32]{0:T(128)S(1)} copy-done((s32[32]{0:T(128)S(1)}, s32[32]{0:T(128)}, u32[]{:S(2)}) %copy-start.5) | copy-done | bytes 152
  6.5 0.0 copy-start.1
  6.5 2.1 %tables.1 = (bf16[384,512]{1,0:T(8,128)(2,1)S(1)}, f32[2,32,256]{2,1,0:T(8,128)S(1)}, f32[8,128]{1,0:T(8,128)S(1)}, bf16[512,128]{1,0:T(8,128)(2,1)S(1)}, bf16[4...) custom-call(s32[8,128]{1,0:T(8,128)S(1)} %bitcast.5, ...), custom_call_target="tpu_custom_call" | custom-call | flops 2147483648 | bytes 1048576 | tf_op jit(solution)/shard_map/tables/pallas_call | solution.py:325
  8.6 0.0 collective-permute-done.refs_1_
  8.6 0.0 collective-permute-done.1.refs_2_
  8.6 0.0 collective-permute-done.2.refs_3_
  8.6 0.0 copy-done.1
  8.6 0.0 copy-start
  8.6 0.0 copy-start.3
  8.6 0.5 %analyse_grid.1 = bf16[32,8,128]{2,1,0:T(8,128)(2,1)S(1)} custom-call(bf16[384,512]{1,0:T(8,128)(2,1)S(1)} %get-tuple-element.18.right_ref, f32[2,32,256]{2,1,0:T(8,128)S(1)} %get-tuple-element.19.turn_ref, f32[8,128]{1,0:T(8,128)S(1)} %get-tuple-element.20.weight_ref, f32[2,2,4,1024]{3,2,1,0:T(4,128)S(1)} %copy-done.1, ...), custom_call_target="tpu_custom_call" | custom-call | flops 2147483648 | bytes 1048576 | tf_op jit(solution)/shard_map/analyse_grid/pallas_call | solution.py:341
  9.2 12.1 %all_to_all.10.folded_ref = bf16[32,8,128]{2,1,0:T(8,128)(2,1)S(1)} all-to-all(bf16[32,8,128]{2,1,0:T(8,128)(2,1)S(1)} %analyse_grid.1), channel_id=1, replica_groups=mesh['band'=8,'lon'=4] {'band','lon'}, dimensions={0} | all-to-all | bytes 131072 | tf_op jit(solution)/shard_map/all_to_all | solution.py:351
  21.3 0.0 copy-done
  21.3 0.0 copy-done.3
  21.3 2.3 %spectral.1 = bf16[32,16,256]{2,1,0:T(8,128)(2,1)S(1)} custom-call(bf16[512,128]{1,0:T(8,128)(2,1)S(1)} %get-tuple-element.15.pick_ref, bf16[4,128,256]{2,1,0:T(8,128)(2,1)S(1)} %get-tuple-element.16.put_ref, s32[128,128]{1,0:T(8,128)S(1)} %get-tuple-element.17.rows_ref, bf16[32,8,128]{2,1,0:T(8,128)(2,1)S(1)} %all_to_all.10.folded_ref, ...), custom_call_target="tpu_custom_call" | custom-call | flops 4294967296 | bytes 1048576 | tf_op jit(solution)/shard_map/spectral/pallas_call | solution.py:354
  23.6 12.3 %all_to_all.11.values_ref = bf16[32,16,256]{2,1,0:T(8,128)(2,1)S(1)} all-to-all(bf16[32,16,256]{2,1,0:T(8,128)(2,1)S(1)} %spectral.1), channel_id=1, replica_groups=mesh['band'=8,'lon'=4] {'band','lon'}, dimensions={0} | all-to-all | bytes 524288 | tf_op jit(solution)/shard_map/all_to_all | solution.py:364
  35.8 1.4 %synthesise_grid.1 = f32[2,2,4,1024]{3,2,1,0:T(4,128)} custom-call(f32[2,8,8,128]{3,2,1,0:T(8,128)S(1)} %get-tuple-element.13.turn_ref, bf16[2,128,2048]{2,1,0:T(8,128)(2,1)S(1)} %get-tuple-element.14.basis_ref, bf16[32,16,256]{2,1,0:T(8,128)(2,1)S(1)} %all_to_all.11.values_ref), custom_call_target="tpu_custom_call" | custom-call | flops 2147483648 | bytes 1048576 | tf_op jit(solution)/shard_map/synthesise_grid/pallas_call | solution.py:366
Async XLA Ops:
  0.0 8.6 %collective-permute-start = (f32[2,2,4,1024]{3,2,1,0:T(4,128)}, f32[2,2,4,1024]{3,2,1,0:T(4,128)S(1)}, u32[]{:S(2)}, u32[]{:S(2)}) collective-permute-start(f32[2,2,4,1024]{3,2,1,0:T(4,128)} %refs_0_.1), channel_id=1, source_target_pairs={{0,1},{1,2},{2,3},{3,0},{4,5},{5,6},{6,7},{7,4},{8,9},{9,10},{10,1... | collective-permute-start | bytes 196616 | tf_op jit(solution)/shard_map/ppermute | solution.py:322
  0.5 8.1 %collective-permute-start.1 = (f32[2,2,4,1024]{3,2,1,0:T(4,128)}, f32[2,2,4,1024]{3,2,1,0:T(4,128)S(1)}, u32[]{:S(2)}, u32[]{:S(2)}) collective-permute-start(f32[2,2,4,1024]{3,2,1,0:T(4,128)} %refs_0_.1), channel_id=1, source_target_pairs={{0,2},{1,3},{2,0},{3,1},{4,6},{5,7},{6,4},{7,5},{8,10},{9,11},{10,... | collective-permute-start | bytes 196616 | tf_op jit(solution)/shard_map/ppermute | solution.py:322
  3.0 5.6 %collective-permute-start.2 = (f32[2,2,4,1024]{3,2,1,0:T(4,128)}, f32[2,2,4,1024]{3,2,1,0:T(4,128)S(1)}, u32[]{:S(2)}, u32[]{:S(2)}) collective-permute-start(f32[2,2,4,1024]{3,2,1,0:T(4,128)} %refs_0_.1), channel_id=1, source_target_pairs={{0,3},{1,0},{2,1},{3,2},{4,7},{5,4},{6,5},{7,6},{8,11},{9,8},{10,9... | collective-permute-start | bytes 196616 | tf_op jit(solution)/shard_map/ppermute | solution.py:322
  4.5 0.7 %copy-start.2 = (s32[1024]{0:T(1024)S(1)}, s32[1024]{0:T(1024)}, u32[]{:S(2)}) copy-start(s32[1024]{0:T(1024)} %param.10) | copy-start | bytes 12292
  5.2 0.7 %copy-start.4 = (f32[32]{0:T(128)S(1)}, f32[32]{0:T(128)}, u32[]{:S(2)}) copy-start(f32[32]{0:T(128)} %weight_ref.1) | copy-start | bytes 388
  5.8 0.7 %copy-start.5 = (s32[32]{0:T(128)S(1)}, s32[32]{0:T(128)}, u32[]{:S(2)}) copy-start(s32[32]{0:T(128)} %cycle_ref.1) | copy-start | bytes 388
  6.5 2.1 %copy-start.1 = (f32[2,2,4,1024]{3,2,1,0:T(4,128)S(1)}, f32[2,2,4,1024]{3,2,1,0:T(4,128)}, u32[]{:S(2)}) copy-start(f32[2,2,4,1024]{3,2,1,0:T(4,128)} %refs_0_.1) | copy-start | bytes 196612
  8.6 12.7 %copy-start = (bf16[128,256,32]{1,2,0:T(8,128)(2,1)S(1)}, bf16[128,256,32]{1,2,0:T(8,128)(2,1)}, u32[]{:S(2)}) copy-start(bf16[128,256,32]{1,2,0:T(8,128)(2,1)} %param.7) | copy-start | bytes 6291460
  8.6 12.7 %copy-start.3 = (f32[2,2,256]{2,1,0:T(2,128)S(1)}, f32[2,2,256]{2,1,0:T(2,128)}, u32[]{:S(2)}) copy-start(f32[2,2,256]{2,1,0:T(2,128)} %love_ref.1) | copy-start | bytes 12292

commit v3 on v2

--- a/solution.py
+++ b/solution.py
@@ -141,7 +141,8 @@
     found = iota((northern, LANES), 0) == cycle_lanes(2)
     for p in range(2):
         one = jnp.where(found & (parity_lane == p), 1.0, 0.0)
-        pick_ref[p * wide : (p + 1) * wide] = jnp.concatenate([one] * group, axis=0).astype(jnp.bfloat16)
+        copies = jnp.concatenate([one] * (LANES // northern), axis=0)
+        pick_ref[p * LANES : (p + 1) * LANES] = copies.astype(jnp.bfloat16)
 
     leaving = cycle_lanes(4).astype(jnp.float32)
     cycle_rows = jnp.transpose(jnp.broadcast_to(leaving, (LANES, LANES))).astype(jnp.int32)
@@ -183,60 +184,64 @@
     pick = pick_ref[...]
 
     pad = jnp.zeros((LANES - 2 * northern, LANES), jnp.float32)
+    turned = []
     for q in range(lon_count):
         pieces = [folded_ref[b * lon_count + q].astype(jnp.float32) for b in range(owners)]
-        turned = jnp.transpose(jnp.concatenate(pieces + [pad], axis=0)).astype(jnp.bfloat16)
-        spread_ref[q] = dot_nt(turned, pick)
+        turned.append(jnp.transpose(jnp.concatenate(pieces + [pad], axis=0)))
+    spread_ref[...] = dot_nt(jnp.concatenate(turned, axis=0).astype(jnp.bfloat16), pick)
 
     degree = lon * degrees + iota((ROWS, degrees), 1)
     diagonal = iota((ROWS, wide), 0) == iota((ROWS, wide), 1) // northern
     love = [[love_ref[g, f : f + 1, :] for f in range(2)] for g in range(2)]
-
-    for q in range(lon_count):
-        for pair in range(quarter // (2 * group)):
-            halves = []
-            for half in range(2):
-                first = (pair * 2 + half) * group
-                left = []
-                for f in range(2):
-                    for p in range(2):
-                        for c in range(2):
-                            at = (f * 2 + c) * quarter + first
-                            left.append(
-                                jnp.where(diagonal, spread_ref[q, at : at + group, p * wide : (p + 1) * wide], 0.0)
-                            )
-                left = jnp.concatenate(left, axis=0).astype(jnp.bfloat16)
-                start = (q * quarter + first) * northern
-                table = legendre_ref[start : start + wide]
-                analysed = dot(left, table)
-                order = rows_ref[q * quarter + first : q * quarter + first + group]
-                gap = degree - jnp.concatenate([order] * (degrees // LANES), axis=1)
-                valid = gap >= 0
-                keep = [valid & ((gap & 1) == p) for p in range(2)]
-                mixed = []
-                for g in range(2):
-                    for p in range(2):
-                        for c in range(2):
-                            lo = (p * 2 + c) * group
-                            hi = ((2 + p) * 2 + c) * group
-                            value = love[g][0] * analysed[lo : lo + group] + love[g][1] * analysed[hi : hi + group]
-                            mixed.append(jnp.where(keep[p], value, 0.0))
-                mixed = jnp.concatenate(mixed, axis=0).astype(jnp.bfloat16)
-                halves.append(dot_nt(mixed, table))
-            at = q * quarter + pair * 2 * group
-            for g in range(2):
+    groups = per_owner // group
+
+    def analyse(n):
+        q, first = n * group // quarter, n * group % quarter
+        left = []
+        for f in range(2):
+            for p in range(2):
                 for c in range(2):
-                    rows = []
-                    for half in range(2):
-                        even = halves[half][(g * 4 + c) * group : (g * 4 + c + 1) * group]
-                        odd = halves[half][(g * 4 + 2 + c) * group : (g * 4 + 3 + c) * group]
-                        rows.append((even, odd))
-                    for h in range(2):
-                        both = [even + odd if h == 0 else even - odd for even, odd in rows]
-                        both = [jnp.where(diagonal, value, 0.0) for value in both]
-                        kept_ref[g * 2 + h, c * per_owner + at : c * per_owner + at + 2 * group, :] = jnp.concatenate(
-                            both, axis=0
-                        ).astype(jnp.bfloat16)
+                    at = q * LANES + (f * 2 + c) * quarter + first
+                    piece = spread_ref[at : at + group, p * LANES : (p + 1) * LANES]
+                    left.append(jnp.where(diagonal, jnp.concatenate([piece] * (wide // LANES), axis=1), 0.0))
+        left = jnp.concatenate(left, axis=0).astype(jnp.bfloat16)
+        return dot(left, legendre_ref[n * wide : (n + 1) * wide])
+
+    def respond(n, analysed):
+        order = rows_ref[n * group : (n + 1) * group]
+        gap = degree - jnp.concatenate([order] * (degrees // LANES), axis=1)
+        valid = gap >= 0
+        keep = [valid & ((gap & 1) == p) for p in range(2)]
+        mixed = []
+        for g in range(2):
+            for p in range(2):
+                for c in range(2):
+                    lo = (p * 2 + c) * group
+                    hi = ((2 + p) * 2 + c) * group
+                    value = love[g][0] * analysed[lo : lo + group] + love[g][1] * analysed[hi : hi + group]
+                    mixed.append(jnp.where(keep[p], value, 0.0))
+        mixed = jnp.concatenate(mixed, axis=0).astype(jnp.bfloat16)
+        return dot_nt(mixed, legendre_ref[n * wide : (n + 1) * wide])
+
+    def keep_pair(n, halves):
+        for g in range(2):
+            for c in range(2):
+                lo, hi = (g * 4 + c) * group, (g * 4 + 2 + c) * group
+                rows = [(half[lo : lo + group], half[hi : hi + group]) for half in halves]
+                at = c * per_owner + n * group
+                for h in range(2):
+                    both = [even + odd if h == 0 else even - odd for even, odd in rows]
+                    both = [jnp.where(diagonal, value, 0.0) for value in both]
+                    kept_ref[g * 2 + h, at : at + 2 * group, :] = jnp.concatenate(both, axis=0).astype(jnp.bfloat16)
+
+    analysed, partial = {}, {}
+    for n in range(groups + 2):
+        if n < groups:
+            analysed[n] = analyse(n)
+        if 1 <= n <= groups:
+            partial[n - 1] = respond(n - 1, analysed.pop(n - 1))
+        if n >= 3 and n % 2 == 1:
+            keep_pair(n - 3, [partial.pop(n - 3), partial.pop(n - 2)])
 
     total = None
     for i in range(4):
@@ -253,6 +258,7 @@
     rows = values_ref.shape[1]
     cycles = out_ref.shape[2]
     count = owners * per_owner
+    half = blocks * rows
     for b in range(owners):
         value = values_ref[b * lon_count].astype(jnp.float32)
         for q in range(1, lon_count):
@@ -263,11 +269,10 @@
             ca, sa = turn_ref[0, b, a : a + 1], turn_ref[1, b, a : a + 1]
             for c, term in ((0, ca * re - sa * im), (1, -(sa * re + ca * im))):
                 high, low = split(term)
-                left_ref[0, a * rows : (a + 1) * rows, c * count + at : c * count + at + per_owner] = high
-                left_ref[1, a * rows : (a + 1) * rows, c * count + at : c * count + at + per_owner] = low
-    grid = dot_nt(left_ref[0], basis_ref[0])
-    grid = grid + dot_nt(left_ref[1], basis_ref[0])
-    grid = grid + dot_nt(left_ref[0], basis_ref[1])
+                left_ref[a * rows : (a + 1) * rows, c * count + at : c * count + at + per_owner] = high
+                left_ref[half + a * rows : half + (a + 1) * rows, c * count + at : c * count + at + per_owner] = low
+    grid = dot_nt(left_ref[...], basis_ref[0])
+    grid = grid[:half] + grid[half:] + dot_nt(left_ref[:half], basis_ref[1])
     for a in range(blocks):
         for g in range(2):
             for h in range(2):
@@ -328,7 +333,7 @@
             jax.ShapeDtypeStruct((3 * LANES, 2 * width), jnp.bfloat16),
             jax.ShapeDtypeStruct((2, count, width), jnp.float32),
             jax.ShapeDtypeStruct((2 * cycles, LANES), jnp.float32),
-            jax.ShapeDtypeStruct((2 * degrees, LANES), jnp.bfloat16),
+            jax.ShapeDtypeStruct((2 * LANES, LANES), jnp.bfloat16),
             jax.ShapeDtypeStruct((4, LANES, degrees), jnp.bfloat16),
             jax.ShapeDtypeStruct((per_owner, LANES), jnp.int32),
             jax.ShapeDtypeStruct((2, owners, blocks, per_owner), jnp.float32),
@@ -356,7 +361,7 @@
         jax.ShapeDtypeStruct((devices, 4 * cycles, 2 * per_owner), jnp.bfloat16),
         [vmem] * 6,
         [
-            pltpu.VMEM((lon_count, LANES, 2 * degrees), jnp.float32),
+            pltpu.VMEM((lon_count * LANES, 2 * LANES), jnp.float32),
             pltpu.VMEM((4, 2 * per_owner, degrees), jnp.bfloat16),
         ],
         1 << 32,
@@ -367,7 +372,7 @@
         functools.partial(synthesise_grid, lon_count),
         jax.ShapeDtypeStruct(loads.shape, jnp.float32),
         [vmem] * 3,
-        [pltpu.VMEM((2, 4 * cycles * blocks, 2 * owners * per_owner), jnp.bfloat16)],
+        [pltpu.VMEM((2 * 4 * cycles * blocks, 2 * owners * per_owner), jnp.bfloat16)],
         1 << 31,
     )(turns, basis, returned)
 

time: 37.5 us -> 36.9 us (0.984)
  Pallas kernels: 6.32 us -> 5.72 us
    pallas_call x1, Pallas kernels: 2.25 us -> 1.74 us  [per_device_kernels(): kernel(functools.partial(spectral, lon_count, owners), jax.ShapeDtypeStru...]
where the time goes in v3:
time: 36.9 us; the launch traced here: 36.7 us
  blocking collectives  24.4 us (66%)
  Pallas kernels  5.72 us (16%)
  starting transfers between devices  4.46 us (12%)
  local copies, waits for them, and re-layouts  2.01 us (5%)
    all_to_all x1, blocking collectives, per_device_kernels(): lax.all_to_all(values, everyone, split_axis=0, concat_axis=0, tiled=True)  12.3 us
    all_to_all x1, blocking collectives, per_device_kernels(): lax.all_to_all(folded, everyone, split_axis=0, concat_axis=0, tiled=True)  12.1 us
    ppermute x3, starting transfers between devices, per_device_kernels(): lax.ppermute(loads, 'lon', [(i, (i + k) % lon_count) for i in range(lon_c...  4.46 us
    pallas_call x1, Pallas kernels, per_device_kernels(): kernel(functools.partial(tables, lon_count, cycles, degrees, blocks, tota...  2.09 us
    unnamed x12, local copies, waits for them, and re-layouts  2.01 us
    pallas_call x1, Pallas kernels, per_device_kernels(): kernel(functools.partial(spectral, lon_count, owners), jax.ShapeDtypeStru...  1.74 us
    pallas_call x1, Pallas kernels, per_device_kernels(): kernel(functools.partial(synthesise_grid, lon_count), jax.ShapeDtypeStruc...  1.34 us
  transfers between devices with their start and end apart: 3, of which 0 were waited for; matrix products, arithmetic and copies ran while one was open for 0% of the time, Pallas kernels for 6%

profile of v3, /device:TPU:0, one launch (start us, length us, event | category | flops | bytes accessed | tf_op | source)
XLA Modules:
  0.0 36.7 jit_solution(15690913796714360552)
XLA Ops:
  0.0 0.5 %collective-permute-start = (f32[2,2,4,1024]{3,2,1,0:T(4,128)}, f32[2,2,4,1024]{3,2,1,0:T(4,128)S(1)}, u32[]{:S(2)}, u32[]{:S(2)}) collective-permute-start(f32[2,2,4,1024]{3,2,1,0:T(4,128)} %refs_0_.1), channel_id=1, source_target_pairs={{0,1},{1,2},{2,3},{3,0},{4,5},{5,6},{6,7},{7,4},{8,9},{9,10},{10,1... | collective-permute-start | bytes 196616 | tf_op jit(solution)/shard_map/ppermute | solution.py:327
  0.5 2.5 %collective-permute-start.1 = (f32[2,2,4,1024]{3,2,1,0:T(4,128)}, f32[2,2,4,1024]{3,2,1,0:T(4,128)S(1)}, u32[]{:S(2)}, u32[]{:S(2)}) collective-permute-start(f32[2,2,4,1024]{3,2,1,0:T(4,128)} %refs_0_.1), channel_id=1, source_target_pairs={{0,2},{1,3},{2,0},{3,1},{4,6},{5,7},{6,4},{7,5},{8,10},{9,11},{10,... | collective-permute-start | bytes 196616 | tf_op jit(solution)/shard_map/ppermute | solution.py:327
  3.0 1.5 %collective-permute-start.2 = (f32[2,2,4,1024]{3,2,1,0:T(4,128)}, f32[2,2,4,1024]{3,2,1,0:T(4,128)S(1)}, u32[]{:S(2)}, u32[]{:S(2)}) collective-permute-start(f32[2,2,4,1024]{3,2,1,0:T(4,128)} %refs_0_.1), channel_id=1, source_target_pairs={{0,3},{1,0},{2,1},{3,2},{4,7},{5,4},{6,5},{7,6},{8,11},{9,8},{10,9... | collective-permute-start | bytes 196616 | tf_op jit(solution)/shard_map/ppermute | solution.py:327
  4.5 0.0 copy-start.2
  4.5 0.7 %copy-done.2 = s32[1024]{0:T(1024)S(1)} copy-done((s32[1024]{0:T(1024)S(1)}, s32[1024]{0:T(1024)}, u32[]{:S(2)}) %copy-start.2) | copy-done | bytes 4120
  5.2 0.0 copy-start.4
  5.2 0.7 %copy-done.4 = f32[32]{0:T(128)S(1)} copy-done((f32[32]{0:T(128)S(1)}, f32[32]{0:T(128)}, u32[]{:S(2)}) %copy-start.4) | copy-done | bytes 152
  5.8 0.0 copy-start.5
  5.8 0.7 %copy-done.5 = s32[32]{0:T(128)S(1)} copy-done((s32[32]{0:T(128)S(1)}, s32[32]{0:T(128)}, u32[]{:S(2)}) %copy-start.5) | copy-done | bytes 152
  6.5 0.0 copy-start.1
  6.5 2.1 %tables.1 = (bf16[384,512]{1,0:T(8,128)(2,1)S(1)}, f32[2,32,256]{2,1,0:T(8,128)S(1)}, f32[8,128]{1,0:T(8,128)S(1)}, bf16[256,128]{1,0:T(8,128)(2,1)S(1)}, bf16[4...) custom-call(s32[8,128]{1,0:T(8,128)S(1)} %bitcast.5, ...), custom_call_target="tpu_custom_call" | custom-call | flops 2147483648 | bytes 1048576 | tf_op jit(solution)/shard_map/tables/pallas_call | solution.py:330
  8.6 0.0 collective-permute-done.refs_1_
  8.6 0.0 collective-permute-done.1.refs_2_
  8.6 0.0 collective-permute-done.2.refs_3_
  8.6 0.0 copy-done.1
  8.6 0.0 copy-start
  8.6 0.0 copy-start.3
  8.6 0.5 %analyse_grid.1 = bf16[32,8,128]{2,1,0:T(8,128)(2,1)S(1)} custom-call(bf16[384,512]{1,0:T(8,128)(2,1)S(1)} %get-tuple-element.18.right_ref, f32[2,32,256]{2,1,0:T(8,128)S(1)} %get-tuple-element.19.turn_ref, f32[8,128]{1,0:T(8,128)S(1)} %get-tuple-element.20.weight_ref, f32[2,2,4,1024]{3,2,1,0:T(4,128)S(1)} %copy-done.1, ...), custom_call_target="tpu_custom_call" | custom-call | flops 2147483648 | bytes 1048576 | tf_op jit(solution)/shard_map/analyse_grid/pallas_call | solution.py:346
  9.2 12.1 %all_to_all.10.folded_ref = bf16[32,8,128]{2,1,0:T(8,128)(2,1)S(1)} all-to-all(bf16[32,8,128]{2,1,0:T(8,128)(2,1)S(1)} %analyse_grid.1), channel_id=1, replica_groups=mesh['band'=8,'lon'=4] {'band','lon'}, dimensions={0} | all-to-all | bytes 131072 | tf_op jit(solution)/shard_map/all_to_all | solution.py:356
  21.3 0.0 copy-done
  21.3 0.0 copy-done.3
  21.3 1.7 %spectral.1 = bf16[32,16,256]{2,1,0:T(8,128)(2,1)S(1)} custom-call(bf16[256,128]{1,0:T(8,128)(2,1)S(1)} %get-tuple-element.15.pick_ref, bf16[4,128,256]{2,1,0:T(8,128)(2,1)S(1)} %get-tuple-element.16.put_ref, s32[128,128]{1,0:T(8,128)S(1)} %get-tuple-element.17.rows_ref, bf16[32,8,128]{2,1,0:T(8,128)(2,1)S(1)} %all_to_all.10.folded_ref, ...), custom_call_target="tpu_custom_call" | custom-call | flops 4294967296 | bytes 1048576 | tf_op jit(solution)/shard_map/spectral/pallas_call | solution.py:359
  23.0 12.3 %all_to_all.11.values_ref = bf16[32,16,256]{2,1,0:T(8,128)(2,1)S(1)} all-to-all(bf16[32,16,256]{2,1,0:T(8,128)(2,1)S(1)} %spectral.1), channel_id=1, replica_groups=mesh['band'=8,'lon'=4] {'band','lon'}, dimensions={0} | all-to-all | bytes 524288 | tf_op jit(solution)/shard_map/all_to_all | solution.py:369
  35.3 1.3 %synthesise_grid.1 = f32[2,2,4,1024]{3,2,1,0:T(4,128)} custom-call(f32[2,8,8,128]{3,2,1,0:T(8,128)S(1)} %get-tuple-element.13.turn_ref, bf16[2,128,2048]{2,1,0:T(8,128)(2,1)S(1)} %get-tuple-element.14.basis_ref, bf16[32,16,256]{2,1,0:T(8,128)(2,1)S(1)} %all_to_all.11.values_ref), custom_call_target="tpu_custom_call" | custom-call | flops 2147483648 | bytes 1048576 | tf_op jit(solution)/shard_map/synthesise_grid/pallas_call | solution.py:371
Async XLA Ops:
  0.0 8.6 %collective-permute-start = (f32[2,2,4,1024]{3,2,1,0:T(4,128)}, f32[2,2,4,1024]{3,2,1,0:T(4,128)S(1)}, u32[]{:S(2)}, u32[]{:S(2)}) collective-permute-start(f32[2,2,4,1024]{3,2,1,0:T(4,128)} %refs_0_.1), channel_id=1, source_target_pairs={{0,1},{1,2},{2,3},{3,0},{4,5},{5,6},{6,7},{7,4},{8,9},{9,10},{10,1... | collective-permute-start | bytes 196616 | tf_op jit(solution)/shard_map/ppermute | solution.py:327
  0.5 8.1 %collective-permute-start.1 = (f32[2,2,4,1024]{3,2,1,0:T(4,128)}, f32[2,2,4,1024]{3,2,1,0:T(4,128)S(1)}, u32[]{:S(2)}, u32[]{:S(2)}) collective-permute-start(f32[2,2,4,1024]{3,2,1,0:T(4,128)} %refs_0_.1), channel_id=1, source_target_pairs={{0,2},{1,3},{2,0},{3,1},{4,6},{5,7},{6,4},{7,5},{8,10},{9,11},{10,... | collective-permute-start | bytes 196616 | tf_op jit(solution)/shard_map/ppermute | solution.py:327
  3.0 5.6 %collective-permute-start.2 = (f32[2,2,4,1024]{3,2,1,0:T(4,128)}, f32[2,2,4,1024]{3,2,1,0:T(4,128)S(1)}, u32[]{:S(2)}, u32[]{:S(2)}) collective-permute-start(f32[2,2,4,1024]{3,2,1,0:T(4,128)} %refs_0_.1), channel_id=1, source_target_pairs={{0,3},{1,0},{2,1},{3,2},{4,7},{5,4},{6,5},{7,6},{8,11},{9,8},{10,9... | collective-permute-start | bytes 196616 | tf_op jit(solution)/shard_map/ppermute | solution.py:327
  4.5 0.7 %copy-start.2 = (s32[1024]{0:T(1024)S(1)}, s32[1024]{0:T(1024)}, u32[]{:S(2)}) copy-start(s32[1024]{0:T(1024)} %param.10) | copy-start | bytes 12292
  5.2 0.7 %copy-start.4 = (f32[32]{0:T(128)S(1)}, f32[32]{0:T(128)}, u32[]{:S(2)}) copy-start(f32[32]{0:T(128)} %weight_ref.1) | copy-start | bytes 388
  5.8 0.7 %copy-start.5 = (s32[32]{0:T(128)S(1)}, s32[32]{0:T(128)}, u32[]{:S(2)}) copy-start(s32[32]{0:T(128)} %cycle_ref.1) | copy-start | bytes 388
  6.5 2.1 %copy-start.1 = (f32[2,2,4,1024]{3,2,1,0:T(4,128)S(1)}, f32[2,2,4,1024]{3,2,1,0:T(4,128)}, u32[]{:S(2)}) copy-start(f32[2,2,4,1024]{3,2,1,0:T(4,128)} %refs_0_.1) | copy-start | bytes 196612
  8.6 12.7 %copy-start = (bf16[128,256,32]{1,2,0:T(8,128)(2,1)S(1)}, bf16[128,256,32]{1,2,0:T(8,128)(2,1)}, u32[]{:S(2)}) copy-start(bf16[128,256,32]{1,2,0:T(8,128)(2,1)} %param.7) | copy-start | bytes 6291460
  8.6 12.7 %copy-start.3 = (f32[2,2,256]{2,1,0:T(2,128)S(1)}, f32[2,2,256]{2,1,0:T(2,128)}, u32[]{:S(2)}) copy-start(f32[2,2,256]{2,1,0:T(2,128)} %love_ref.1) | copy-start | bytes 12292

commit v4 on v3

--- a/solution.py
+++ b/solution.py
@@ -155,21 +155,28 @@
     own = orders_ref[pl.ds(band, 1), :].astype(jnp.float32)
     rows_ref[...] = jnp.transpose(jnp.broadcast_to(own, (LANES, per_owner))).astype(jnp.int32)
 
+    share = per_owner // 2
+    first_lanes = lane < share
+
+    def halves(x, y):
+        return jnp.where(first_lanes, x, pltpu.roll(y, share, 1)), jnp.where(first_lanes, pltpu.roll(x, share, 1), y)
+
     scale = 1.0 / math.sqrt(total)
-    count = owners * per_owner
     for b in range(owners):
         order = orders_ref[b : b + 1, :]
         factor = jnp.where(order == 0, scale, 2.0 * scale)
         step = iota((blocks, per_owner), 0) + lon * blocks
         cos_a, sin_a = turn((step * LANES * order) & (total - 1), total)
-        turn_ref[0, b] = cos_a * factor
-        turn_ref[1, b] = sin_a * factor
+        cos_a, sin_a = cos_a * factor, sin_a * factor
+        for half, table in enumerate(halves(cos_a, -cos_a)):
+            turn_ref[half, 0, b] = table
+        for half, table in enumerate(halves(-sin_a, -sin_a)):
+            turn_ref[half, 1, b] = table
         cos_b, sin_b = turn((iota((LANES, per_owner), 0) * order) & (total - 1), total)
-        for c, table in ((0, cos_b), (1, sin_b)):
+        for half, table in enumerate(halves(cos_b, sin_b)):
             high, low = split(table)
-            at = c * count + b * per_owner
-            basis_ref[0, :, at : at + per_owner] = high
-            basis_ref[1, :, at : at + per_owner] = low
+            basis_ref[half, 0, :, b * per_owner : (b + 1) * per_owner] = high
+            basis_ref[half, 1, :, b * per_owner : (b + 1) * per_owner] = low
 
 
 def spectral(lon_count, owners, pick_ref, put_ref, rows_ref, folded_ref, legendre_ref, love_ref, out_ref, spread_ref, kept_ref):
@@ -181,6 +188,7 @@
     group = degrees // northern
     wide = group * northern
     lon = lax.axis_index("lon")
+    share = per_owner // 2
     pick = pick_ref[...]
 
     pad = jnp.zeros((LANES - 2 * northern, LANES), jnp.float32)
@@ -228,7 +236,7 @@
             for c in range(2):
                 lo, hi = (g * 4 + c) * group, (g * 4 + 2 + c) * group
                 rows = [(half[lo : lo + group], half[hi : hi + group]) for half in halves]
-                at = c * per_owner + n * group
+                at = (n * group // share * 2 + c) * share + n * group % share
                 for h in range(2):
                     both = [even + odd if h == 0 else even - odd for even, odd in rows]
                     both = [jnp.where(diagonal, value, 0.0) for value in both]
@@ -250,30 +258,43 @@
     total = total.astype(out_ref.dtype)
     for b in range(owners):
         for q in range(lon_count):
-            out_ref[b * lon_count + q] = total[b * 4 * cycles : (b + 1) * 4 * cycles]
-
-
-def synthesise_grid(lon_count, turn_ref, basis_ref, values_ref, out_ref, left_ref):
-    owners, blocks, per_owner = turn_ref.shape[1:]
-    rows = values_ref.shape[1]
-    cycles = out_ref.shape[2]
-    count = owners * per_owner
-    half = blocks * rows
-    for b in range(owners):
+            lanes = slice(q % 2 * 2 * share, (q % 2 + 1) * 2 * share)
+            out_ref[b * lon_count + q] = total[b * 4 * cycles : (b + 1) * 4 * cycles, lanes]
+
+
+def add_degrees(lon_count, values_ref, out_ref):
+    for b in range(out_ref.shape[0]):
         value = values_ref[b * lon_count].astype(jnp.float32)
         for q in range(1, lon_count):
             value = value + values_ref[b * lon_count + q].astype(jnp.float32)
-        re, im = value[:, :per_owner], value[:, per_owner:]
-        at = b * per_owner
+        out_ref[b] = value
+
+
+def half_grid(which, turn_ref, basis_ref, value_ref, left_ref):
+    owners, rows, lanes = value_ref.shape
+    blocks = turn_ref.shape[3]
+    height = blocks * rows
+    for b in range(owners):
+        value = value_ref[b]
+        other = pltpu.roll(value, lanes // 2, 1)
         for a in range(blocks):
-            ca, sa = turn_ref[0, b, a : a + 1], turn_ref[1, b, a : a + 1]
-            for c, term in ((0, ca * re - sa * im), (1, -(sa * re + ca * im))):
-                high, low = split(term)
-                left_ref[a * rows : (a + 1) * rows, c * count + at : c * count + at + per_owner] = high
-                left_ref[half + a * rows : half + (a + 1) * rows, c * count + at : c * count + at + per_owner] = low
-    grid = dot_nt(left_ref[...], basis_ref[0])
-    grid = grid[:half] + grid[half:] + dot_nt(left_ref[:half], basis_ref[1])
-    for a in range(blocks):
+            term = value * turn_ref[which, 0, b, a : a + 1] + other * turn_ref[which, 1, b, a : a + 1]
+            high, low = split(term)
+            left_ref[a * rows : (a + 1) * rows, b * lanes : (b + 1) * lanes] = high
+            left_ref[height + a * rows : height + (a + 1) * rows, b * lanes : (b + 1) * lanes] = low
+    grid = dot_nt(left_ref[...], basis_ref[which, 0])
+    return grid[:height] + grid[height:] + dot_nt(left_ref[:height], basis_ref[which, 1])
+
+
+def own_grid(turn_ref, basis_ref, value_ref, out_ref, left_ref):
+    out_ref[...] = half_grid(lax.axis_index("lon") % 2, turn_ref, basis_ref, value_ref, left_ref)
+
+
+def synthesise_grid(turn_ref, basis_ref, value_ref, grid_ref, out_ref, left_ref):
+    rows = value_ref.shape[1]
+    cycles = out_ref.shape[2]
+    grid = grid_ref[...] + half_grid(1 - lax.axis_index("lon") % 2, turn_ref, basis_ref, value_ref, left_ref)
+    for a in range(grid.shape[0] // rows):
         for g in range(2):
             for h in range(2):
                 at = a * rows + (g * 2 + h) * cycles
@@ -286,6 +307,7 @@
     return (
         per_owner == LANES
         and 4 * per_owner == lon_count * LANES
+        and lon_count % 2 == 0
         and 2 * cycles == ROWS
         and 4 * northern == LANES
         and ROWS * northern == degrees
@@ -336,8 +358,8 @@
             jax.ShapeDtypeStruct((2 * LANES, LANES), jnp.bfloat16),
             jax.ShapeDtypeStruct((4, LANES, degrees), jnp.bfloat16),
             jax.ShapeDtypeStruct((per_owner, LANES), jnp.int32),
-            jax.ShapeDtypeStruct((2, owners, blocks, per_owner), jnp.float32),
-            jax.ShapeDtypeStruct((2, LANES, 2 * owners * per_owner), jnp.bfloat16),
+            jax.ShapeDtypeStruct((2, 2, owners, blocks, per_owner), jnp.float32),
+            jax.ShapeDtypeStruct((2, 2, LANES, owners * per_owner), jnp.bfloat16),
         ),
         [vmem, smem, smem],
         [],
@@ -358,7 +380,7 @@
     rows = jnp.transpose(legendre, (0, 2, 1)).reshape(per_owner * northern, degrees)
     values = kernel(
         functools.partial(spectral, lon_count, owners),
-        jax.ShapeDtypeStruct((devices, 4 * cycles, 2 * per_owner), jnp.bfloat16),
+        jax.ShapeDtypeStruct((devices, 4 * cycles, per_owner), jnp.bfloat16),
         [vmem] * 6,
         [
             pltpu.VMEM((lon_count * LANES, 2 * LANES), jnp.float32),
@@ -368,13 +390,21 @@
     )(pick, put, order_rows, arrived, rows, love)
     returned = lax.all_to_all(values, everyone, split_axis=0, concat_axis=0, tiled=True)
 
-    return kernel(
-        functools.partial(synthesise_grid, lon_count),
-        jax.ShapeDtypeStruct(loads.shape, jnp.float32),
-        [vmem] * 3,
-        [pltpu.VMEM((2 * 4 * cycles * blocks, 2 * owners * per_owner), jnp.bfloat16)],
-        1 << 31,
-    )(turns, basis, returned)
+    own = kernel(
+        functools.partial(add_degrees, lon_count),
+        jax.ShapeDtypeStruct((owners, 4 * cycles, per_owner), jnp.float32),
+        [vmem],
+        [],
+        1 << 28,
+    )(returned)
+    other = lax.ppermute(own, "lon", [(i, i ^ 1) for i in range(lon_count)])
+    left = [pltpu.VMEM((2 * 4 * cycles * blocks, owners * per_owner), jnp.bfloat16)]
+    grid = kernel(
+        own_grid, jax.ShapeDtypeStruct((4 * cycles * blocks, LANES), jnp.float32), [vmem] * 3, left, 1 << 30
+    )(turns, basis, own)
+    return kernel(synthesise_grid, jax.ShapeDtypeStruct(loads.shape, jnp.float32), [vmem] * 4, left, 1 << 30)(
+        turns, basis, other, grid
+    )
 
 
 def per_device(loads, legendre, love, cycle_weight, order_list, cycle_order):

time: 36.9 us -> 35.5 us (0.962)
  blocking collectives: 24.4 us -> 22 us
  waiting for transfers between devices: 0.01 us -> 0.55 us
    all_to_all x1, blocking collectives: 12.3 us -> 9.91 us  [per_device_kernels(): lax.all_to_all(values, everyone, split_axis=0, concat_axis=0, tiled=True)]
    ppermute x0 -> x1, waiting for transfers between devices: none -> 0.54 us  [per_device_kernels(): other = lax.ppermute(own, 'lon', [(i, i ^ 1) for i in range(lon_count)])]
    pallas_call x1 -> x3, Pallas kernels: 1.34 us -> 1.7 us  [the longest x1 1.19 us: per_device_kernels(): kernel(synthesise_grid, jax.ShapeDtypeStruct(loads.shape, jnp.float32), [...]
  transfers between devices with their start and end apart: 3 -> 4, of which waited for: 0 -> 1; matrix products, arithmetic and copies ran while one was open for 0% -> 0% of each run, Pallas kernels for 6% -> 7%
where the time goes in v4:
time: 35.5 us; the launch traced here: 35.3 us
  blocking collectives  22 us (62%)
  Pallas kernels  5.86 us (17%)
  starting transfers between devices  4.74 us (13%)
  local copies, waits for them, and re-layouts  2.01 us (6%)
  waiting for transfers between devices  0.55 us (2%)
    all_to_all x1, blocking collectives, per_device_kernels(): lax.all_to_all(folded, everyone, split_axis=0, concat_axis=0, tiled=True)  12.1 us
    all_to_all x1, blocking collectives, per_device_kernels(): lax.all_to_all(values, everyone, split_axis=0, concat_axis=0, tiled=True)  9.91 us
    ppermute x3, starting transfers between devices, per_device_kernels(): lax.ppermute(loads, 'lon', [(i, (i + k) % lon_count) for i in range(lon_c...  4.46 us
    unnamed x12, local copies, waits for them, and re-layouts  2.01 us
    pallas_call x1, Pallas kernels, per_device_kernels(): kernel(functools.partial(tables, lon_count, cycles, degrees, blocks, tota...  1.89 us
    pallas_call x1, Pallas kernels, per_device_kernels(): kernel(functools.partial(spectral, lon_count, owners), jax.ShapeDtypeStru...  1.72 us
    pallas_call x1, Pallas kernels, per_device_kernels(): kernel(synthesise_grid, jax.ShapeDtypeStruct(loads.shape, jnp.float32), [...  1.19 us
  transfers between devices with their start and end apart: 4, of which 1 were waited for; matrix products, arithmetic and copies ran while one was open for 0% of the time, Pallas kernels for 7%

profile of v4, /device:TPU:0, one launch (start us, length us, event | category | flops | bytes accessed | tf_op | source)
XLA Modules:
  0.0 35.3 jit_solution(6925626293259129777)
XLA Ops:
  0.0 0.5 %collective-permute-start = (f32[2,2,4,1024]{3,2,1,0:T(4,128)}, f32[2,2,4,1024]{3,2,1,0:T(4,128)S(1)}, u32[]{:S(2)}, u32[]{:S(2)}) collective-permute-start(f32[2,2,4,1024]{3,2,1,0:T(4,128)} %refs_0_.1), channel_id=1, source_target_pairs={{0,1},{1,2},{2,3},{3,0},{4,5},{5,6},{6,7},{7,4},{8,9},{9,10},{10,1... | collective-permute-start | bytes 196616 | tf_op jit(solution)/shard_map/ppermute | solution.py:349
  0.5 2.5 %collective-permute-start.1 = (f32[2,2,4,1024]{3,2,1,0:T(4,128)}, f32[2,2,4,1024]{3,2,1,0:T(4,128)S(1)}, u32[]{:S(2)}, u32[]{:S(2)}) collective-permute-start(f32[2,2,4,1024]{3,2,1,0:T(4,128)} %refs_0_.1), channel_id=1, source_target_pairs={{0,2},{1,3},{2,0},{3,1},{4,6},{5,7},{6,4},{7,5},{8,10},{9,11},{10,... | collective-permute-start | bytes 196616 | tf_op jit(solution)/shard_map/ppermute | solution.py:349
  3.0 1.5 %collective-permute-start.2 = (f32[2,2,4,1024]{3,2,1,0:T(4,128)}, f32[2,2,4,1024]{3,2,1,0:T(4,128)S(1)}, u32[]{:S(2)}, u32[]{:S(2)}) collective-permute-start(f32[2,2,4,1024]{3,2,1,0:T(4,128)} %refs_0_.1), channel_id=1, source_target_pairs={{0,3},{1,0},{2,1},{3,2},{4,7},{5,4},{6,5},{7,6},{8,11},{9,8},{10,9... | collective-permute-start | bytes 196616 | tf_op jit(solution)/shard_map/ppermute | solution.py:349
  4.5 0.0 copy-start.2
  4.5 0.7 %copy-done.2 = s32[1024]{0:T(1024)S(1)} copy-done((s32[1024]{0:T(1024)S(1)}, s32[1024]{0:T(1024)}, u32[]{:S(2)}) %copy-start.2) | copy-done | bytes 4120
  5.2 0.0 copy-start.4
  5.2 0.7 %copy-done.4 = f32[32]{0:T(128)S(1)} copy-done((f32[32]{0:T(128)S(1)}, f32[32]{0:T(128)}, u32[]{:S(2)}) %copy-start.4) | copy-done | bytes 152
  5.8 0.0 copy-start.5
  5.8 0.7 %copy-done.5 = s32[32]{0:T(128)S(1)} copy-done((s32[32]{0:T(128)S(1)}, s32[32]{0:T(128)}, u32[]{:S(2)}) %copy-start.5) | copy-done | bytes 152
  6.5 0.0 copy-start.1
  6.5 1.9 %tables.1 = (bf16[384,512]{1,0:T(8,128)(2,1)S(1)}, f32[2,32,256]{2,1,0:T(8,128)S(1)}, f32[8,128]{1,0:T(8,128)S(1)}, bf16[256,128]{1,0:T(8,128)(2,1)S(1)}, bf16[4...) custom-call(s32[8,128]{1,0:T(8,128)S(1)} %bitcast.5, ...), custom_call_target="tpu_custom_call" | custom-call | flops 2147483648 | bytes 1048576 | tf_op jit(solution)/shard_map/tables/pallas_call | solution.py:352
  8.4 0.0 collective-permute-done.refs_1_
  8.4 0.0 collective-permute-done.1.refs_2_
  8.4 0.0 collective-permute-done.2.refs_3_
  8.4 0.0 copy-done.1
  8.4 0.0 copy-start
  8.4 0.0 copy-start.3
  8.4 0.5 %analyse_grid.1 = bf16[32,8,128]{2,1,0:T(8,128)(2,1)S(1)} custom-call(bf16[384,512]{1,0:T(8,128)(2,1)S(1)} %get-tuple-element.18.right_ref, f32[2,32,256]{2,1,0:T(8,128)S(1)} %get-tuple-element.19.turn_ref, f32[8,128]{1,0:T(8,128)S(1)} %get-tuple-element.20.weight_ref, f32[2,2,4,1024]{3,2,1,0:T(4,128)S(1)} %copy-done.1, ...), custom_call_target="tpu_custom_call" | custom-call | flops 2147483648 | bytes 1048576 | tf_op jit(solution)/shard_map/analyse_grid/pallas_call | solution.py:368
  9.0 12.1 %all_to_all.10.folded_ref = bf16[32,8,128]{2,1,0:T(8,128)(2,1)S(1)} all-to-all(bf16[32,8,128]{2,1,0:T(8,128)(2,1)S(1)} %analyse_grid.1), channel_id=1, replica_groups=mesh['band'=8,'lon'=4] {'band','lon'}, dimensions={0} | all-to-all | bytes 131072 | tf_op jit(solution)/shard_map/all_to_all | solution.py:378
  21.1 0.0 copy-done
  21.1 0.0 copy-done.3
  21.1 1.7 %spectral.1 = bf16[32,16,128]{2,1,0:T(8,128)(2,1)S(1)} custom-call(bf16[256,128]{1,0:T(8,128)(2,1)S(1)} %get-tuple-element.15.pick_ref, bf16[4,128,256]{2,1,0:T(8,128)(2,1)S(1)} %get-tuple-element.16.put_ref, s32[128,128]{1,0:T(8,128)S(1)} %get-tuple-element.17.rows_ref, bf16[32,8,128]{2,1,0:T(8,128)(2,1)S(1)} %all_to_all.10.folded_ref, ...), custom_call_target="tpu_custom_call" | custom-call | flops 4294967296 | bytes 1048576 | tf_op jit(solution)/shard_map/spectral/pallas_call | solution.py:381
  22.8 9.9 %all_to_all.11.values_ref = bf16[32,16,128]{2,1,0:T(8,128)(2,1)S(1)} all-to-all(bf16[32,16,128]{2,1,0:T(8,128)(2,1)S(1)} %spectral.1), channel_id=1, replica_groups=mesh['band'=8,'lon'=4] {'band','lon'}, dimensions={0} | all-to-all | bytes 262144 | tf_op jit(solution)/shard_map/all_to_all | solution.py:391
  32.7 0.3 collective-permute-start.3
  33.0 0.5 %own_grid.1.grid_ref = f32[128,128]{1,0:T(8,128)S(1)} custom-call(f32[2,2,8,8,128]{4,3,2,1,0:T(8,128)S(1)} %get-tuple-element.13.turn_ref, bf16[2,2,128,1024]{3,2,1,0:T(8,128)(2,1)S(1)} %get-tuple-element.14.basis_ref, f32[8,16,128]{2,1,0:T(8,128)S(1)} %add_degrees.1.value_ref), custom_call_target="tpu_custom_call" | custom-call | flops 1073741824 | bytes 1048576 | tf_op jit(solution)/shard_map/own_grid/pallas_call | solution.py:402
  33.5 0.5 %collective-permute-done.3.value_ref = f32[8,16,128]{2,1,0:T(8,128)S(1)} collective-permute-done((f32[8,16,128]{2,1,0:T(8,128)S(1)}, f32[8,16,128]{2,1,0:T(8,128)S(1)}, u32[]{:S(2)}, u32[]{:S(2)}) %collective-permute-start.3) | collective-permute-done | bytes 65568 | tf_op jit(solution)/shard_map/ppermute | solution.py:400
  34.1 1.2 %synthesise_grid.1 = f32[2,2,4,1024]{3,2,1,0:T(4,128)} custom-call(f32[2,2,8,8,128]{4,3,2,1,0:T(8,128)S(1)} %get-tuple-element.13.turn_ref, bf16[2,2,128,1024]{3,2,1,0:T(8,128)(2,1)S(1)} %get-tuple-element.14.basis_ref, f32[8,16,128]{2,1,0:T(8,128)S(1)} %collective-permute-done.3.value_ref, f32[128,128]{1,0:T(8,128)S(1)} %own_grid.1.grid_ref), custom_call_target="tpu_custom_call" | custom-call | flops 1073741824 | bytes 1048576 | tf_op jit(solution)/shard_map/synthesise_grid/pallas_call | solution.py:405
  (1 shorter events, 0.0 us)
Async XLA Ops:
  0.0 8.4 %collective-permute-start = (f32[2,2,4,1024]{3,2,1,0:T(4,128)}, f32[2,2,4,1024]{3,2,1,0:T(4,128)S(1)}, u32[]{:S(2)}, u32[]{:S(2)}) collective-permute-start(f32[2,2,4,1024]{3,2,1,0:T(4,128)} %refs_0_.1), channel_id=1, source_target_pairs={{0,1},{1,2},{2,3},{3,0},{4,5},{5,6},{6,7},{7,4},{8,9},{9,10},{10,1... | collective-permute-start | bytes 196616 | tf_op jit(solution)/shard_map/ppermute | solution.py:349
  0.5 7.9 %collective-permute-start.1 = (f32[2,2,4,1024]{3,2,1,0:T(4,128)}, f32[2,2,4,1024]{3,2,1,0:T(4,128)S(1)}, u32[]{:S(2)}, u32[]{:S(2)}) collective-permute-start(f32[2,2,4,1024]{3,2,1,0:T(4,128)} %refs_0_.1), channel_id=1, source_target_pairs={{0,2},{1,3},{2,0},{3,1},{4,6},{5,7},{6,4},{7,5},{8,10},{9,11},{10,... | collective-permute-start | bytes 196616 | tf_op jit(solution)/shard_map/ppermute | solution.py:349
  3.0 5.4 %collective-permute-start.2 = (f32[2,2,4,1024]{3,2,1,0:T(4,128)}, f32[2,2,4,1024]{3,2,1,0:T(4,128)S(1)}, u32[]{:S(2)}, u32[]{:S(2)}) collective-permute-start(f32[2,2,4,1024]{3,2,1,0:T(4,128)} %refs_0_.1), channel_id=1, source_target_pairs={{0,3},{1,0},{2,1},{3,2},{4,7},{5,4},{6,5},{7,6},{8,11},{9,8},{10,9... | collective-permute-start | bytes 196616 | tf_op jit(solution)/shard_map/ppermute | solution.py:349
  4.5 0.7 %copy-start.2 = (s32[1024]{0:T(1024)S(1)}, s32[1024]{0:T(1024)}, u32[]{:S(2)}) copy-start(s32[1024]{0:T(1024)} %param.10) | copy-start | bytes 12292
  5.2 0.7 %copy-start.4 = (f32[32]{0:T(128)S(1)}, f32[32]{0:T(128)}, u32[]{:S(2)}) copy-start(f32[32]{0:T(128)} %weight_ref.1) | copy-start | bytes 388
  5.8 0.7 %copy-start.5 = (s32[32]{0:T(128)S(1)}, s32[32]{0:T(128)}, u32[]{:S(2)}) copy-start(s32[32]{0:T(128)} %cycle_ref.1) | copy-start | bytes 388
  6.5 1.9 %copy-start.1 = (f32[2,2,4,1024]{3,2,1,0:T(4,128)S(1)}, f32[2,2,4,1024]{3,2,1,0:T(4,128)}, u32[]{:S(2)}) copy-start(f32[2,2,4,1024]{3,2,1,0:T(4,128)} %refs_0_.1) | copy-start | bytes 196612
  8.4 12.7 %copy-start = (bf16[128,256,32]{1,2,0:T(8,128)(2,1)S(1)}, bf16[128,256,32]{1,2,0:T(8,128)(2,1)}, u32[]{:S(2)}) copy-start(bf16[128,256,32]{1,2,0:T(8,128)(2,1)} %param.7) | copy-start | bytes 6291460
  8.4 12.7 %copy-start.3 = (f32[2,2,256]{2,1,0:T(2,128)S(1)}, f32[2,2,256]{2,1,0:T(2,128)}, u32[]{:S(2)}) copy-start(f32[2,2,256]{2,1,0:T(2,128)} %love_ref.1) | copy-start | bytes 12292
  32.7 1.3 %collective-permute-start.3 = (f32[8,16,128]{2,1,0:T(8,128)S(1)}, f32[8,16,128]{2,1,0:T(8,128)S(1)}, u32[]{:S(2)}, u32[]{:S(2)}) collective-permute-start(f32[8,16,128]{2,1,0:T(8,128)S(1)} %add_degrees.1.value_ref), channel_id=1, source_target_pairs={{0,1},{1,0},{2,3},{3,2},{4,5},{5,4},{6,7},{7,6},{8,9},{9,8},{10,11... | collective-permute-start | bytes 196616 | tf_op jit(solution)/shard_map/ppermute | solution.py:400

commit v5 on v4

--- a/solution.py
+++ b/solution.py
@@ -49,12 +49,12 @@
 
 def analyse_grid(right_ref, turn_ref, weight_ref, *refs):
     parts, out_ref, points_ref, mid_ref = refs[:-3], refs[-3], refs[-2], refs[-1]
-    lon_count = len(parts)
     cycles = parts[0].shape[2]
     blocks = parts[0].shape[3] // LANES
-    owners = out_ref.shape[0] // lon_count
     count, width = turn_ref.shape[1:]
-    quarter = width // owners
+    owners = width // (LANES // 2)
+    lon_count = out_ref.shape[0] // owners
+    quarter = width // owners // 2
     pieces = LANES // quarter
     step = 2 * cycles
 
@@ -81,89 +81,69 @@
     slot = iota((1, LANES), 1) // quarter
     weight = weight_ref[...]
     for owner in range(owners):
-        t, i = owner // pieces, owner % pieces
-        block = None
-        for e in range(4):
-            piece = sums[e // 2][e % 2][:, t * LANES : (t + 1) * LANES]
-            move = (e - i) * quarter % LANES
-            piece = pltpu.roll(piece, move, 1) if move else piece
-            block = piece if block is None else jnp.where(slot == e, piece, block)
-        block = (block * weight).astype(out_ref.dtype)
-        for q in range(lon_count):
-            out_ref[owner * lon_count + q] = block
-
-
-def tables(lon_count, cycles, degrees, blocks, total, orders_ref, weight_ref, cycle_ref, *out_refs):
-    right_ref, first_ref, column_ref, pick_ref, put_ref, rows_ref, turn_ref, basis_ref = out_refs
+        for side in range(2):
+            t, i = (2 * owner + side) // pieces, (2 * owner + side) % pieces
+            block = None
+            for e in range(4):
+                piece = sums[e // 2][e % 2][:, t * LANES : (t + 1) * LANES]
+                move = (e - i) * quarter % LANES
+                piece = pltpu.roll(piece, move, 1) if move else piece
+                block = piece if block is None else jnp.where(slot == e, piece, block)
+            block = block * weight
+            for q in range(side, lon_count, 2):
+                out_ref[owner * lon_count + q] = block
+
+
+def add_points(parts_ref, out_ref):
+    sides, owners = out_ref.shape[:2]
+    lon_count = parts_ref.shape[0] // owners
+    for c in range(sides):
+        for b in range(owners):
+            value = parts_ref[b * lon_count + c]
+            for q in range(c + sides, lon_count, sides):
+                value = value + parts_ref[b * lon_count + q]
+            out_ref[c, b] = value.astype(out_ref.dtype)
+
+
+def order_tables(blocks, total, orders_ref, right_ref, first_ref, rows_ref, turn_ref, basis_ref):
     owners, per_owner = orders_ref.shape
-    quarter = per_owner // lon_count
-    pieces = LANES // quarter
-    northern = owners * cycles
-    group = degrees // northern
-    wide = group * northern
+    share = per_owner // 2
     band, lon = lax.axis_index("band"), lax.axis_index("lon")
+    side = lon % 2
     lane = iota((1, LANES), 1)
-
-    mine = pltpu.roll(orders_ref[...], (LANES - quarter * lon) % LANES, 1)
-    slot = lane // quarter
-    shifted = [mine if i == 0 else pltpu.roll(mine, quarter * i, 1) for i in range(pieces)]
-    rows = []
-    for t in range(owners // pieces):
-        row = shifted[0][t * pieces : t * pieces + 1]
-        for i in range(1, pieces):
-            row = jnp.where(slot == i, shifted[i][t * pieces + i : t * pieces + i + 1], row)
-        rows.append(row)
-    orders = jnp.concatenate(rows, axis=1)
+    first_lanes = lane < share
+
+    mine = pltpu.roll(orders_ref[...], (LANES - share * side) % LANES, 1)
+    moved = pltpu.roll(mine, share, 1)
+    orders = jnp.concatenate(
+        [jnp.where(first_lanes, mine[b : b + 1], moved[b + 1 : b + 2]) for b in range(0, owners, 2)], axis=1
+    )
     width = orders.shape[1]
     for c, table in enumerate(turn((iota((LANES, width), 0) * orders) & (total - 1), total)):
         high, low = split(table)
         for k, value in enumerate((high, high, low)):
             right_ref[k * LANES : (k + 1) * LANES, c * width : (c + 1) * width] = value
-    for k in range(lon_count):
-        origin = (lon + lon_count - k) % lon_count
+    for k in range(2):
+        origin = lon if k == 0 else lon + 1 - 2 * side
         step = iota((blocks, width), 0) + origin * blocks
         for c, table in enumerate(turn((step * LANES * orders) & (total - 1), total)):
             first_ref[c, k * blocks : (k + 1) * blocks] = table
-    sub = iota((2 * cycles, LANES), 0) % cycles
-    weight = jnp.zeros((2 * cycles, LANES), jnp.float32)
-    for j in range(cycles):
-        weight = jnp.where(sub == j, weight_ref[cycle_ref[band * cycles + j]], weight)
-    column_ref[...] = weight * (1.0 / math.sqrt(total))
-
-    def cycle_lanes(repeat):
-        place = (lane // (repeat * cycles)) * cycles + lane % cycles
-        row = jnp.full((1, LANES), -1, jnp.int32)
-        for i in range(northern):
-            row = jnp.where(place == i, cycle_ref[i], row)
-        return row
-
-    parity_lane = (lane // cycles) % 2
-    found = iota((northern, LANES), 0) == cycle_lanes(2)
-    for p in range(2):
-        one = jnp.where(found & (parity_lane == p), 1.0, 0.0)
-        copies = jnp.concatenate([one] * (LANES // northern), axis=0)
-        pick_ref[p * LANES : (p + 1) * LANES] = copies.astype(jnp.bfloat16)
-
-    leaving = cycle_lanes(4).astype(jnp.float32)
-    cycle_rows = jnp.transpose(jnp.broadcast_to(leaving, (LANES, LANES))).astype(jnp.int32)
-    found = cycle_rows == iota((LANES, LANES), 1) % northern
-    part = (iota((LANES, LANES), 0) // cycles) % 4
-    for i in range(4):
-        put = jnp.where(found & (part == i), 1.0, 0.0)
-        put_ref[i] = jnp.concatenate([put] * (wide // LANES), axis=1).astype(jnp.bfloat16)
 
     own = orders_ref[pl.ds(band, 1), :].astype(jnp.float32)
     rows_ref[...] = jnp.transpose(jnp.broadcast_to(own, (LANES, per_owner))).astype(jnp.int32)
 
-    share = per_owner // 2
-    first_lanes = lane < share
+    quarter = per_owner // 4
+    slot = lane // quarter
+    arranged = orders_ref[...]
+    ahead, behind = pltpu.roll(arranged, LANES - quarter, 1), pltpu.roll(arranged, quarter, 1)
+    arranged = jnp.where(slot == 1, ahead, jnp.where(slot == 2, behind, arranged))
 
     def halves(x, y):
         return jnp.where(first_lanes, x, pltpu.roll(y, share, 1)), jnp.where(first_lanes, pltpu.roll(x, share, 1), y)
 
     scale = 1.0 / math.sqrt(total)
     for b in range(owners):
-        order = orders_ref[b : b + 1, :]
+        order = arranged[b : b + 1]
         factor = jnp.where(order == 0, scale, 2.0 * scale)
         step = iota((blocks, per_owner), 0) + lon * blocks
         cos_a, sin_a = turn((step * LANES * order) & (total - 1), total)
@@ -179,32 +159,71 @@
             basis_ref[half, 1, :, b * per_owner : (b + 1) * per_owner] = low
 
 
-def spectral(lon_count, owners, pick_ref, put_ref, rows_ref, folded_ref, legendre_ref, love_ref, out_ref, spread_ref, kept_ref):
-    per_owner = rows_ref.shape[0]
-    quarter = per_owner // lon_count
+def cycle_tables(owners, cycles, degrees, total, weight_ref, cycle_ref, column_ref, pick_ref, put_ref):
+    northern = owners * cycles
+    wide = degrees // northern * northern
+    band = lax.axis_index("band")
+    lane = iota((1, LANES), 1)
+    sub = iota((2 * cycles, LANES), 0) % cycles
+    weight = jnp.zeros((2 * cycles, LANES), jnp.float32)
+    for j in range(cycles):
+        weight = jnp.where(sub == j, weight_ref[cycle_ref[band * cycles + j]], weight)
+    column_ref[...] = weight * (1.0 / math.sqrt(total))
+
+    def cycle_lanes(repeat):
+        place = (lane // (repeat * cycles)) * cycles + lane % cycles
+        row = jnp.full((1, LANES), -1, jnp.int32)
+        for i in range(northern):
+            row = jnp.where(place == i, cycle_ref[i], row)
+        return row
+
+    parity_lane = (lane // cycles) % 2
+    found = iota((northern, LANES), 0) == cycle_lanes(2)
+    for p in range(2):
+        one = jnp.where(found & (parity_lane == p), 1.0, 0.0)
+        copies = jnp.concatenate([one] * (LANES // northern), axis=0)
+        pick_ref[p * LANES : (p + 1) * LANES] = copies.astype(jnp.bfloat16)
+
+    leaving = cycle_lanes(4).astype(jnp.float32)
+    cycle_rows = jnp.transpose(jnp.broadcast_to(leaving, (LANES, LANES))).astype(jnp.int32)
+    found = cycle_rows == iota((LANES, LANES), 1) % northern
+    part = (iota((LANES, LANES), 0) // cycles) % 4
+    for i in range(4):
+        put = jnp.where(found & (part == i), 1.0, 0.0)
+        put_ref[i] = jnp.concatenate([put] * (wide // LANES), axis=1).astype(jnp.bfloat16)
+
+
+def spectral_half(side, pick_ref, put_ref, rows_ref, folded_ref, legendre_ref, love_ref, spread_ref, kept_ref):
+    parts, owners, height = folded_ref.shape[:3]
+    quarter = rows_ref.shape[0] // 4
     degrees = legendre_ref.shape[1]
-    cycles = folded_ref.shape[1] // 2
-    northern = owners * cycles
+    northern = owners * height // 2
     group = degrees // northern
     wide = group * northern
     lon = lax.axis_index("lon")
-    share = per_owner // 2
-    pick = pick_ref[...]
 
     pad = jnp.zeros((LANES - 2 * northern, LANES), jnp.float32)
     turned = []
-    for q in range(lon_count):
-        pieces = [folded_ref[b * lon_count + q].astype(jnp.float32) for b in range(owners)]
+    for q in range(parts):
+        pieces = [folded_ref[q, b].astype(jnp.float32) for b in range(owners)]
         turned.append(jnp.transpose(jnp.concatenate(pieces + [pad], axis=0)))
-    spread_ref[...] = dot_nt(jnp.concatenate(turned, axis=0).astype(jnp.bfloat16), pick)
+    spread_ref[...] = dot_nt(jnp.concatenate(turned, axis=0).astype(jnp.bfloat16), pick_ref[...])
 
     degree = lon * degrees + iota((ROWS, degrees), 1)
     diagonal = iota((ROWS, wide), 0) == iota((ROWS, wide), 1) // northern
     love = [[love_ref[g, f : f + 1, :] for f in range(2)] for g in range(2)]
-    groups = per_owner // group
+    groups = parts * quarter // group
+
+    def place(n):
+        q, first = n * group // quarter, n * group % quarter
+        return q, first, (2 * q + side) * quarter + first
+
+    def table(n):
+        start = pl.multiple_of(place(n)[2] * northern, wide)
+        return legendre_ref[pl.ds(start, wide)]
 
     def analyse(n):
-        q, first = n * group // quarter, n * group % quarter
+        q, first, _ = place(n)
         left = []
         for f in range(2):
             for p in range(2):
@@ -212,11 +231,10 @@
                     at = q * LANES + (f * 2 + c) * quarter + first
                     piece = spread_ref[at : at + group, p * LANES : (p + 1) * LANES]
                     left.append(jnp.where(diagonal, jnp.concatenate([piece] * (wide // LANES), axis=1), 0.0))
-        left = jnp.concatenate(left, axis=0).astype(jnp.bfloat16)
-        return dot(left, legendre_ref[n * wide : (n + 1) * wide])
+        return dot(jnp.concatenate(left, axis=0).astype(jnp.bfloat16), table(n))
 
     def respond(n, analysed):
-        order = rows_ref[n * group : (n + 1) * group]
+        order = rows_ref[pl.ds(pl.multiple_of(place(n)[2], group), group)]
         gap = degree - jnp.concatenate([order] * (degrees // LANES), axis=1)
         valid = gap >= 0
         keep = [valid & ((gap & 1) == p) for p in range(2)]
@@ -228,15 +246,14 @@
                     hi = ((2 + p) * 2 + c) * group
                     value = love[g][0] * analysed[lo : lo + group] + love[g][1] * analysed[hi : hi + group]
                     mixed.append(jnp.where(keep[p], value, 0.0))
-        mixed = jnp.concatenate(mixed, axis=0).astype(jnp.bfloat16)
-        return dot_nt(mixed, legendre_ref[n * wide : (n + 1) * wide])
+        return dot_nt(jnp.concatenate(mixed, axis=0).astype(jnp.bfloat16), table(n))
 
     def keep_pair(n, halves):
         for g in range(2):
             for c in range(2):
                 lo, hi = (g * 4 + c) * group, (g * 4 + 2 + c) * group
                 rows = [(half[lo : lo + group], half[hi : hi + group]) for half in halves]
-                at = (n * group // share * 2 + c) * share + n * group % share
+                at = c * parts * quarter + n * group
                 for h in range(2):
                     both = [even + odd if h == 0 else even - odd for even, odd in rows]
                     both = [jnp.where(diagonal, value, 0.0) for value in both]
@@ -255,11 +272,28 @@
     for i in range(4):
         term = dot_nt(put_ref[i], kept_ref[i])
         total = term if total is None else total + term
-    total = total.astype(out_ref.dtype)
+    return total.astype(jnp.bfloat16)
+
+
+def own_spectral(pick_ref, put_ref, rows_ref, folded_ref, legendre_ref, love_ref, out_ref, spread_ref, kept_ref):
+    side = lax.axis_index("lon") % 2
+    out_ref[...] = spectral_half(
+        side, pick_ref, put_ref, rows_ref, folded_ref, legendre_ref, love_ref, spread_ref, kept_ref
+    )
+
+
+def spectral(pick_ref, put_ref, rows_ref, folded_ref, legendre_ref, love_ref, own_ref, out_ref, spread_ref, kept_ref):
+    side = lax.axis_index("lon") % 2
+    other = spectral_half(
+        1 - side, pick_ref, put_ref, rows_ref, folded_ref, legendre_ref, love_ref, spread_ref, kept_ref
+    )
+    owners = folded_ref.shape[1]
+    lon_count = out_ref.shape[0] // owners
+    height = out_ref.shape[1]
     for b in range(owners):
-        for q in range(lon_count):
-            lanes = slice(q % 2 * 2 * share, (q % 2 + 1) * 2 * share)
-            out_ref[b * lon_count + q] = total[b * 4 * cycles : (b + 1) * 4 * cycles, lanes]
+        for q in range(0, lon_count, 2):
+            out_ref[b * lon_count + q + side] = own_ref[b * height : (b + 1) * height]
+            out_ref[b * lon_count + q + 1 - side] = other[b * height : (b + 1) * height]
 
 
 def add_degrees(lon_count, values_ref, out_ref):
@@ -344,50 +378,66 @@
             name=getattr(body, "func", body).__name__,
         )
 
-    parts = [loads]
-    for k in range(1, lon_count):
-        parts.append(lax.ppermute(loads, "lon", [(i, (i + k) % lon_count) for i in range(lon_count)]))
-    count = lon_count * blocks
-    width = owners * per_owner // lon_count
-    right, first, column, pick, put, order_rows, turns, basis = kernel(
-        functools.partial(tables, lon_count, cycles, degrees, blocks, total),
+    partner = [(i, i ^ 1) for i in range(lon_count)]
+    parts = [loads, lax.ppermute(loads, "lon", partner)]
+    count = 2 * blocks
+    width = owners * per_owner // 2
+    right, first, order_rows, turns, basis = kernel(
+        functools.partial(order_tables, blocks, total),
         (
             jax.ShapeDtypeStruct((3 * LANES, 2 * width), jnp.bfloat16),
             jax.ShapeDtypeStruct((2, count, width), jnp.float32),
-            jax.ShapeDtypeStruct((2 * cycles, LANES), jnp.float32),
-            jax.ShapeDtypeStruct((2 * LANES, LANES), jnp.bfloat16),
-            jax.ShapeDtypeStruct((4, LANES, degrees), jnp.bfloat16),
             jax.ShapeDtypeStruct((per_owner, LANES), jnp.int32),
             jax.ShapeDtypeStruct((2, 2, owners, blocks, per_owner), jnp.float32),
             jax.ShapeDtypeStruct((2, 2, LANES, owners * per_owner), jnp.bfloat16),
         ),
-        [vmem, smem, smem],
+        [vmem],
         [],
         1 << 31,
-    )(table, cycle_weight, cycle_order)
-    folded = kernel(
+    )(table)
+    column, pick, put = kernel(
+        functools.partial(cycle_tables, owners, cycles, degrees, total),
+        (
+            jax.ShapeDtypeStruct((2 * cycles, LANES), jnp.float32),
+            jax.ShapeDtypeStruct((2 * LANES, LANES), jnp.bfloat16),
+            jax.ShapeDtypeStruct((4, LANES, degrees), jnp.bfloat16),
+        ),
+        [smem, smem],
+        [],
+        1 << 30,
+    )(cycle_weight, cycle_order)
+    sums = kernel(
         analyse_grid,
-        jax.ShapeDtypeStruct((devices, 2 * cycles, LANES), jnp.bfloat16),
-        [vmem] * (3 + lon_count),
+        jax.ShapeDtypeStruct((devices, 2 * cycles, LANES), jnp.float32),
+        [vmem] * (3 + len(parts)),
         [
             pltpu.VMEM((count * 4 * cycles, LANES), jnp.float32),
             pltpu.VMEM((count * 4 * cycles, 2 * width), jnp.float32),
         ],
         1 << 31,
     )(right, first, column, *parts)
-    arrived = lax.all_to_all(folded, everyone, split_axis=0, concat_axis=0, tiled=True)
+    arrived = lax.all_to_all(sums, everyone, split_axis=0, concat_axis=0, tiled=True)
+    folded = kernel(
+        add_points,
+        jax.ShapeDtypeStruct((2, owners, 2 * cycles, LANES), jnp.bfloat16),
+        [vmem],
+        [],
+        1 << 28,
+    )(arrived)
+    others = lax.ppermute(folded, "lon", partner)
 
     rows = jnp.transpose(legendre, (0, 2, 1)).reshape(per_owner * northern, degrees)
+    scratch = [
+        pltpu.VMEM((2 * LANES, 2 * LANES), jnp.float32),
+        pltpu.VMEM((4, per_owner, degrees), jnp.bfloat16),
+    ]
+    height = owners * 4 * cycles
+    mine = kernel(own_spectral, jax.ShapeDtypeStruct((height, per_owner), jnp.bfloat16), [vmem] * 6, scratch, 1 << 31)(
+        pick, put, order_rows, folded, rows, love
+    )
     values = kernel(
-        functools.partial(spectral, lon_count, owners),
-        jax.ShapeDtypeStruct((devices, 4 * cycles, per_owner), jnp.bfloat16),
-        [vmem] * 6,
-        [
-            pltpu.VMEM((lon_count * LANES, 2 * LANES), jnp.float32),
-            pltpu.VMEM((4, 2 * per_owner, degrees), jnp.bfloat16),
-        ],
-        1 << 32,
-    )(pick, put, order_rows, arrived, rows, love)
+        spectral, jax.ShapeDtypeStruct((devices, 4 * cycles, per_owner), jnp.bfloat16), [vmem] * 7, scratch, 1 << 31
+    )(pick, put, order_rows, others, rows, love, mine)
     returned = lax.all_to_all(values, everyone, split_axis=0, concat_axis=0, tiled=True)
 
     own = kernel(
@@ -397,7 +447,7 @@
         [],
         1 << 28,
     )(returned)
-    other = lax.ppermute(own, "lon", [(i, i ^ 1) for i in range(lon_count)])
+    other = lax.ppermute(own, "lon", partner)
     left = [pltpu.VMEM((2 * 4 * cycles * blocks, owners * per_owner), jnp.bfloat16)]
     grid = kernel(
         own_grid, jax.ShapeDtypeStruct((4 * cycles * blocks, LANES), jnp.float32), [vmem] * 3, left, 1 << 30

time: 35.5 us -> 34.8 us (0.980)
  starting transfers between devices: 4.74 us -> 1.05 us
  blocking collectives: 22 us -> 24.9 us
  Pallas kernels: 5.86 us -> 7.15 us
  local copies, waits for them, and re-layouts: 2.01 us -> 0.85 us
    ppermute x4 -> x3, starting transfers between devices: 4.74 us -> 1.05 us  [the longest x1 0.49 us: per_device_kernels(): parts = [loads, lax.ppermute(loads, 'lon', partner)]]
    all_to_all x1, blocking collectives: 12.1 us -> 15 us  [per_device_kernels(): lax.all_to_all(sums, everyone, split_axis=0, concat_axis=0, tiled=True)]
    pallas_call x2 -> x5, Pallas kernels: 3.61 us -> 4.85 us  [the longest x1 1.72 us: per_device_kernels(): kernel(functools.partial(order_tables, blocks, total), (jax.ShapeDtypeStr...]
    unnamed x12, local copies, waits for them, and re-layouts: 2.01 us -> 0.85 us
  transfers between devices with their start and end apart: 4 -> 3, of which waited for: 1 -> 1; matrix products, arithmetic and copies ran while one was open for 0% -> 0% of each run, Pallas kernels for 7% -> 12%
where the time goes in v5:
time: 34.8 us; the launch traced here: 34.5 us
  blocking collectives  24.9 us (72%)
  Pallas kernels  7.15 us (21%)
  starting transfers between devices  1.05 us (3%)
  local copies, waits for them, and re-layouts  0.85 us (2%)
  waiting for transfers between devices  0.54 us (2%)
    all_to_all x1, blocking collectives, per_device_kernels(): lax.all_to_all(sums, everyone, split_axis=0, concat_axis=0, tiled=True)  15 us
    all_to_all x1, blocking collectives, per_device_kernels(): lax.all_to_all(values, everyone, split_axis=0, concat_axis=0, tiled=True)  9.91 us
    pallas_call x1, Pallas kernels, per_device_kernels(): kernel(functools.partial(order_tables, blocks, total), (jax.ShapeDtypeStr...  1.72 us
    pallas_call x1, Pallas kernels, per_device_kernels(): kernel(spectral, jax.ShapeDtypeStruct((devices, 4 * cycles, per_owner), j...  1.23 us
    pallas_call x1, Pallas kernels, per_device_kernels(): kernel(own_spectral, jax.ShapeDtypeStruct((height, per_owner), jnp.bfloat...  1.22 us
    pallas_call x1, Pallas kernels, per_device_kernels(): kernel(synthesise_grid, jax.ShapeDtypeStruct(loads.shape, jnp.float32), [...  1.18 us
    unnamed x12, local copies, waits for them, and re-layouts  0.85 us
  transfers between devices with their start and end apart: 3, of which 1 were waited for; matrix products, arithmetic and copies ran while one was open for 0% of the time, Pallas kernels for 12%

profile of v5, /device:TPU:0, one launch (start us, length us, event | category | flops | bytes accessed | tf_op | source)
XLA Modules:
  0.0 34.5 jit_solution(8889162098106822970)
XLA Ops:
  0.0 0.5 %collective-permute-start = (f32[2,2,4,1024]{3,2,1,0:T(4,128)}, f32[2,2,4,1024]{3,2,1,0:T(4,128)S(1)}, u32[]{:S(2)}, u32[]{:S(2)}) collective-permute-start(f32[2,2,4,1024]{3,2,1,0:T(4,128)} %refs_0_.1), channel_id=1, source_target_pairs={{0,1},{1,0},{2,3},{3,2},{4,5},{5,4},{6,7},{7,6},{8,9},{9,8},{10,11... | collective-permute-start | bytes 196616 | tf_op jit(solution)/shard_map/ppermute | solution.py:382
  0.5 0.0 copy-start.2
  0.5 0.7 %copy-done.2 = s32[1024]{0:T(1024)S(1)} copy-done((s32[1024]{0:T(1024)S(1)}, s32[1024]{0:T(1024)}, u32[]{:S(2)}) %copy-start.2) | copy-done | bytes 4120
  1.2 0.0 copy-start.4
  1.2 0.0 copy-start.5
  1.2 1.7 %order_tables.1 = (bf16[384,1024]{1,0:T(8,128)(2,1)S(1)}, f32[2,16,512]{2,1,0:T(8,128)S(1)}, s32[128,128]{1,0:T(8,128)S(1)}, f32[2,2,8,8,128]{4,3,2,1,0:T(8,128)S(1)}, bf16[2,2,128,1024]{3,2,1,0:T(8,128)(2,1)S(1)}) custom-call(s32[8,128]{1,0:T(8,128)S(1)} %bitcast.6), custom_call_target="tpu_custom_call" | custom-call | flops 2147483648 | bytes 1048576 | tf_op jit(solution)/shard_map/order_tables/pallas_call | solution.py:385
  2.9 0.0 copy-done.4
  2.9 0.0 copy-done.5
  2.9 0.0 copy-start.1
  2.9 0.7 %cycle_tables.1 = (f32[8,128]{1,0:T(8,128)S(1)}, bf16[256,128]{1,0:T(8,128)(2,1)S(1)}, bf16[4,128,256]{2,1,0:T(8,128)(2,1)S(1)}) custom-call(f32[32]{0:T(128)S(1)} %copy-done.4, s32[32]{0:T(128)S(1)} %copy-done.5), custom_call_target="tpu_custom_call" | custom-call | flops 1073741824 | bytes 1048576 | tf_op jit(solution)/shard_map/cycle_tables/pallas_call | solution.py:398
  3.6 0.0 collective-permute-done.refs_1_
  3.6 0.1 copy-done.1
  3.8 0.0 copy-start
  3.8 0.0 copy-start.3
  3.8 0.6 %analyse_grid.1 = f32[32,8,128]{2,1,0:T(8,128)S(1)} custom-call(bf16[384,1024]{1,0:T(8,128)(2,1)S(1)} %get-tuple-element.18.right_ref, f32[2,16,512]{2,1,0:T(8,128)S(1)} %get-tuple-element.19.turn_ref, f32[8,128]{1,0:T(8,128)S(1)} %get-tuple-element.20.weight_ref, f32[2,2,4,1024]{3,2,1,0:T(4,128)S(1)} %copy-done.1, ...), custom_call_target="tpu_custom_call" | custom-call | flops 2147483648 | bytes 1048576 | tf_op jit(solution)/shard_map/analyse_grid/pallas_call | solution.py:409
  4.4 15.0 %all_to_all.10.parts_ref = f32[32,8,128]{2,1,0:T(8,128)S(1)} all-to-all(f32[32,8,128]{2,1,0:T(8,128)S(1)} %analyse_grid.1), channel_id=1, replica_groups=mesh['band'=8,'lon'=4] {'band','lon'}, dimensions={0} | all-to-all | bytes 262144 | tf_op jit(solution)/shard_map/all_to_all | solution.py:419
  19.4 0.3 collective-permute-start.1
  19.6 0.0 copy-done
  19.6 0.0 copy-done.3
  19.6 1.2 %own_spectral.1.own_ref = bf16[128,128]{1,0:T(8,128)(2,1)S(1)} custom-call(bf16[256,128]{1,0:T(8,128)(2,1)S(1)} %get-tuple-element.15.pick_ref, bf16[4,128,256]{2,1,0:T(8,128)(2,1)S(1)} %get-tuple-element.16.put_ref, s32[128,128]{1,0:T(8,128)S(1)} %get-tuple-element.17.rows_ref, bf16[2,8,8,128]{3,2,1,0:T(8,128)(2,1)S(1)} %add_points.1.folded_ref, ...), custom_call_target="tpu_custom_call" | custom-call | flops 2147483648 | bytes 1048576 | tf_op jit(solution)/shard_map/own_spectral/pallas_call | solution.py:435
  20.9 0.0 collective-permute-done.1.folded_ref
  20.9 1.2 %spectral.1 = bf16[32,16,128]{2,1,0:T(8,128)(2,1)S(1)} custom-call(bf16[256,128]{1,0:T(8,128)(2,1)S(1)} %get-tuple-element.15.pick_ref, bf16[4,128,256]{2,1,0:T(8,128)(2,1)S(1)} %get-tuple-element.16.put_ref, s32[128,128]{1,0:T(8,128)S(1)} %get-tuple-element.17.rows_ref, bf16[2,8,8,128]{3,2,1,0:T(8,128)(2,1)S(1)} %collective-permute-done.1.folded_ref, ...), custom_call_target="tpu_custom_call" | custom-call | flops 2147483648 | bytes 1048576 | tf_op jit(solution)/shard_map/spectral/pallas_call | solution.py:438
  22.1 9.9 %all_to_all.11.values_ref = bf16[32,16,128]{2,1,0:T(8,128)(2,1)S(1)} all-to-all(bf16[32,16,128]{2,1,0:T(8,128)(2,1)S(1)} %spectral.1), channel_id=1, replica_groups=mesh['band'=8,'lon'=4] {'band','lon'}, dimensions={0} | all-to-all | bytes 262144 | tf_op jit(solution)/shard_map/all_to_all | solution.py:441
  32.0 0.3 collective-permute-start.2
  32.3 0.5 %own_grid.1.grid_ref = f32[128,128]{1,0:T(8,128)S(1)} custom-call(f32[2,2,8,8,128]{4,3,2,1,0:T(8,128)S(1)} %get-tuple-element.13.turn_ref, bf16[2,2,128,1024]{3,2,1,0:T(8,128)(2,1)S(1)} %get-tuple-element.14.basis_ref, f32[8,16,128]{2,1,0:T(8,128)S(1)} %add_degrees.1.value_ref), custom_call_target="tpu_custom_call" | custom-call | flops 1073741824 | bytes 1048576 | tf_op jit(solution)/shard_map/own_grid/pallas_call | solution.py:452
  32.8 0.5 %collective-permute-done.2.value_ref = f32[8,16,128]{2,1,0:T(8,128)S(1)} collective-permute-done((f32[8,16,128]{2,1,0:T(8,128)S(1)}, f32[8,16,128]{2,1,0:T(8,128)S(1)}, u32[]{:S(2)}, u32[]{:S(2)}) %collective-permute-start.2) | collective-permute-done | bytes 65568 | tf_op jit(solution)/shard_map/ppermute | solution.py:450
  33.4 1.2 %synthesise_grid.1 = f32[2,2,4,1024]{3,2,1,0:T(4,128)} custom-call(f32[2,2,8,8,128]{4,3,2,1,0:T(8,128)S(1)} %get-tuple-element.13.turn_ref, bf16[2,2,128,1024]{3,2,1,0:T(8,128)(2,1)S(1)} %get-tuple-element.14.basis_ref, f32[8,16,128]{2,1,0:T(8,128)S(1)} %collective-permute-done.2.value_ref, f32[128,128]{1,0:T(8,128)S(1)} %own_grid.1.grid_ref), custom_call_target="tpu_custom_call" | custom-call | flops 1073741824 | bytes 1048576 | tf_op jit(solution)/shard_map/synthesise_grid/pallas_call | solution.py:455
  (2 shorter events, 0.0 us)
Async XLA Ops:
  0.0 3.6 %collective-permute-start = (f32[2,2,4,1024]{3,2,1,0:T(4,128)}, f32[2,2,4,1024]{3,2,1,0:T(4,128)S(1)}, u32[]{:S(2)}, u32[]{:S(2)}) collective-permute-start(f32[2,2,4,1024]{3,2,1,0:T(4,128)} %refs_0_.1), channel_id=1, source_target_pairs={{0,1},{1,0},{2,3},{3,2},{4,5},{5,4},{6,7},{7,6},{8,9},{9,8},{10,11... | collective-permute-start | bytes 196616 | tf_op jit(solution)/shard_map/ppermute | solution.py:382
  0.5 0.7 %copy-start.2 = (s32[1024]{0:T(1024)S(1)}, s32[1024]{0:T(1024)}, u32[]{:S(2)}) copy-start(s32[1024]{0:T(1024)} %param.10) | copy-start | bytes 12292
  1.2 1.7 %copy-start.4 = (f32[32]{0:T(128)S(1)}, f32[32]{0:T(128)}, u32[]{:S(2)}) copy-start(f32[32]{0:T(128)} %weight_ref.1) | copy-start | bytes 388
  1.2 1.7 %copy-start.5 = (s32[32]{0:T(128)S(1)}, s32[32]{0:T(128)}, u32[]{:S(2)}) copy-start(s32[32]{0:T(128)} %cycle_ref.1) | copy-start | bytes 388
  2.9 0.8 %copy-start.1 = (f32[2,2,4,1024]{3,2,1,0:T(4,128)S(1)}, f32[2,2,4,1024]{3,2,1,0:T(4,128)}, u32[]{:S(2)}) copy-start(f32[2,2,4,1024]{3,2,1,0:T(4,128)} %refs_0_.1) | copy-start | bytes 196612
  3.8 15.9 %copy-start = (bf16[128,256,32]{1,2,0:T(8,128)(2,1)S(1)}, bf16[128,256,32]{1,2,0:T(8,128)(2,1)}, u32[]{:S(2)}) copy-start(bf16[128,256,32]{1,2,0:T(8,128)(2,1)} %param.7) | copy-start | bytes 6291460
  3.8 15.9 %copy-start.3 = (f32[2,2,256]{2,1,0:T(2,128)S(1)}, f32[2,2,256]{2,1,0:T(2,128)}, u32[]{:S(2)}) copy-start(f32[2,2,256]{2,1,0:T(2,128)} %love_ref.3) | copy-start | bytes 12292
  19.4 1.5 %collective-permute-start.1 = (bf16[2,8,8,128]{3,2,1,0:T(8,128)(2,1)S(1)}, bf16[2,8,8,128]{3,2,1,0:T(8,128)(2,1)S(1)}, u32[]{:S(2)}, u32[]{:S(2)}) collective-permute-start(bf16[2,8,8,128]{3,2,1,0:T(8,128)(2,1)S(1)} %add_points.1.folded_ref), channel_id=1, source_target_pairs={{0,1},{1,0},{2,3},{3,2},{4,5},{5,4},{6,7},{7,6},{8,9},{9,8},{10,11... | collective-permute-start | bytes 98312 | tf_op jit(solution)/shard_map/ppermute | solution.py:427
  32.0 1.3 %collective-permute-start.2 = (f32[8,16,128]{2,1,0:T(8,128)S(1)}, f32[8,16,128]{2,1,0:T(8,128)S(1)}, u32[]{:S(2)}, u32[]{:S(2)}) collective-permute-start(f32[8,16,128]{2,1,0:T(8,128)S(1)} %add_degrees.1.value_ref), channel_id=1, source_target_pairs={{0,1},{1,0},{2,3},{3,2},{4,5},{5,4},{6,7},{7,6},{8,9},{9,8},{10,11... | collective-permute-start | bytes 196616 | tf_op jit(solution)/shard_map/ppermute | solution.py:450

commit v6 on v5

--- a/solution.py
+++ b/solution.py
@@ -47,7 +47,7 @@
     return lax.dot_general(a, b, NT, preferred_element_type=jnp.float32)
 
 
-def analyse_grid(right_ref, turn_ref, weight_ref, *refs):
+def analyse_grid(total, right_ref, turn_ref, weight_ref, cycle_ref, *refs):
     parts, out_ref, points_ref, mid_ref = refs[:-3], refs[-3], refs[-2], refs[-1]
     cycles = parts[0].shape[2]
     blocks = parts[0].shape[3] // LANES
@@ -79,7 +79,12 @@
             sums[f][1] = sums[f][1] - (sa * tc + ca * ts)
 
     slot = iota((1, LANES), 1) // quarter
-    weight = weight_ref[...]
+    northern = cycle_ref.shape[1]
+    lane = iota((step, northern), 1)
+    row = lax.axis_index("band") * cycles + iota((step, northern), 0) % cycles
+    listed = jnp.sum(jnp.where(lane == row, cycle_ref[...].astype(jnp.float32), 0.0), axis=1, keepdims=True)
+    weight = jnp.sum(jnp.where(lane == listed.astype(jnp.int32), weight_ref[...], 0.0), axis=1, keepdims=True)
+    weight = weight * (1.0 / math.sqrt(total))
     for owner in range(owners):
         for side in range(2):
             t, i = (2 * owner + side) // pieces, (2 * owner + side) % pieces
@@ -105,13 +110,18 @@
             out_ref[c, b] = value.astype(out_ref.dtype)
 
 
-def order_tables(blocks, total, orders_ref, right_ref, first_ref, rows_ref, turn_ref, basis_ref):
+def products(fine, coarse):
+    for k in range(coarse[0].shape[0]):
+        cc, cs = coarse[0][k : k + 1], coarse[1][k : k + 1]
+        yield fine[0] * cc - fine[1] * cs, fine[1] * cc + fine[0] * cs
+
+
+def forward_tables(blocks, total, orders_ref, right_ref, first_ref):
     owners, per_owner = orders_ref.shape
     share = per_owner // 2
-    band, lon = lax.axis_index("band"), lax.axis_index("lon")
+    lon = lax.axis_index("lon")
     side = lon % 2
-    lane = iota((1, LANES), 1)
-    first_lanes = lane < share
+    first_lanes = iota((1, LANES), 1) < share
 
     mine = pltpu.roll(orders_ref[...], (LANES - share * side) % LANES, 1)
     moved = pltpu.roll(mine, share, 1)
@@ -119,16 +129,55 @@
         [jnp.where(first_lanes, mine[b : b + 1], moved[b + 1 : b + 2]) for b in range(0, owners, 2)], axis=1
     )
     width = orders.shape[1]
-    for c, table in enumerate(turn((iota((LANES, width), 0) * orders) & (total - 1), total)):
-        high, low = split(table)
-        for k, value in enumerate((high, high, low)):
-            right_ref[k * LANES : (k + 1) * LANES, c * width : (c + 1) * width] = value
+    fine = turn(iota((ROWS, width), 0) * orders, total)
+    coarse = turn((iota((LANES // ROWS, width), 0) * ROWS * orders) & (total - 1), total)
+    kept = []
+    for k, pair in enumerate(products(fine, coarse)):
+        kept.append([split(table) for table in pair])
+        if k % 2 == 0:
+            continue
+        for c in range(2):
+            high, low = [jnp.concatenate([kept[k - 1][c][i], kept[k][c][i]], axis=0) for i in range(2)]
+            for i, value in enumerate((high, high, low)):
+                at = i * LANES + (k - 1) * ROWS
+                right_ref[at : at + 2 * ROWS, c * width : (c + 1) * width] = value
     for k in range(2):
         origin = lon if k == 0 else lon + 1 - 2 * side
         step = iota((blocks, width), 0) + origin * blocks
         for c, table in enumerate(turn((step * LANES * orders) & (total - 1), total)):
             first_ref[c, k * blocks : (k + 1) * blocks] = table
 
+
+def later_tables(cycles, blocks, total, orders_ref, cycle_ref, after_ref, pick_ref, put_ref, rows_ref, turn_ref, basis_ref):
+    del after_ref
+    owners, per_owner = orders_ref.shape
+    northern = owners * cycles
+    wide = put_ref.shape[2]
+    share = per_owner // 2
+    band, lon = lax.axis_index("band"), lax.axis_index("lon")
+    lane = iota((1, LANES), 1)
+    first_lanes = lane < share
+
+    listed = jnp.broadcast_to(cycle_ref[...].astype(jnp.float32), (LANES, northern)).astype(jnp.bfloat16)
+    index = iota((LANES, northern), 0)
+
+    def places(repeat):
+        place = index // (repeat * cycles) * cycles + index % cycles
+        return jnp.where(place == iota((LANES, northern), 1), 1.0, 0.0).astype(jnp.bfloat16)
+
+    arriving = dot_nt(listed[: 2 * ROWS], places(2))[:1].astype(jnp.int32)
+    found = (iota((northern, LANES), 0) == arriving) & (lane < 2 * northern)
+    for p in range(2):
+        one = jnp.where(found & (lane // cycles % 2 == p), 1.0, 0.0)
+        copies = jnp.concatenate([one] * (LANES // northern), axis=0)
+        pick_ref[p * LANES : (p + 1) * LANES] = copies.astype(jnp.bfloat16)
+    leaving = dot_nt(places(4), listed).astype(jnp.int32)
+    found = leaving == iota((LANES, LANES), 1) % northern
+    part = iota((LANES, LANES), 0) // cycles % 4
+    for i in range(4):
+        put = jnp.where(found & (part == i), 1.0, 0.0)
+        put_ref[i] = jnp.concatenate([put] * (wide // LANES), axis=1).astype(jnp.bfloat16)
+
     own = orders_ref[pl.ds(band, 1), :].astype(jnp.float32)
     rows_ref[...] = jnp.transpose(jnp.broadcast_to(own, (LANES, per_owner))).astype(jnp.int32)
 
@@ -137,86 +186,61 @@
     arranged = orders_ref[...]
     ahead, behind = pltpu.roll(arranged, LANES - quarter, 1), pltpu.roll(arranged, quarter, 1)
     arranged = jnp.where(slot == 1, ahead, jnp.where(slot == 2, behind, arranged))
-
-    def halves(x, y):
-        return jnp.where(first_lanes, x, pltpu.roll(y, share, 1)), jnp.where(first_lanes, pltpu.roll(x, share, 1), y)
+    swapped = pltpu.roll(arranged, share, 1)
+    doubled = [jnp.where(first_lanes, arranged, swapped), jnp.where(first_lanes, swapped, arranged)]
 
     scale = 1.0 / math.sqrt(total)
-    for b in range(owners):
-        order = arranged[b : b + 1]
-        factor = jnp.where(order == 0, scale, 2.0 * scale)
-        step = iota((blocks, per_owner), 0) + lon * blocks
-        cos_a, sin_a = turn((step * LANES * order) & (total - 1), total)
-        cos_a, sin_a = cos_a * factor, sin_a * factor
-        for half, table in enumerate(halves(cos_a, -cos_a)):
-            turn_ref[half, 0, b] = table
-        for half, table in enumerate(halves(-sin_a, -sin_a)):
-            turn_ref[half, 1, b] = table
-        cos_b, sin_b = turn((iota((LANES, per_owner), 0) * order) & (total - 1), total)
-        for half, table in enumerate(halves(cos_b, sin_b)):
-            high, low = split(table)
-            basis_ref[half, 0, :, b * per_owner : (b + 1) * per_owner] = high
-            basis_ref[half, 1, :, b * per_owner : (b + 1) * per_owner] = low
-
-
-def cycle_tables(owners, cycles, degrees, total, weight_ref, cycle_ref, column_ref, pick_ref, put_ref):
-    northern = owners * cycles
-    wide = degrees // northern * northern
-    band = lax.axis_index("band")
-    lane = iota((1, LANES), 1)
-    sub = iota((2 * cycles, LANES), 0) % cycles
-    weight = jnp.zeros((2 * cycles, LANES), jnp.float32)
-    for j in range(cycles):
-        weight = jnp.where(sub == j, weight_ref[cycle_ref[band * cycles + j]], weight)
-    column_ref[...] = weight * (1.0 / math.sqrt(total))
-
-    def cycle_lanes(repeat):
-        place = (lane // (repeat * cycles)) * cycles + lane % cycles
-        row = jnp.full((1, LANES), -1, jnp.int32)
-        for i in range(northern):
-            row = jnp.where(place == i, cycle_ref[i], row)
-        return row
-
-    parity_lane = (lane // cycles) % 2
-    found = iota((northern, LANES), 0) == cycle_lanes(2)
-    for p in range(2):
-        one = jnp.where(found & (parity_lane == p), 1.0, 0.0)
-        copies = jnp.concatenate([one] * (LANES // northern), axis=0)
-        pick_ref[p * LANES : (p + 1) * LANES] = copies.astype(jnp.bfloat16)
-
-    leaving = cycle_lanes(4).astype(jnp.float32)
-    cycle_rows = jnp.transpose(jnp.broadcast_to(leaving, (LANES, LANES))).astype(jnp.int32)
-    found = cycle_rows == iota((LANES, LANES), 1) % northern
-    part = (iota((LANES, LANES), 0) // cycles) % 4
-    for i in range(4):
-        put = jnp.where(found & (part == i), 1.0, 0.0)
-        put_ref[i] = jnp.concatenate([put] * (wide // LANES), axis=1).astype(jnp.bfloat16)
-
-
-def spectral_half(side, pick_ref, put_ref, rows_ref, folded_ref, legendre_ref, love_ref, spread_ref, kept_ref):
-    parts, owners, height = folded_ref.shape[:3]
-    quarter = rows_ref.shape[0] // 4
+    for half in range(2):
+        for b in range(owners):
+            order = doubled[half][b : b + 1]
+            factor = jnp.where(order == 0, scale, 2.0 * scale)
+            step = iota((blocks, per_owner), 0) + lon * blocks
+            cos_a, sin_a = turn((step * LANES * order) & (total - 1), total)
+            turn_ref[half, 0, b] = jnp.where(first_lanes, cos_a, -cos_a) * factor
+            turn_ref[half, 1, b] = -sin_a * factor
+            back = jnp.where(first_lanes, 0, total - total // 4)
+            fine = turn((iota((ROWS, per_owner), 0) * order + back) & (total - 1), total)
+            coarse = turn((iota((LANES // ROWS, per_owner), 0) * ROWS * order) & (total - 1), total)
+            kept = []
+            for k in range(LANES // ROWS):
+                value = fine[0] * coarse[0][k : k + 1] - fine[1] * coarse[1][k : k + 1]
+                kept.append(split(value))
+                if k % 2 == 1:
+                    for i in range(2):
+                        basis_ref[
+                            half, i, (k - 1) * ROWS : (k + 1) * ROWS, b * per_owner : (b + 1) * per_owner
+                        ] = jnp.concatenate([kept[k - 1][i], kept[k][i]], axis=0)
+
+
+def spectral(
+    pick_ref, put_ref, rows_ref, own_ref, other_ref, legendre_ref, love_ref, out_ref, spread_ref, kept_ref
+):
+    parts, owners, height = own_ref.shape[:3]
+    quarter = rows_ref.shape[0] // (2 * parts)
     degrees = legendre_ref.shape[1]
     northern = owners * height // 2
     group = degrees // northern
     wide = group * northern
     lon = lax.axis_index("lon")
+    side = lon % 2
 
     pad = jnp.zeros((LANES - 2 * northern, LANES), jnp.float32)
     turned = []
-    for q in range(parts):
-        pieces = [folded_ref[q, b].astype(jnp.float32) for b in range(owners)]
-        turned.append(jnp.transpose(jnp.concatenate(pieces + [pad], axis=0)))
+    for folded_ref in (own_ref, other_ref):
+        for q in range(parts):
+            pieces = [folded_ref[q, b].astype(jnp.float32) for b in range(owners)]
+            turned.append(jnp.transpose(jnp.concatenate(pieces + [pad], axis=0)))
     spread_ref[...] = dot_nt(jnp.concatenate(turned, axis=0).astype(jnp.bfloat16), pick_ref[...])
 
     degree = lon * degrees + iota((ROWS, degrees), 1)
     diagonal = iota((ROWS, wide), 0) == iota((ROWS, wide), 1) // northern
     love = [[love_ref[g, f : f + 1, :] for f in range(2)] for g in range(2)]
-    groups = parts * quarter // group
+    groups = 2 * parts * quarter // group
 
     def place(n):
         q, first = n * group // quarter, n * group % quarter
-        return q, first, (2 * q + side) * quarter + first
+        taken = side if q < parts else 1 - side
+        return q, first, (2 * (q % parts) + taken) * quarter + first
 
     def table(n):
         start = pl.multiple_of(place(n)[2] * northern, wide)
@@ -253,7 +277,8 @@
             for c in range(2):
                 lo, hi = (g * 4 + c) * group, (g * 4 + 2 + c) * group
                 rows = [(half[lo : lo + group], half[hi : hi + group]) for half in halves]
-                at = c * parts * quarter + n * group
+                share = parts * quarter
+                at = (n * group // share * 2 + c) * share + n * group % share
                 for h in range(2):
                     both = [even + odd if h == 0 else even - odd for even, odd in rows]
                     both = [jnp.where(diagonal, value, 0.0) for value in both]
@@ -272,28 +297,13 @@
     for i in range(4):
         term = dot_nt(put_ref[i], kept_ref[i])
         total = term if total is None else total + term
-    return total.astype(jnp.bfloat16)
-
-
-def own_spectral(pick_ref, put_ref, rows_ref, folded_ref, legendre_ref, love_ref, out_ref, spread_ref, kept_ref):
-    side = lax.axis_index("lon") % 2
-    out_ref[...] = spectral_half(
-        side, pick_ref, put_ref, rows_ref, folded_ref, legendre_ref, love_ref, spread_ref, kept_ref
-    )
-
-
-def spectral(pick_ref, put_ref, rows_ref, folded_ref, legendre_ref, love_ref, own_ref, out_ref, spread_ref, kept_ref):
-    side = lax.axis_index("lon") % 2
-    other = spectral_half(
-        1 - side, pick_ref, put_ref, rows_ref, folded_ref, legendre_ref, love_ref, spread_ref, kept_ref
-    )
-    owners = folded_ref.shape[1]
+    total = total.astype(out_ref.dtype)
     lon_count = out_ref.shape[0] // owners
-    height = out_ref.shape[1]
+    rows, lanes = out_ref.shape[1:]
     for b in range(owners):
         for q in range(0, lon_count, 2):
-            out_ref[b * lon_count + q + side] = own_ref[b * height : (b + 1) * height]
-            out_ref[b * lon_count + q + 1 - side] = other[b * height : (b + 1) * height]
+            out_ref[b * lon_count + q + side] = total[b * rows : (b + 1) * rows, :lanes]
+            out_ref[b * lon_count + q + 1 - side] = total[b * rows : (b + 1) * rows, lanes:]
 
 
 def add_degrees(lon_count, values_ref, out_ref):
@@ -363,8 +373,8 @@
     blocks = points // LANES
     everyone = ("band", "lon")
     vmem = pl.BlockSpec(memory_space=pltpu.VMEM)
-    smem = pl.BlockSpec(memory_space=pltpu.SMEM)
     table = order_list.reshape(owners, per_owner)
+    cycle_list = cycle_order.reshape(1, northern)
 
     def kernel(body, out_shape, in_specs, scratch_shapes, flops):
         return pl.pallas_call(
@@ -382,40 +392,26 @@
     parts = [loads, lax.ppermute(loads, "lon", partner)]
     count = 2 * blocks
     width = owners * per_owner // 2
-    right, first, order_rows, turns, basis = kernel(
-        functools.partial(order_tables, blocks, total),
+    right, first = kernel(
+        functools.partial(forward_tables, blocks, total),
         (
             jax.ShapeDtypeStruct((3 * LANES, 2 * width), jnp.bfloat16),
             jax.ShapeDtypeStruct((2, count, width), jnp.float32),
-            jax.ShapeDtypeStruct((per_owner, LANES), jnp.int32),
-            jax.ShapeDtypeStruct((2, 2, owners, blocks, per_owner), jnp.float32),
-            jax.ShapeDtypeStruct((2, 2, LANES, owners * per_owner), jnp.bfloat16),
         ),
         [vmem],
         [],
         1 << 31,
     )(table)
-    column, pick, put = kernel(
-        functools.partial(cycle_tables, owners, cycles, degrees, total),
-        (
-            jax.ShapeDtypeStruct((2 * cycles, LANES), jnp.float32),
-            jax.ShapeDtypeStruct((2 * LANES, LANES), jnp.bfloat16),
-            jax.ShapeDtypeStruct((4, LANES, degrees), jnp.bfloat16),
-        ),
-        [smem, smem],
-        [],
-        1 << 30,
-    )(cycle_weight, cycle_order)
     sums = kernel(
-        analyse_grid,
+        functools.partial(analyse_grid, total),
         jax.ShapeDtypeStruct((devices, 2 * cycles, LANES), jnp.float32),
-        [vmem] * (3 + len(parts)),
+        [vmem] * (4 + len(parts)),
         [
             pltpu.VMEM((count * 4 * cycles, LANES), jnp.float32),
             pltpu.VMEM((count * 4 * cycles, 2 * width), jnp.float32),
         ],
-        1 << 31,
-    )(right, first, column, *parts)
+        1 << 34,
+    )(right, first, cycle_weight.reshape(1, northern), cycle_list, *parts)
     arrived = lax.all_to_all(sums, everyone, split_axis=0, concat_axis=0, tiled=True)
     folded = kernel(
         add_points,
@@ -425,19 +421,31 @@
         1 << 28,
     )(arrived)
     others = lax.ppermute(folded, "lon", partner)
+    pick, put, order_rows, turns, basis = kernel(
+        functools.partial(later_tables, cycles, blocks, total),
+        (
+            jax.ShapeDtypeStruct((2 * LANES, LANES), jnp.bfloat16),
+            jax.ShapeDtypeStruct((4, LANES, degrees), jnp.bfloat16),
+            jax.ShapeDtypeStruct((per_owner, LANES), jnp.int32),
+            jax.ShapeDtypeStruct((2, 2, owners, blocks, per_owner), jnp.float32),
+            jax.ShapeDtypeStruct((2, 2, LANES, owners * per_owner), jnp.bfloat16),
+        ),
+        [vmem, vmem, vmem],
+        [],
+        1 << 26,
+    )(table, cycle_list, folded)
 
     rows = jnp.transpose(legendre, (0, 2, 1)).reshape(per_owner * northern, degrees)
-    scratch = [
-        pltpu.VMEM((2 * LANES, 2 * LANES), jnp.float32),
-        pltpu.VMEM((4, per_owner, degrees), jnp.bfloat16),
-    ]
-    height = owners * 4 * cycles
-    mine = kernel(own_spectral, jax.ShapeDtypeStruct((height, per_owner), jnp.bfloat16), [vmem] * 6, scratch, 1 << 31)(
-        pick, put, order_rows, folded, rows, love
-    )
     values = kernel(
-        spectral, jax.ShapeDtypeStruct((devices, 4 * cycles, per_owner), jnp.bfloat16), [vmem] * 7, scratch, 1 << 31
-    )(pick, put, order_rows, others, rows, love, mine)
+        spectral,
+        jax.ShapeDtypeStruct((devices, 4 * cycles, per_owner), jnp.bfloat16),
+        [vmem] * 7,
+        [
+            pltpu.VMEM((4 * LANES, 2 * LANES), jnp.float32),
+            pltpu.VMEM((4, 2 * per_owner, degrees), jnp.bfloat16),
+        ],
+        1 << 31,
+    )(pick, put, order_rows, folded, others, rows, love)
     returned = lax.all_to_all(values, everyone, split_axis=0, concat_axis=0, tiled=True)
 
     own = kernel(

time: 34.8 us -> 33.4 us (0.960)
  Pallas kernels: 7.15 us -> 5.48 us
    pallas_call x4 -> x3, Pallas kernels: 4.22 us -> 2.05 us  [the longest x1 0.97 us: per_device_kernels(): kernel(functools.partial(later_tables, cycles, blocks, total), (jax.Shape...]
    pallas_call x1, Pallas kernels: 1.23 us -> 1.73 us  [per_device_kernels(): kernel(spectral, jax.ShapeDtypeStruct((devices, 4 * cycles, per_owner), j...]
    unnamed x12 -> x14, local copies, waits for them, and re-layouts: 0.85 us -> 1.08 us
  transfers between devices with their start and end apart: 3 -> 3, of which waited for: 1 -> 1; matrix products, arithmetic and copies ran while one was open for 0% -> 0% of each run, Pallas kernels for 12% -> 6%
where the time goes in v6:
time: 33.4 us; the launch traced here: 33.2 us
  blocking collectives  24.9 us (75%)
  Pallas kernels  5.48 us (16%)
  local copies, waits for them, and re-layouts  1.08 us (3%)
  starting transfers between devices  1.05 us (3%)
  waiting for transfers between devices  0.55 us (2%)
    all_to_all x1, blocking collectives, per_device_kernels(): lax.all_to_all(sums, everyone, split_axis=0, concat_axis=0, tiled=True)  15 us
    all_to_all x1, blocking collectives, per_device_kernels(): lax.all_to_all(values, everyone, split_axis=0, concat_axis=0, tiled=True)  9.96 us
    pallas_call x1, Pallas kernels, per_device_kernels(): kernel(spectral, jax.ShapeDtypeStruct((devices, 4 * cycles, per_owner), j...  1.73 us
    pallas_call x1, Pallas kernels, per_device_kernels(): kernel(synthesise_grid, jax.ShapeDtypeStruct(loads.shape, jnp.float32), [...  1.18 us
    unnamed x14, local copies, waits for them, and re-layouts  1.08 us
    pallas_call x1, Pallas kernels, per_device_kernels(): kernel(functools.partial(later_tables, cycles, blocks, total), (jax.Shape...  0.97 us
  transfers between devices with their start and end apart: 3, of which 1 were waited for; matrix products, arithmetic and copies ran while one was open for 0% of the time, Pallas kernels for 6%

profile of v6, /device:TPU:0, one launch (start us, length us, event | category | flops | bytes accessed | tf_op | source)
XLA Modules:
  0.0 33.2 jit_solution(16209547051662570611)
XLA Ops:
  0.0 0.5 %collective-permute-start = (f32[2,2,4,1024]{3,2,1,0:T(4,128)}, f32[2,2,4,1024]{3,2,1,0:T(4,128)S(1)}, u32[]{:S(2)}, u32[]{:S(2)}) collective-permute-start(f32[2,2,4,1024]{3,2,1,0:T(4,128)} %refs_0_.1), channel_id=1, source_target_pairs={{0,1},{1,0},{2,3},{3,2},{4,5},{5,4},{6,7},{7,6},{8,9},{9,8},{10,11... | collective-permute-start | bytes 196616 | tf_op jit(solution)/shard_map/ppermute | solution.py:392
  0.5 0.0 copy-start.2
  0.5 0.7 %copy-done.2 = s32[1024]{0:T(1024)S(1)} copy-done((s32[1024]{0:T(1024)S(1)}, s32[1024]{0:T(1024)}, u32[]{:S(2)}) %copy-start.2) | copy-done | bytes 4120
  1.2 0.0 copy-start.1
  1.2 0.0 copy-start.5
  1.2 0.0 copy-start.6
  1.2 0.4 %forward_tables.1 = (bf16[384,1024]{1,0:T(8,128)(2,1)S(1)}, f32[2,16,512]{2,1,0:T(8,128)S(1)}) custom-call(s32[8,128]{1,0:T(8,128)S(1)} %bitcast.7), custom_call_target="tpu_custom_call" | custom-call | flops 2147483648 | bytes 1048576 | tf_op jit(solution)/shard_map/forward_tables/pallas_call | solution.py:395
  1.6 0.0 collective-permute-done.refs_1_
  1.6 0.4 %copy-done.1 = f32[2,2,4,1024]{3,2,1,0:T(4,128)S(1)} copy-done((f32[2,2,4,1024]{3,2,1,0:T(4,128)S(1)}, f32[2,2,4,1024]{3,2,1,0:T(4,128)}, u32[]{:S(2)}) %copy-start.1) | copy-done | bytes 65560
  2.0 0.0 copy-done.5
  2.0 0.0 copy-done.6
  2.0 0.0 copy-start.3
  2.0 0.0 copy-start
  2.0 0.0 copy-start.4
  2.0 0.6 %analyse_grid.1 = f32[32,8,128]{2,1,0:T(8,128)S(1)} custom-call(bf16[384,1024]{1,0:T(8,128)(2,1)S(1)} %get-tuple-element.12.right_ref, f32[2,16,512]{2,1,0:T(8,128)S(1)} %get-tuple-element.13.turn_ref, f32[1,32]{1,0:T(1,128)S(1)} %bitcast.9, s32[1,32]{1,0:T(1,128)S(1)} %bitcast.10, f32[2,2,4,1024]{3,2,1,0:T(4,128)S(1)} %copy-done.1, ...), custom_call_target="tpu_custom_call" | custom-call | flops 17179869184 | bytes 1048576 | tf_op jit(solution)/shard_map/analyse_grid/pallas_call | solution.py:405
  2.7 15.0 %all_to_all.10.parts_ref = f32[32,8,128]{2,1,0:T(8,128)S(1)} all-to-all(f32[32,8,128]{2,1,0:T(8,128)S(1)} %analyse_grid.1), channel_id=1, replica_groups=mesh['band'=8,'lon'=4] {'band','lon'}, dimensions={0} | all-to-all | bytes 262144 | tf_op jit(solution)/shard_map/all_to_all | solution.py:415
  17.7 0.3 collective-permute-start.1
  17.9 0.0 copy-done.3
  17.9 1.0 %later_tables.1 = (bf16[256,128]{1,0:T(8,128)(2,1)S(1)}, bf16[4,128,256]{2,1,0:T(8,128)(2,1)S(1)}, s32[128,128]{1,0:T(8,128)S(1)}, f32[2,2,8,8,128]{4,3,2,1,0:T(8,128)S(1)}, bf16[2,2,128,1024]{3,2,1,0:T(8,128)(2,1)S(1)}) custom-call(s32[8,128]{1,0:T(8,128)S(1)} %bitcast.8, s32[1,32]{1,0:T(1,128)S(1)} %bitcast.11, ...), custom_call_target="tpu_custom_call" | custom-call | flops 67108864 | bytes 1048576 | tf_op jit(solution)/shard_map/later_tables/pallas_call | solution.py:424
  18.9 0.0 collective-permute-done.1.other_ref
  18.9 0.0 copy-done
  18.9 0.0 copy-done.4
  18.9 1.7 %spectral.1 = bf16[32,16,128]{2,1,0:T(8,128)(2,1)S(1)} custom-call(bf16[256,128]{1,0:T(8,128)(2,1)S(1)} %get-tuple-element.16.pick_ref, bf16[4,128,256]{2,1,0:T(8,128)(2,1)S(1)} %get-tuple-element.17.put_ref, s32[128,128]{1,0:T(8,128)S(1)} %get-tuple-element.18.rows_ref, bf16[2,8,8,128]{3,2,1,0:T(8,128)(2,1)S(1)} %add_points.1.after_ref.own_ref, ...), custom_call_target="tpu_custom_call" | custom-call | flops 2147483648 | bytes 1048576 | tf_op jit(solution)/shard_map/spectral/pallas_call | solution.py:439
  20.7 10.0 %all_to_all.11.values_ref = bf16[32,16,128]{2,1,0:T(8,128)(2,1)S(1)} all-to-all(bf16[32,16,128]{2,1,0:T(8,128)(2,1)S(1)} %spectral.1), channel_id=1, replica_groups=mesh['band'=8,'lon'=4] {'band','lon'}, dimensions={0} | all-to-all | bytes 262144 | tf_op jit(solution)/shard_map/all_to_all | solution.py:449
  30.7 0.3 collective-permute-start.2
  30.9 0.5 %own_grid.1.grid_ref = f32[128,128]{1,0:T(8,128)S(1)} custom-call(f32[2,2,8,8,128]{4,3,2,1,0:T(8,128)S(1)} %get-tuple-element.14.turn_ref, bf16[2,2,128,1024]{3,2,1,0:T(8,128)(2,1)S(1)} %get-tuple-element.15.basis_ref, f32[8,16,128]{2,1,0:T(8,128)S(1)} %add_degrees.1.value_ref), custom_call_target="tpu_custom_call" | custom-call | flops 1073741824 | bytes 1048576 | tf_op jit(solution)/shard_map/own_grid/pallas_call | solution.py:460
  31.4 0.5 %collective-permute-done.2.value_ref = f32[8,16,128]{2,1,0:T(8,128)S(1)} collective-permute-done((f32[8,16,128]{2,1,0:T(8,128)S(1)}, f32[8,16,128]{2,1,0:T(8,128)S(1)}, u32[]{:S(2)}, u32[]{:S(2)}) %collective-permute-start.2) | collective-permute-done | bytes 65568 | tf_op jit(solution)/shard_map/ppermute | solution.py:458
  32.0 1.2 %synthesise_grid.1 = f32[2,2,4,1024]{3,2,1,0:T(4,128)} custom-call(f32[2,2,8,8,128]{4,3,2,1,0:T(8,128)S(1)} %get-tuple-element.14.turn_ref, bf16[2,2,128,1024]{3,2,1,0:T(8,128)(2,1)S(1)} %get-tuple-element.15.basis_ref, f32[8,16,128]{2,1,0:T(8,128)S(1)} %collective-permute-done.2.value_ref, f32[128,128]{1,0:T(8,128)S(1)} %own_grid.1.grid_ref), custom_call_target="tpu_custom_call" | custom-call | flops 1073741824 | bytes 1048576 | tf_op jit(solution)/shard_map/synthesise_grid/pallas_call | solution.py:463
  (2 shorter events, 0.0 us)
Async XLA Ops:
  0.0 1.6 %collective-permute-start = (f32[2,2,4,1024]{3,2,1,0:T(4,128)}, f32[2,2,4,1024]{3,2,1,0:T(4,128)S(1)}, u32[]{:S(2)}, u32[]{:S(2)}) collective-permute-start(f32[2,2,4,1024]{3,2,1,0:T(4,128)} %refs_0_.1), channel_id=1, source_target_pairs={{0,1},{1,0},{2,3},{3,2},{4,5},{5,4},{6,7},{7,6},{8,9},{9,8},{10,11... | collective-permute-start | bytes 196616 | tf_op jit(solution)/shard_map/ppermute | solution.py:392
  0.5 0.7 %copy-start.2 = (s32[1024]{0:T(1024)S(1)}, s32[1024]{0:T(1024)}, u32[]{:S(2)}) copy-start(s32[1024]{0:T(1024)} %param.10) | copy-start | bytes 12292
  1.2 0.8 %copy-start.1 = (f32[2,2,4,1024]{3,2,1,0:T(4,128)S(1)}, f32[2,2,4,1024]{3,2,1,0:T(4,128)}, u32[]{:S(2)}) copy-start(f32[2,2,4,1024]{3,2,1,0:T(4,128)} %refs_0_.1) | copy-start | bytes 196612
  1.2 0.8 %copy-start.5 = (f32[32]{0:T(128)S(1)}, f32[32]{0:T(128)}, u32[]{:S(2)}) copy-start(f32[32]{0:T(128)} %param.9) | copy-start | bytes 388
  1.2 0.8 %copy-start.6 = (s32[32]{0:T(128)S(1)}, s32[32]{0:T(128)}, u32[]{:S(2)}) copy-start(s32[32]{0:T(128)} %param.11) | copy-start | bytes 388
  2.0 15.9 %copy-start.3 = (s32[1024]{0:T(1024)S(1)}, s32[1024]{0:T(1024)}, u32[]{:S(2)}) copy-start(s32[1024]{0:T(1024)} %param.10) | copy-start | bytes 12292
  2.0 16.9 %copy-start = (bf16[128,256,32]{1,2,0:T(8,128)(2,1)S(1)}, bf16[128,256,32]{1,2,0:T(8,128)(2,1)}, u32[]{:S(2)}) copy-start(bf16[128,256,32]{1,2,0:T(8,128)(2,1)} %param.7) | copy-start | bytes 6291460
  2.0 16.9 %copy-start.4 = (f32[2,2,256]{2,1,0:T(2,128)S(1)}, f32[2,2,256]{2,1,0:T(2,128)}, u32[]{:S(2)}) copy-start(f32[2,2,256]{2,1,0:T(2,128)} %love_ref.1) | copy-start | bytes 12292
  17.7 1.3 %collective-permute-start.1 = (bf16[2,8,8,128]{3,2,1,0:T(8,128)(2,1)S(1)}, bf16[2,8,8,128]{3,2,1,0:T(8,128)(2,1)S(1)}, u32[]{:S(2)}, u32[]{:S(2)}) collective-permute-start(bf16[2,8,8,128]{3,2,1,0:T(8,128)(2,1)S(1)} %add_points.1.after_ref.own_ref), channel_id=1, source_target_pairs={{0,1},{1,0},{2,3},{3,2},{4,5},{5,4},{6,7},{7,6},{8,9},{9,8},{10,11... | collective-permute-start | bytes 98312 | tf_op jit(solution)/shard_map/ppermute | solution.py:423
  30.7 1.3 %collective-permute-start.2 = (f32[8,16,128]{2,1,0:T(8,128)S(1)}, f32[8,16,128]{2,1,0:T(8,128)S(1)}, u32[]{:S(2)}, u32[]{:S(2)}) collective-permute-start(f32[8,16,128]{2,1,0:T(8,128)S(1)} %add_degrees.1.value_ref), channel_id=1, source_target_pairs={{0,1},{1,0},{2,3},{3,2},{4,5},{5,4},{6,7},{7,6},{8,9},{9,8},{10,11... | collective-permute-start | bytes 196616 | tf_op jit(solution)/shard_map/ppermute | solution.py:458

commit v7 on v6

--- a/solution.py
+++ b/solution.py
@@ -47,7 +47,8 @@
     return lax.dot_general(a, b, NT, preferred_element_type=jnp.float32)
 
 
-def analyse_grid(total, right_ref, turn_ref, weight_ref, cycle_ref, *refs):
+def analyse_grid(total, after_ref, right_ref, turn_ref, weight_ref, cycle_ref, *refs):
+    del after_ref
     parts, out_ref, points_ref, mid_ref = refs[:-3], refs[-3], refs[-2], refs[-1]
     cycles = parts[0].shape[2]
     blocks = parts[0].shape[3] // LANES
@@ -116,7 +117,12 @@
         yield fine[0] * cc - fine[1] * cs, fine[1] * cc + fine[0] * cs
 
 
-def forward_tables(blocks, total, orders_ref, right_ref, first_ref):
+def opening(out_ref):
+    out_ref[...] = jnp.zeros_like(out_ref)
+
+
+def forward_tables(blocks, total, orders_ref, after_ref, right_ref, first_ref):
+    del after_ref
     owners, per_owner = orders_ref.shape
     share = per_owner // 2
     lon = lax.axis_index("lon")
@@ -148,15 +154,11 @@
             first_ref[c, k * blocks : (k + 1) * blocks] = table
 
 
-def later_tables(cycles, blocks, total, orders_ref, cycle_ref, after_ref, pick_ref, put_ref, rows_ref, turn_ref, basis_ref):
+def cycle_tables(owners, cycles, after_ref, cycle_ref, pick_ref, put_ref):
     del after_ref
-    owners, per_owner = orders_ref.shape
     northern = owners * cycles
     wide = put_ref.shape[2]
-    share = per_owner // 2
-    band, lon = lax.axis_index("band"), lax.axis_index("lon")
     lane = iota((1, LANES), 1)
-    first_lanes = lane < share
 
     listed = jnp.broadcast_to(cycle_ref[...].astype(jnp.float32), (LANES, northern)).astype(jnp.bfloat16)
     index = iota((LANES, northern), 0)
@@ -178,38 +180,57 @@
         put = jnp.where(found & (part == i), 1.0, 0.0)
         put_ref[i] = jnp.concatenate([put] * (wide // LANES), axis=1).astype(jnp.bfloat16)
 
-    own = orders_ref[pl.ds(band, 1), :].astype(jnp.float32)
+
+def half_tables(which, total, orders_ref, turn_ref, basis_ref):
+    owners, per_owner = orders_ref.shape
+    blocks = turn_ref.shape[2]
+    share, quarter = per_owner // 2, per_owner // 4
+    lon = lax.axis_index("lon")
+    lane = iota((1, LANES), 1)
+    first_lanes = lane < share
+    slot = lane // quarter
+
+    orders = orders_ref[...]
+    moved = [orders] + [pltpu.roll(orders, quarter * i, 1) for i in range(1, 4)]
+    even = [moved[0], moved[3], moved[2], moved[1]]
+    odd = [moved[3], moved[2], moved[1], moved[0]]
+    doubled = jnp.zeros_like(orders)
+    for i in range(4):
+        doubled = jnp.where(slot == i, jnp.where(which == 0, even[i], odd[i]), doubled)
+
+    scale = 1.0 / math.sqrt(total)
+    back = jnp.where(first_lanes, 0, total - total // 4)
+    for b in range(owners):
+        order = doubled[b : b + 1]
+        factor = jnp.where(order == 0, scale, 2.0 * scale)
+        step = iota((blocks, per_owner), 0) + lon * blocks
+        cos_a, sin_a = turn((step * LANES * order) & (total - 1), total)
+        turn_ref[0, b] = jnp.where(first_lanes, cos_a, -cos_a) * factor
+        turn_ref[1, b] = -sin_a * factor
+        fine = turn((iota((ROWS, per_owner), 0) * order + back) & (total - 1), total)
+        coarse = turn((iota((LANES // ROWS, per_owner), 0) * ROWS * order) & (total - 1), total)
+        kept = []
+        for k in range(LANES // ROWS):
+            value = fine[0] * coarse[0][k : k + 1] - fine[1] * coarse[1][k : k + 1]
+            kept.append(split(value))
+            if k % 2 == 1:
+                rows = slice((k - 1) * ROWS, (k + 1) * ROWS)
+                for i in range(2):
+                    both = jnp.concatenate([kept[k - 1][i], kept[k][i]], axis=0)
+                    basis_ref[i, rows, b * per_owner : (b + 1) * per_owner] = both
+
+
+def own_tables(total, orders_ref, after_ref, rows_ref, turn_ref, basis_ref):
+    del after_ref
+    per_owner = orders_ref.shape[1]
+    own = orders_ref[pl.ds(lax.axis_index("band"), 1), :].astype(jnp.float32)
     rows_ref[...] = jnp.transpose(jnp.broadcast_to(own, (LANES, per_owner))).astype(jnp.int32)
-
-    quarter = per_owner // 4
-    slot = lane // quarter
-    arranged = orders_ref[...]
-    ahead, behind = pltpu.roll(arranged, LANES - quarter, 1), pltpu.roll(arranged, quarter, 1)
-    arranged = jnp.where(slot == 1, ahead, jnp.where(slot == 2, behind, arranged))
-    swapped = pltpu.roll(arranged, share, 1)
-    doubled = [jnp.where(first_lanes, arranged, swapped), jnp.where(first_lanes, swapped, arranged)]
-
-    scale = 1.0 / math.sqrt(total)
-    for half in range(2):
-        for b in range(owners):
-            order = doubled[half][b : b + 1]
-            factor = jnp.where(order == 0, scale, 2.0 * scale)
-            step = iota((blocks, per_owner), 0) + lon * blocks
-            cos_a, sin_a = turn((step * LANES * order) & (total - 1), total)
-            turn_ref[half, 0, b] = jnp.where(first_lanes, cos_a, -cos_a) * factor
-            turn_ref[half, 1, b] = -sin_a * factor
-            back = jnp.where(first_lanes, 0, total - total // 4)
-            fine = turn((iota((ROWS, per_owner), 0) * order + back) & (total - 1), total)
-            coarse = turn((iota((LANES // ROWS, per_owner), 0) * ROWS * order) & (total - 1), total)
-            kept = []
-            for k in range(LANES // ROWS):
-                value = fine[0] * coarse[0][k : k + 1] - fine[1] * coarse[1][k : k + 1]
-                kept.append(split(value))
-                if k % 2 == 1:
-                    for i in range(2):
-                        basis_ref[
-                            half, i, (k - 1) * ROWS : (k + 1) * ROWS, b * per_owner : (b + 1) * per_owner
-                        ] = jnp.concatenate([kept[k - 1][i], kept[k][i]], axis=0)
+    half_tables(lax.axis_index("lon") % 2, total, orders_ref, turn_ref, basis_ref)
+
+
+def other_tables(total, orders_ref, after_ref, turn_ref, basis_ref):
+    del after_ref
+    half_tables(1 - lax.axis_index("lon") % 2, total, orders_ref, turn_ref, basis_ref)
 
 
 def spectral(
@@ -314,30 +335,30 @@
         out_ref[b] = value
 
 
-def half_grid(which, turn_ref, basis_ref, value_ref, left_ref):
+def half_grid(turn_ref, basis_ref, value_ref, left_ref):
     owners, rows, lanes = value_ref.shape
-    blocks = turn_ref.shape[3]
+    blocks = turn_ref.shape[2]
     height = blocks * rows
     for b in range(owners):
         value = value_ref[b]
         other = pltpu.roll(value, lanes // 2, 1)
         for a in range(blocks):
-            term = value * turn_ref[which, 0, b, a : a + 1] + other * turn_ref[which, 1, b, a : a + 1]
+            term = value * turn_ref[0, b, a : a + 1] + other * turn_ref[1, b, a : a + 1]
             high, low = split(term)
             left_ref[a * rows : (a + 1) * rows, b * lanes : (b + 1) * lanes] = high
             left_ref[height + a * rows : height + (a + 1) * rows, b * lanes : (b + 1) * lanes] = low
-    grid = dot_nt(left_ref[...], basis_ref[which, 0])
-    return grid[:height] + grid[height:] + dot_nt(left_ref[:height], basis_ref[which, 1])
+    grid = dot_nt(left_ref[...], basis_ref[0])
+    return grid[:height] + grid[height:] + dot_nt(left_ref[:height], basis_ref[1])
 
 
 def own_grid(turn_ref, basis_ref, value_ref, out_ref, left_ref):
-    out_ref[...] = half_grid(lax.axis_index("lon") % 2, turn_ref, basis_ref, value_ref, left_ref)
+    out_ref[...] = half_grid(turn_ref, basis_ref, value_ref, left_ref)
 
 
 def synthesise_grid(turn_ref, basis_ref, value_ref, grid_ref, out_ref, left_ref):
     rows = value_ref.shape[1]
     cycles = out_ref.shape[2]
-    grid = grid_ref[...] + half_grid(1 - lax.axis_index("lon") % 2, turn_ref, basis_ref, value_ref, left_ref)
+    grid = grid_ref[...] + half_grid(turn_ref, basis_ref, value_ref, left_ref)
     for a in range(grid.shape[0] // rows):
         for g in range(2):
             for h in range(2):
@@ -392,26 +413,37 @@
     parts = [loads, lax.ppermute(loads, "lon", partner)]
     count = 2 * blocks
     width = owners * per_owner // 2
+    opened = kernel(opening, jax.ShapeDtypeStruct((ROWS, LANES), jnp.float32), [], [], 1 << 34)()
     right, first = kernel(
         functools.partial(forward_tables, blocks, total),
         (
             jax.ShapeDtypeStruct((3 * LANES, 2 * width), jnp.bfloat16),
             jax.ShapeDtypeStruct((2, count, width), jnp.float32),
         ),
-        [vmem],
+        [vmem, vmem],
         [],
         1 << 31,
-    )(table)
+    )(table, opened)
+    pick, put = kernel(
+        functools.partial(cycle_tables, owners, cycles),
+        (
+            jax.ShapeDtypeStruct((2 * LANES, LANES), jnp.bfloat16),
+            jax.ShapeDtypeStruct((4, LANES, degrees), jnp.bfloat16),
+        ),
+        [vmem, vmem],
+        [],
+        1 << 28,
+    )(first, cycle_list)
     sums = kernel(
         functools.partial(analyse_grid, total),
         jax.ShapeDtypeStruct((devices, 2 * cycles, LANES), jnp.float32),
-        [vmem] * (4 + len(parts)),
+        [vmem] * (5 + len(parts)),
         [
             pltpu.VMEM((count * 4 * cycles, LANES), jnp.float32),
             pltpu.VMEM((count * 4 * cycles, 2 * width), jnp.float32),
         ],
         1 << 34,
-    )(right, first, cycle_weight.reshape(1, northern), cycle_list, *parts)
+    )(pick, right, first, cycle_weight.reshape(1, northern), cycle_list, *parts)
     arrived = lax.all_to_all(sums, everyone, split_axis=0, concat_axis=0, tiled=True)
     folded = kernel(
         add_points,
@@ -421,19 +453,17 @@
         1 << 28,
     )(arrived)
     others = lax.ppermute(folded, "lon", partner)
-    pick, put, order_rows, turns, basis = kernel(
-        functools.partial(later_tables, cycles, blocks, total),
-        (
-            jax.ShapeDtypeStruct((2 * LANES, LANES), jnp.bfloat16),
-            jax.ShapeDtypeStruct((4, LANES, degrees), jnp.bfloat16),
-            jax.ShapeDtypeStruct((per_owner, LANES), jnp.int32),
-            jax.ShapeDtypeStruct((2, 2, owners, blocks, per_owner), jnp.float32),
-            jax.ShapeDtypeStruct((2, 2, LANES, owners * per_owner), jnp.bfloat16),
-        ),
-        [vmem, vmem, vmem],
+    halves = (
+        jax.ShapeDtypeStruct((2, owners, blocks, per_owner), jnp.float32),
+        jax.ShapeDtypeStruct((2, LANES, owners * per_owner), jnp.bfloat16),
+    )
+    order_rows, own_turns, own_basis = kernel(
+        functools.partial(own_tables, total),
+        (jax.ShapeDtypeStruct((per_owner, LANES), jnp.int32), *halves),
+        [vmem, vmem],
         [],
         1 << 26,
-    )(table, cycle_list, folded)
+    )(table, folded)
 
     rows = jnp.transpose(legendre, (0, 2, 1)).reshape(per_owner * northern, degrees)
     values = kernel(
@@ -457,11 +487,12 @@
     )(returned)
     other = lax.ppermute(own, "lon", partner)
     left = [pltpu.VMEM((2 * 4 * cycles * blocks, owners * per_owner), jnp.bfloat16)]
+    other_turns, other_basis = kernel(functools.partial(other_tables, total), halves, [vmem] * 2, [], 1 << 20)(table, own)
     grid = kernel(
-        own_grid, jax.ShapeDtypeStruct((4 * cycles * blocks, LANES), jnp.float32), [vmem] * 3, left, 1 << 30
-    )(turns, basis, own)
+        own_grid, jax.ShapeDtypeStruct((4 * cycles * blocks, LANES), jnp.float32), [vmem] * 3, left, 1 << 20
+    )(own_turns, own_basis, own)
     return kernel(synthesise_grid, jax.ShapeDtypeStruct(loads.shape, jnp.float32), [vmem] * 4, left, 1 << 30)(
-        turns, basis, other, grid
+        other_turns, other_basis, other, grid
     )
 
 

time: 33.4 us -> 33.3 us (level)
  local copies, waits for them, and re-layouts: 1.08 us -> 0.41 us
  blocking collectives: 24.9 us -> 25.3 us
    unnamed x14 -> x12, local copies, waits for them, and re-layouts: 1.08 us -> 0.41 us
    ppermute x1, waiting for transfers between devices: 0.01 us -> 0.51 us  [per_device_kernels(): others = lax.ppermute(folded, 'lon', partner)]
    ppermute x1, waiting for transfers between devices: 0.54 us -> 0.06 us  [per_device_kernels(): other = lax.ppermute(own, 'lon', partner)]
    pallas_call x1 -> x4, Pallas kernels: 0.97 us -> 1.13 us  [the longest x1 0.48 us: per_device_kernels(): kernel(functools.partial(own_tables, total), (jax.ShapeDtypeStruct((per_o...]
  transfers between devices with their start and end apart: 3 -> 3, of which waited for: 1 -> 3; matrix products, arithmetic and copies ran while one was open for 0% -> 0% of each run, Pallas kernels for 6% -> 6%
where the time goes in v7:
time: 33.3 us; the launch traced here: 33.1 us
  blocking collectives  25.3 us (76%)
  Pallas kernels  5.67 us (17%)
  starting transfers between devices  1.05 us (3%)
  waiting for transfers between devices  0.65 us (2%)
  local copies, waits for them, and re-layouts  0.41 us (1%)
    all_to_all x1, blocking collectives, per_device_kernels(): lax.all_to_all(sums, everyone, split_axis=0, concat_axis=0, tiled=True)  15.3 us
    all_to_all x1, blocking collectives, per_device_kernels(): lax.all_to_all(values, everyone, split_axis=0, concat_axis=0, tiled=True)  9.97 us
    pallas_call x1, Pallas kernels, per_device_kernels(): kernel(spectral, jax.ShapeDtypeStruct((devices, 4 * cycles, per_owner), j...  1.73 us
    pallas_call x1, Pallas kernels, per_device_kernels(): kernel(synthesise_grid, jax.ShapeDtypeStruct(loads.shape, jnp.float32), [...  1.2 us
  transfers between devices with their start and end apart: 3, of which 3 were waited for; matrix products, arithmetic and copies ran while one was open for 0% of the time, Pallas kernels for 6%

profile of v7, /device:TPU:0, one launch (start us, length us, event | category | flops | bytes accessed | tf_op | source)
XLA Modules:
  0.0 33.1 jit_solution(3123873815545411359)
XLA Ops:
  0.0 0.0 copy-start
  0.0 0.5 %collective-permute-start = (f32[2,2,4,1024]{3,2,1,0:T(4,128)}, f32[2,2,4,1024]{3,2,1,0:T(4,128)S(1)}, u32[]{:S(2)}, u32[]{:S(2)}) collective-permute-start(f32[2,2,4,1024]{3,2,1,0:T(4,128)} %refs_0_.1), channel_id=1, source_target_pairs={{0,1},{1,0},{2,3},{3,2},{4,5},{5,4},{6,7},{7,6},{8,9},{9,8},{10,11... | collective-permute-start | bytes 196616 | tf_op jit(solution)/shard_map/ppermute | solution.py:413
  0.5 0.2 copy-done
  0.7 0.0 copy-start.4
  0.7 0.0 copy-start.2
  0.7 0.0 copy-start.5
  0.7 0.4 %forward_tables.1 = (bf16[384,1024]{1,0:T(8,128)(2,1)S(1)}, f32[2,16,512]{2,1,0:T(8,128)S(1)}) custom-call(s32[8,128]{1,0:T(8,128)S(1)} %bitcast.6, f32[8,128]{1,0:T(8,128)S(1)} %opening.1.after_ref), custom_call_target="tpu_custom_call" | custom-call | flops 2147483648 | bytes 1048576 | tf_op jit(solution)/shard_map/forward_tables/pallas_call | solution.py:417
  1.1 0.2 copy-done.4
  1.3 0.2 cycle_tables.1
  1.5 0.1 collective-permute-done.refs_1_
  1.6 0.0 copy-done.2
  1.6 0.0 copy-done.5
  1.6 0.0 copy-start.1
  1.6 0.0 copy-start.3
  1.6 0.6 %analyse_grid.1 = f32[32,8,128]{2,1,0:T(8,128)S(1)} custom-call(bf16[256,128]{1,0:T(8,128)(2,1)S(1)} %get-tuple-element.15.after_ref.pick_ref, bf16[384,1024]{1,0:T(8,128)(2,1)S(1)} %get-tuple-element.17.right_ref, f32[2,16,512]{2,1,0:T(8,128)S(1)} %get-tuple-element.14.after_ref.turn_ref, f32[1,32]{1,0:T(1,128)S(1)} %bitcast.12, s32[1,32]{1,0:T(1,128)S(1)} %bitcast.11, ...), custom_call_target="tpu_custom_call" | custom-call | flops 17179869184 | bytes 1048576 | tf_op jit(solution)/shard_map/analyse_grid/pallas_call | solution.py:437
  2.3 15.3 %all_to_all.10.parts_ref = f32[32,8,128]{2,1,0:T(8,128)S(1)} all-to-all(f32[32,8,128]{2,1,0:T(8,128)S(1)} %analyse_grid.1), channel_id=1, replica_groups=mesh['band'=8,'lon'=4] {'band','lon'}, dimensions={0} | all-to-all | bytes 262144 | tf_op jit(solution)/shard_map/all_to_all | solution.py:447
  17.6 0.3 collective-permute-start.1
  17.9 0.5 %own_tables.1 = (s32[128,128]{1,0:T(8,128)S(1)}, f32[2,8,8,128]{3,2,1,0:T(8,128)S(1)}, bf16[2,128,1024]{2,1,0:T(8,128)(2,1)S(1)}) custom-call(s32[8,128]{1,0:T(8,128)S(1)} %bitcast.7, bf16[2,8,8,128]{3,2,1,0:T(8,128)(2,1)S(1)} %add_points.1.after_ref.own_ref), custom_call_target="tpu_custom_call" | custom-call | flops 67108864 | bytes 1048576 | tf_op jit(solution)/shard_map/own_tables/pallas_call | solution.py:460
  18.3 0.5 %collective-permute-done.1.other_ref = bf16[2,8,8,128]{3,2,1,0:T(8,128)(2,1)S(1)} collective-permute-done((bf16[2,8,8,128]{3,2,1,0:T(8,128)(2,1)S(1)}, bf16[2,8,8,128]{3,2,1,0:T(8,128)(2,1)S(1)}, u32[]{:S(2)}, u32[]{:S(2)}) %collective-permute-start.1) | collective-permute-done | bytes 32800 | tf_op jit(solution)/shard_map/ppermute | solution.py:455
  18.9 0.0 copy-done.1
  18.9 0.0 copy-done.3
  18.9 1.7 %spectral.1 = bf16[32,16,128]{2,1,0:T(8,128)(2,1)S(1)} custom-call(bf16[256,128]{1,0:T(8,128)(2,1)S(1)} %get-tuple-element.15.after_ref.pick_ref, bf16[4,128,256]{2,1,0:T(8,128)(2,1)S(1)} %get-tuple-element.16.put_ref, s32[128,128]{1,0:T(8,128)S(1)} %get-tuple-element.18.rows_ref, bf16[2,8,8,128]{3,2,1,0:T(8,128)(2,1)S(1)} %add_points.1.after_ref.own_ref, ...), custom_call_target="tpu_custom_call" | custom-call | flops 2147483648 | bytes 1048576 | tf_op jit(solution)/shard_map/spectral/pallas_call | solution.py:469
  20.6 10.0 %all_to_all.11.values_ref = bf16[32,16,128]{2,1,0:T(8,128)(2,1)S(1)} all-to-all(bf16[32,16,128]{2,1,0:T(8,128)(2,1)S(1)} %spectral.1), channel_id=1, replica_groups=mesh['band'=8,'lon'=4] {'band','lon'}, dimensions={0} | all-to-all | bytes 262144 | tf_op jit(solution)/shard_map/all_to_all | solution.py:479
  30.6 0.3 collective-permute-start.2
  30.9 0.5 %other_tables.1 = (f32[2,8,8,128]{3,2,1,0:T(8,128)S(1)}, bf16[2,128,1024]{2,1,0:T(8,128)(2,1)S(1)}) custom-call(s32[8,128]{1,0:T(8,128)S(1)} %bitcast.8, f32[8,16,128]{2,1,0:T(8,128)S(1)} %add_degrees.1.after_ref.value_ref), custom_call_target="tpu_custom_call" | custom-call | flops 1048576 | bytes 1048576 | tf_op jit(solution)/shard_map/other_tables/pallas_call | solution.py:490
  31.3 0.5 %own_grid.1.grid_ref = f32[128,128]{1,0:T(8,128)S(1)} custom-call(f32[2,8,8,128]{3,2,1,0:T(8,128)S(1)} %get-tuple-element.21.turn_ref, bf16[2,128,1024]{2,1,0:T(8,128)(2,1)S(1)} %get-tuple-element.22.basis_ref, f32[8,16,128]{2,1,0:T(8,128)S(1)} %add_degrees.1.after_ref.value_ref), custom_call_target="tpu_custom_call" | custom-call | flops 1048576 | bytes 1048576 | tf_op jit(solution)/shard_map/own_grid/pallas_call | solution.py:491
  31.8 0.1 collective-permute-done.2.value_ref
  31.9 1.2 %synthesise_grid.1 = f32[2,2,4,1024]{3,2,1,0:T(4,128)} custom-call(f32[2,8,8,128]{3,2,1,0:T(8,128)S(1)} %get-tuple-element.19.turn_ref, bf16[2,128,1024]{2,1,0:T(8,128)(2,1)S(1)} %get-tuple-element.20.basis_ref, f32[8,16,128]{2,1,0:T(8,128)S(1)} %collective-permute-done.2.value_ref, f32[128,128]{1,0:T(8,128)S(1)} %own_grid.1.grid_ref), custom_call_target="tpu_custom_call" | custom-call | flops 1073741824 | bytes 1048576 | tf_op jit(solution)/shard_map/synthesise_grid/pallas_call | solution.py:494
  (3 shorter events, 0.0 us)
Async XLA Ops:
  0.0 0.7 %copy-start = (s32[1024]{0:T(1024)S(1)}, s32[1024]{0:T(1024)}, u32[]{:S(2)}) copy-start(s32[1024]{0:T(1024)} %param.10) | copy-start | bytes 12292
  0.0 1.6 %collective-permute-start = (f32[2,2,4,1024]{3,2,1,0:T(4,128)}, f32[2,2,4,1024]{3,2,1,0:T(4,128)S(1)}, u32[]{:S(2)}, u32[]{:S(2)}) collective-permute-start(f32[2,2,4,1024]{3,2,1,0:T(4,128)} %refs_0_.1), channel_id=1, source_target_pairs={{0,1},{1,0},{2,3},{3,2},{4,5},{5,4},{6,7},{7,6},{8,9},{9,8},{10,11... | collective-permute-start | bytes 196616 | tf_op jit(solution)/shard_map/ppermute | solution.py:413
  0.7 0.7 %copy-start.4 = (s32[32]{0:T(128)S(1)}, s32[32]{0:T(128)}, u32[]{:S(2)}) copy-start(s32[32]{0:T(128)} %param.11) | copy-start | bytes 388
  0.7 0.9 %copy-start.2 = (f32[2,2,4,1024]{3,2,1,0:T(4,128)S(1)}, f32[2,2,4,1024]{3,2,1,0:T(4,128)}, u32[]{:S(2)}) copy-start(f32[2,2,4,1024]{3,2,1,0:T(4,128)} %refs_0_.1) | copy-start | bytes 196612
  0.7 0.9 %copy-start.5 = (f32[32]{0:T(128)S(1)}, f32[32]{0:T(128)}, u32[]{:S(2)}) copy-start(f32[32]{0:T(128)} %param.9) | copy-start | bytes 388
  1.6 17.2 %copy-start.1 = (bf16[128,256,32]{1,2,0:T(8,128)(2,1)S(1)}, bf16[128,256,32]{1,2,0:T(8,128)(2,1)}, u32[]{:S(2)}) copy-start(bf16[128,256,32]{1,2,0:T(8,128)(2,1)} %param.7) | copy-start | bytes 6291460
  1.6 17.2 %copy-start.3 = (f32[2,2,256]{2,1,0:T(2,128)S(1)}, f32[2,2,256]{2,1,0:T(2,128)}, u32[]{:S(2)}) copy-start(f32[2,2,256]{2,1,0:T(2,128)} %love_ref.1) | copy-start | bytes 12292
  17.6 1.3 %collective-permute-start.1 = (bf16[2,8,8,128]{3,2,1,0:T(8,128)(2,1)S(1)}, bf16[2,8,8,128]{3,2,1,0:T(8,128)(2,1)S(1)}, u32[]{:S(2)}, u32[]{:S(2)}) collective-permute-start(bf16[2,8,8,128]{3,2,1,0:T(8,128)(2,1)S(1)} %add_points.1.after_ref.own_ref), channel_id=1, source_target_pairs={{0,1},{1,0},{2,3},{3,2},{4,5},{5,4},{6,7},{7,6},{8,9},{9,8},{10,11... | collective-permute-start | bytes 98312 | tf_op jit(solution)/shard_map/ppermute | solution.py:455
  30.6 1.3 %collective-permute-start.2 = (f32[8,16,128]{2,1,0:T(8,128)S(1)}, f32[8,16,128]{2,1,0:T(8,128)S(1)}, u32[]{:S(2)}, u32[]{:S(2)}) collective-permute-start(f32[8,16,128]{2,1,0:T(8,128)S(1)} %add_degrees.1.after_ref.value_ref), channel_id=1, source_target_pairs={{0,1},{1,0},{2,3},{3,2},{4,5},{5,4},{6,7},{7,6},{8,9},{9,8},{10,11... | collective-permute-start | bytes 196616 | tf_op jit(solution)/shard_map/ppermute | solution.py:488

commit v8 on v7

--- a/solution.py
+++ b/solution.py
@@ -47,8 +47,8 @@
     return lax.dot_general(a, b, NT, preferred_element_type=jnp.float32)
 
 
-def analyse_grid(total, after_ref, right_ref, turn_ref, weight_ref, cycle_ref, *refs):
-    del after_ref
+def analyse_grid(total, after_ref, also_after_ref, right_ref, turn_ref, weight_ref, cycle_ref, *refs):
+    del after_ref, also_after_ref
     parts, out_ref, points_ref, mid_ref = refs[:-3], refs[-3], refs[-2], refs[-1]
     cycles = parts[0].shape[2]
     blocks = parts[0].shape[3] // LANES
@@ -157,7 +157,6 @@
 def cycle_tables(owners, cycles, after_ref, cycle_ref, pick_ref, put_ref):
     del after_ref
     northern = owners * cycles
-    wide = put_ref.shape[2]
     lane = iota((1, LANES), 1)
 
     listed = jnp.broadcast_to(cycle_ref[...].astype(jnp.float32), (LANES, northern)).astype(jnp.bfloat16)
@@ -178,97 +177,103 @@
     part = iota((LANES, LANES), 0) // cycles % 4
     for i in range(4):
         put = jnp.where(found & (part == i), 1.0, 0.0)
-        put_ref[i] = jnp.concatenate([put] * (wide // LANES), axis=1).astype(jnp.bfloat16)
-
-
-def half_tables(which, total, orders_ref, turn_ref, basis_ref):
+        put_ref[i // 2, :, i % 2 * LANES : (i % 2 + 1) * LANES] = put.astype(jnp.bfloat16)
+
+
+def inverse_tables(total, orders_ref, after_ref, rows_ref, turn_ref, basis_ref):
+    del after_ref
     owners, per_owner = orders_ref.shape
     blocks = turn_ref.shape[2]
-    share, quarter = per_owner // 2, per_owner // 4
+    quarter = per_owner // 4
     lon = lax.axis_index("lon")
-    lane = iota((1, LANES), 1)
-    first_lanes = lane < share
-    slot = lane // quarter
-
+    own = orders_ref[pl.ds(lax.axis_index("band"), 1), :].astype(jnp.float32)
+    rows_ref[...] = jnp.transpose(jnp.broadcast_to(own, (LANES, per_owner))).astype(jnp.int32)
+
+    slot = iota((1, LANES), 1) // quarter
     orders = orders_ref[...]
-    moved = [orders] + [pltpu.roll(orders, quarter * i, 1) for i in range(1, 4)]
-    even = [moved[0], moved[3], moved[2], moved[1]]
-    odd = [moved[3], moved[2], moved[1], moved[0]]
-    doubled = jnp.zeros_like(orders)
-    for i in range(4):
-        doubled = jnp.where(slot == i, jnp.where(which == 0, even[i], odd[i]), doubled)
-
+    ahead, behind = pltpu.roll(orders, LANES - quarter, 1), pltpu.roll(orders, quarter, 1)
+    arranged = jnp.where(slot == 1, ahead, jnp.where(slot == 2, behind, orders))
     scale = 1.0 / math.sqrt(total)
-    back = jnp.where(first_lanes, 0, total - total // 4)
     for b in range(owners):
-        order = doubled[b : b + 1]
+        order = arranged[b : b + 1]
         factor = jnp.where(order == 0, scale, 2.0 * scale)
         step = iota((blocks, per_owner), 0) + lon * blocks
-        cos_a, sin_a = turn((step * LANES * order) & (total - 1), total)
-        turn_ref[0, b] = jnp.where(first_lanes, cos_a, -cos_a) * factor
-        turn_ref[1, b] = -sin_a * factor
-        fine = turn((iota((ROWS, per_owner), 0) * order + back) & (total - 1), total)
+        for c, table in enumerate(turn((step * LANES * order) & (total - 1), total)):
+            turn_ref[c, b] = table * factor
+        fine = turn(iota((ROWS, per_owner), 0) * order, total)
         coarse = turn((iota((LANES // ROWS, per_owner), 0) * ROWS * order) & (total - 1), total)
         kept = []
-        for k in range(LANES // ROWS):
-            value = fine[0] * coarse[0][k : k + 1] - fine[1] * coarse[1][k : k + 1]
-            kept.append(split(value))
+        for k, pair in enumerate(products(fine, coarse)):
+            kept.append([split(table) for table in pair])
             if k % 2 == 1:
                 rows = slice((k - 1) * ROWS, (k + 1) * ROWS)
-                for i in range(2):
-                    both = jnp.concatenate([kept[k - 1][i], kept[k][i]], axis=0)
-                    basis_ref[i, rows, b * per_owner : (b + 1) * per_owner] = both
-
-
-def own_tables(total, orders_ref, after_ref, rows_ref, turn_ref, basis_ref):
-    del after_ref
-    per_owner = orders_ref.shape[1]
-    own = orders_ref[pl.ds(lax.axis_index("band"), 1), :].astype(jnp.float32)
-    rows_ref[...] = jnp.transpose(jnp.broadcast_to(own, (LANES, per_owner))).astype(jnp.int32)
-    half_tables(lax.axis_index("lon") % 2, total, orders_ref, turn_ref, basis_ref)
-
-
-def other_tables(total, orders_ref, after_ref, turn_ref, basis_ref):
-    del after_ref
-    half_tables(1 - lax.axis_index("lon") % 2, total, orders_ref, turn_ref, basis_ref)
+                for c in range(2):
+                    at = (c * owners + b) * per_owner
+                    for i in range(2):
+                        both = jnp.concatenate([kept[k - 1][c][i], kept[k][c][i]], axis=0)
+                        basis_ref[i, rows, at : at + per_owner] = both
 
 
 def spectral(
-    pick_ref, put_ref, rows_ref, own_ref, other_ref, legendre_ref, love_ref, out_ref, spread_ref, kept_ref
+    pick_ref,
+    put_ref,
+    rows_ref,
+    folded_ref,
+    own_table_ref,
+    other_table_hbm,
+    own_love_ref,
+    other_love_ref,
+    out_ref,
+    spread_ref,
+    kept_ref,
+    partial_ref,
+    other_table_ref,
+    landed,
 ):
-    parts, owners, height = own_ref.shape[:3]
+    parts, owners, height = folded_ref.shape[:3]
     quarter = rows_ref.shape[0] // (2 * parts)
-    degrees = legendre_ref.shape[1]
+    degrees = own_table_ref.shape[1]
     northern = owners * height // 2
     group = degrees // northern
     wide = group * northern
     lon = lax.axis_index("lon")
     side = lon % 2
 
+    span = quarter * northern
+    copies = []
+    for q in range(parts):
+        start = pl.multiple_of((2 * q + side) * span, span)
+        source = other_table_hbm.at[pl.ds(start, span)]
+        copies.append(pltpu.make_async_copy(source, other_table_ref.at[q * span : (q + 1) * span], landed.at[q]))
+        copies[q].start()
+
     pad = jnp.zeros((LANES - 2 * northern, LANES), jnp.float32)
     turned = []
-    for folded_ref in (own_ref, other_ref):
-        for q in range(parts):
-            pieces = [folded_ref[q, b].astype(jnp.float32) for b in range(owners)]
-            turned.append(jnp.transpose(jnp.concatenate(pieces + [pad], axis=0)))
+    for q in range(parts):
+        pieces = [folded_ref[q, b].astype(jnp.float32) for b in range(owners)]
+        turned.append(jnp.transpose(jnp.concatenate(pieces + [pad], axis=0)))
     spread_ref[...] = dot_nt(jnp.concatenate(turned, axis=0).astype(jnp.bfloat16), pick_ref[...])
 
-    degree = lon * degrees + iota((ROWS, degrees), 1)
+    lane = iota((ROWS, degrees), 1)
+    degree = [lon * degrees + lane, (lon + 1 - 2 * side) * degrees + lane]
+    love = [[[ref[g, f : f + 1, :] for f in range(2)] for g in range(2)] for ref in (own_love_ref, other_love_ref)]
     diagonal = iota((ROWS, wide), 0) == iota((ROWS, wide), 1) // northern
-    love = [[love_ref[g, f : f + 1, :] for f in range(2)] for g in range(2)]
-    groups = 2 * parts * quarter // group
-
-    def place(n):
+    across = LANES // northern
+    upper = iota((ROWS, LANES), 0) < across
+    folded_diagonal = iota((ROWS, LANES), 0) % across == iota((ROWS, LANES), 1) // northern
+    groups = parts * quarter // group
+
+    def first_order(n):
         q, first = n * group // quarter, n * group % quarter
-        taken = side if q < parts else 1 - side
-        return q, first, (2 * (q % parts) + taken) * quarter + first
-
-    def table(n):
-        start = pl.multiple_of(place(n)[2] * northern, wide)
-        return legendre_ref[pl.ds(start, wide)]
-
-    def analyse(n):
-        q, first, _ = place(n)
+        return (2 * q + side) * quarter + first
+
+    def table(n, d):
+        if d == 0:
+            return own_table_ref[pl.ds(pl.multiple_of(first_order(n) * northern, wide), wide)]
+        return other_table_ref[n * wide : (n + 1) * wide]
+
+    def spread(n):
+        q, first = n * group // quarter, n * group % quarter
         left = []
         for f in range(2):
             for p in range(2):
@@ -276,11 +281,11 @@
                     at = q * LANES + (f * 2 + c) * quarter + first
                     piece = spread_ref[at : at + group, p * LANES : (p + 1) * LANES]
                     left.append(jnp.where(diagonal, jnp.concatenate([piece] * (wide // LANES), axis=1), 0.0))
-        return dot(jnp.concatenate(left, axis=0).astype(jnp.bfloat16), table(n))
-
-    def respond(n, analysed):
-        order = rows_ref[pl.ds(pl.multiple_of(place(n)[2], group), group)]
-        gap = degree - jnp.concatenate([order] * (degrees // LANES), axis=1)
+        return jnp.concatenate(left, axis=0).astype(jnp.bfloat16)
+
+    def respond(n, d, analysed):
+        order = rows_ref[pl.ds(pl.multiple_of(first_order(n), group), group)]
+        gap = degree[d] - jnp.concatenate([order] * (degrees // LANES), axis=1)
         valid = gap >= 0
         keep = [valid & ((gap & 1) == p) for p in range(2)]
         mixed = []
@@ -289,77 +294,82 @@
                 for c in range(2):
                     lo = (p * 2 + c) * group
                     hi = ((2 + p) * 2 + c) * group
-                    value = love[g][0] * analysed[lo : lo + group] + love[g][1] * analysed[hi : hi + group]
+                    value = love[d][g][0] * analysed[lo : lo + group] + love[d][g][1] * analysed[hi : hi + group]
                     mixed.append(jnp.where(keep[p], value, 0.0))
-        return dot_nt(jnp.concatenate(mixed, axis=0).astype(jnp.bfloat16), table(n))
+        return dot_nt(jnp.concatenate(mixed, axis=0).astype(jnp.bfloat16), table(n, d))
 
     def keep_pair(n, halves):
         for g in range(2):
             for c in range(2):
                 lo, hi = (g * 4 + c) * group, (g * 4 + 2 + c) * group
-                rows = [(half[lo : lo + group], half[hi : hi + group]) for half in halves]
-                share = parts * quarter
-                at = (n * group // share * 2 + c) * share + n * group % share
+                at = c * parts * quarter + n * group
+                rows = []
+                for half in halves:
+                    even, odd = half[lo : lo + group], half[hi : hi + group]
+                    even = jnp.where(upper, even[:, :LANES], even[:, LANES:])
+                    odd = jnp.where(upper, odd[:, :LANES], odd[:, LANES:])
+                    rows.append([jnp.where(folded_diagonal, x, 0.0) for x in (even + odd, even - odd)])
                 for h in range(2):
-                    both = [even + odd if h == 0 else even - odd for even, odd in rows]
-                    both = [jnp.where(diagonal, value, 0.0) for value in both]
-                    kept_ref[g * 2 + h, at : at + 2 * group, :] = jnp.concatenate(both, axis=0).astype(jnp.bfloat16)
-
+                    both = jnp.concatenate([row[h] for row in rows], axis=0).astype(jnp.bfloat16)
+                    kept_ref[g, at : at + 2 * group, h * LANES : (h + 1) * LANES] = both
+
+    steps = [(n, d) for d in range(2) for n in range(groups)]
+    height = 8 * group
     analysed, partial = {}, {}
-    for n in range(groups + 2):
-        if n < groups:
-            analysed[n] = analyse(n)
-        if 1 <= n <= groups:
-            partial[n - 1] = respond(n - 1, analysed.pop(n - 1))
-        if n >= 3 and n % 2 == 1:
-            keep_pair(n - 3, [partial.pop(n - 3), partial.pop(n - 2)])
-
-    total = None
-    for i in range(4):
-        term = dot_nt(put_ref[i], kept_ref[i])
-        total = term if total is None else total + term
+    for i in range(len(steps) + 2):
+        if i < len(steps):
+            n, d = steps[i]
+            if d == 1 and n * group % quarter == 0:
+                copies[n * group // quarter].wait()
+            analysed[i] = dot(spread(n), table(n, d))
+        if 1 <= i <= len(steps):
+            n, d = steps[i - 1]
+            value = respond(n, d, analysed.pop(i - 1))
+            if d == 0:
+                partial_ref[n * height : (n + 1) * height] = value
+            else:
+                partial[n] = partial_ref[n * height : (n + 1) * height] + value
+        if i > groups + 2 and (i - groups) % 2 == 1:
+            n = i - groups - 3
+            keep_pair(n, [partial.pop(n), partial.pop(n + 1)])
+
+    total = dot_nt(put_ref[0], kept_ref[0]) + dot_nt(put_ref[1], kept_ref[1])
     total = total.astype(out_ref.dtype)
     lon_count = out_ref.shape[0] // owners
-    rows, lanes = out_ref.shape[1:]
+    rows = out_ref.shape[1]
     for b in range(owners):
-        for q in range(0, lon_count, 2):
-            out_ref[b * lon_count + q + side] = total[b * rows : (b + 1) * rows, :lanes]
-            out_ref[b * lon_count + q + 1 - side] = total[b * rows : (b + 1) * rows, lanes:]
-
-
-def add_degrees(lon_count, values_ref, out_ref):
-    for b in range(out_ref.shape[0]):
-        value = values_ref[b * lon_count].astype(jnp.float32)
-        for q in range(1, lon_count):
-            value = value + values_ref[b * lon_count + q].astype(jnp.float32)
-        out_ref[b] = value
-
-
-def half_grid(turn_ref, basis_ref, value_ref, left_ref):
-    owners, rows, lanes = value_ref.shape
-    blocks = turn_ref.shape[2]
+        for q in range(lon_count):
+            out_ref[b * lon_count + q] = total[b * rows : (b + 1) * rows]
+
+
+def synthesise_grid(turn_ref, basis_ref, values_ref, out_ref, left_ref):
+    owners, blocks, per_owner = turn_ref.shape[1:]
+    lon_count = values_ref.shape[0] // owners
+    rows = values_ref.shape[1]
+    cycles = out_ref.shape[2]
+    count = owners * per_owner
     height = blocks * rows
+    first_lanes = iota((1, LANES), 1) < per_owner // 2
     for b in range(owners):
-        value = value_ref[b]
-        other = pltpu.roll(value, lanes // 2, 1)
+        halves = []
+        for c in range(2):
+            value = values_ref[b * lon_count + c].astype(jnp.float32)
+            for q in range(c + 2, lon_count, 2):
+                value = value + values_ref[b * lon_count + q].astype(jnp.float32)
+            halves.append(value)
+        re = jnp.where(first_lanes, halves[0], pltpu.roll(halves[1], per_owner // 2, 1))
+        im = jnp.where(first_lanes, pltpu.roll(halves[0], per_owner // 2, 1), halves[1])
+        at = b * per_owner
         for a in range(blocks):
-            term = value * turn_ref[0, b, a : a + 1] + other * turn_ref[1, b, a : a + 1]
-            high, low = split(term)
-            left_ref[a * rows : (a + 1) * rows, b * lanes : (b + 1) * lanes] = high
-            left_ref[height + a * rows : height + (a + 1) * rows, b * lanes : (b + 1) * lanes] = low
+            ca, sa = turn_ref[0, b, a : a + 1], turn_ref[1, b, a : a + 1]
+            for c, term in ((0, ca * re - sa * im), (1, -(sa * re + ca * im))):
+                high, low = split(term)
+                lanes = slice(c * count + at, c * count + at + per_owner)
+                left_ref[a * rows : (a + 1) * rows, lanes] = high
+                left_ref[height + a * rows : height + (a + 1) * rows, lanes] = low
     grid = dot_nt(left_ref[...], basis_ref[0])
-    return grid[:height] + grid[height:] + dot_nt(left_ref[:height], basis_ref[1])
-
-
-def own_grid(turn_ref, basis_ref, value_ref, out_ref, left_ref):
-    out_ref[...] = half_grid(turn_ref, basis_ref, value_ref, left_ref)
-
-
-def synthesise_grid(turn_ref, basis_ref, value_ref, grid_ref, out_ref, left_ref):
-    rows = value_ref.shape[1]
-    cycles = out_ref.shape[2]
-    grid = grid_ref[...] + half_grid(turn_ref, basis_ref, value_ref, left_ref)
-    for a in range(grid.shape[0] // rows):
+    grid = grid[:height] + grid[height:] + dot_nt(left_ref[:height], basis_ref[1])
+    for a in range(blocks):
         for g in range(2):
             for h in range(2):
                 at = a * rows + (g * 2 + h) * cycles
@@ -410,7 +420,10 @@
         )
 
     partner = [(i, i ^ 1) for i in range(lon_count)]
+    rows = jnp.transpose(legendre, (0, 2, 1)).reshape(per_owner * northern, degrees)
     parts = [loads, lax.ppermute(loads, "lon", partner)]
+    other_rows = lax.ppermute(rows, "lon", partner)
+    other_love = lax.ppermute(love, "lon", partner)
     count = 2 * blocks
     width = owners * per_owner // 2
     opened = kernel(opening, jax.ShapeDtypeStruct((ROWS, LANES), jnp.float32), [], [], 1 << 34)()
@@ -424,26 +437,37 @@
         [],
         1 << 31,
     )(table, opened)
+    order_rows, turns, basis = kernel(
+        functools.partial(inverse_tables, total),
+        (
+            jax.ShapeDtypeStruct((per_owner, LANES), jnp.int32),
+            jax.ShapeDtypeStruct((2, owners, blocks, per_owner), jnp.float32),
+            jax.ShapeDtypeStruct((2, LANES, 2 * owners * per_owner), jnp.bfloat16),
+        ),
+        [vmem, vmem],
+        [],
+        1 << 28,
+    )(table, first)
     pick, put = kernel(
         functools.partial(cycle_tables, owners, cycles),
         (
             jax.ShapeDtypeStruct((2 * LANES, LANES), jnp.bfloat16),
-            jax.ShapeDtypeStruct((4, LANES, degrees), jnp.bfloat16),
+            jax.ShapeDtypeStruct((2, LANES, 2 * LANES), jnp.bfloat16),
         ),
         [vmem, vmem],
         [],
         1 << 28,
-    )(first, cycle_list)
+    )(order_rows, cycle_list)
     sums = kernel(
         functools.partial(analyse_grid, total),
         jax.ShapeDtypeStruct((devices, 2 * cycles, LANES), jnp.float32),
-        [vmem] * (5 + len(parts)),
+        [vmem] * (6 + len(parts)),
         [
             pltpu.VMEM((count * 4 * cycles, LANES), jnp.float32),
             pltpu.VMEM((count * 4 * cycles, 2 * width), jnp.float32),
         ],
         1 << 34,
-    )(pick, right, first, cycle_weight.reshape(1, northern), cycle_list, *parts)
+    )(pick, other_love, right, first, cycle_weight.reshape(1, northern), cycle_list, *parts)
     arrived = lax.all_to_all(sums, everyone, split_axis=0, concat_axis=0, tiled=True)
     folded = kernel(
         add_points,
@@ -452,48 +476,28 @@
         [],
         1 << 28,
     )(arrived)
-    others = lax.ppermute(folded, "lon", partner)
-    halves = (
-        jax.ShapeDtypeStruct((2, owners, blocks, per_owner), jnp.float32),
-        jax.ShapeDtypeStruct((2, LANES, owners * per_owner), jnp.bfloat16),
-    )
-    order_rows, own_turns, own_basis = kernel(
-        functools.partial(own_tables, total),
-        (jax.ShapeDtypeStruct((per_owner, LANES), jnp.int32), *halves),
-        [vmem, vmem],
-        [],
-        1 << 26,
-    )(table, folded)
-
-    rows = jnp.transpose(legendre, (0, 2, 1)).reshape(per_owner * northern, degrees)
     values = kernel(
         spectral,
         jax.ShapeDtypeStruct((devices, 4 * cycles, per_owner), jnp.bfloat16),
-        [vmem] * 7,
+        [vmem] * 5 + [pl.BlockSpec(memory_space=pl.ANY)] + [vmem] * 2,
         [
-            pltpu.VMEM((4 * LANES, 2 * LANES), jnp.float32),
-            pltpu.VMEM((4, 2 * per_owner, degrees), jnp.bfloat16),
+            pltpu.VMEM((2 * LANES, 2 * LANES), jnp.float32),
+            pltpu.VMEM((2, per_owner, 2 * LANES), jnp.bfloat16),
+            pltpu.VMEM((4 * per_owner, degrees), jnp.float32),
+            pltpu.VMEM((per_owner * northern // 2, degrees), jnp.bfloat16),
+            pltpu.SemaphoreType.DMA((2,)),
         ],
         1 << 31,
-    )(pick, put, order_rows, folded, others, rows, love)
+    )(pick, put, order_rows, folded, rows, other_rows, love, other_love)
     returned = lax.all_to_all(values, everyone, split_axis=0, concat_axis=0, tiled=True)
 
-    own = kernel(
-        functools.partial(add_degrees, lon_count),
-        jax.ShapeDtypeStruct((owners, 4 * cycles, per_owner), jnp.float32),
-        [vmem],
-        [],
-        1 << 28,
-    )(returned)
-    other = lax.ppermute(own, "lon", partner)
-    left = [pltpu.VMEM((2 * 4 * cycles * blocks, owners * per_owner), jnp.bfloat16)]
-    other_turns, other_basis = kernel(functools.partial(other_tables, total), halves, [vmem] * 2, [], 1 << 20)(table, own)
-    grid = kernel(
-        own_grid, jax.ShapeDtypeStruct((4 * cycles * blocks, LANES), jnp.float32), [vmem] * 3, left, 1 << 20
-    )(own_turns, own_basis, own)
-    return kernel(synthesise_grid, jax.ShapeDtypeStruct(loads.shape, jnp.float32), [vmem] * 4, left, 1 << 30)(
-        other_turns, other_basis, other, grid
-    )
+    return kernel(
+        synthesise_grid,
+        jax.ShapeDtypeStruct(loads.shape, jnp.float32),
+        [vmem] * 3,
+        [pltpu.VMEM((2 * 4 * cycles * blocks, 2 * owners * per_owner), jnp.bfloat16)],
+        1 << 31,
+    )(turns, basis, returned)
 
 
 def per_device(loads, legendre, love, cycle_weight, order_list, cycle_order):

time: 33.3 us -> 32.1 us (0.964)
  waiting for transfers between devices: 0.65 us -> 0.01 us
  Pallas kernels: 5.67 us -> 5.26 us
    pallas_call x4 -> x1, Pallas kernels: 1.47 us -> 0.66 us  [per_device_kernels(): kernel(functools.partial(inverse_tables, total), (jax.ShapeDtypeStruct((p...]
    ppermute x2, waiting for transfers between devices: 0.56 us -> 0.01 us  [the longest x1 0.01 us: per_device_kernels(): other_rows = lax.ppermute(rows, 'lon', partner)]
    ppermute x1, starting transfers between devices: 0.49 us -> 0.02 us  [per_device_kernels(): parts = [loads, lax.ppermute(loads, 'lon', partner)]]
    ppermute x2, starting transfers between devices: 0.56 us -> 0.99 us  [the longest x1 0.49 us: per_device_kernels(): other_rows = lax.ppermute(rows, 'lon', partner)]
  transfers between devices with their start and end apart: 3 -> 3, of which waited for: 3 -> 0; matrix products, arithmetic and copies ran while one was open for 0% -> 0% of each run, Pallas kernels for 6% -> 6%
where the time goes in v8:
time: 32.1 us; the launch traced here: 31.9 us
  blocking collectives  25.3 us (79%)
  Pallas kernels  5.26 us (16%)
  starting transfers between devices  1 us (3%)
    all_to_all x1, blocking collectives, per_device_kernels(): lax.all_to_all(sums, everyone, split_axis=0, concat_axis=0, tiled=True)  15.3 us
    all_to_all x1, blocking collectives, per_device_kernels(): lax.all_to_all(values, everyone, split_axis=0, concat_axis=0, tiled=True)  9.97 us
    pallas_call x1, Pallas kernels, per_device_kernels(): kernel(spectral, jax.ShapeDtypeStruct((devices, 4 * cycles, per_owner), j...  1.97 us
    pallas_call x1, Pallas kernels, per_device_kernels(): kernel(synthesise_grid, jax.ShapeDtypeStruct(loads.shape, jnp.float32), [...  1.37 us
    pallas_call x1, Pallas kernels, per_device_kernels(): kernel(functools.partial(inverse_tables, total), (jax.ShapeDtypeStruct((p...  0.66 us
  transfers between devices with their start and end apart: 3, of which 0 were waited for; matrix products, arithmetic and copies ran while one was open for 0% of the time, Pallas kernels for 6%

profile of v8, /device:TPU:0, one launch (start us, length us, event | category | flops | bytes accessed | tf_op | source)
XLA Modules:
  0.0 31.9 jit_solution(11026988447647610398)
XLA Ops:
  0.0 0.5 %collective-permute-start = (f32[2,2,256]{2,1,0:T(2,128)}, f32[2,2,256]{2,1,0:T(2,128)S(1)}, u32[]{:S(2)}, u32[]{:S(2)}) collective-permute-start(f32[2,2,256]{2,1,0:T(2,128)} %own_love_ref.1), channel_id=1, source_target_pairs={{0,1},{1,0},{2,3},{3,2},{4,5},{5,4},{6,7},{7,6},{8,9},{9,8},{10,11... | collective-permute-start | bytes 12296 | tf_op jit(solution)/shard_map/ppermute | solution.py:426
  0.5 0.0 collective-permute-start.1
  0.5 0.0 copy-start.2
  0.5 0.5 %collective-permute-start.2 = (bf16[4096,256]{1,0:T(8,128)(2,1)}, bf16[4096,256]{1,0:T(8,128)(2,1)S(1)}, u32[]{:S(2)}, u32[]{:S(2)}) collective-permute-start(bf16[4096,256]{1,0:T(8,128)(2,1)} %bitcast.6), channel_id=1, source_target_pairs={{0,1},{1,0},{2,3},{3,2},{4,5},{5,4},{6,7},{7,6},{8,9},{9,8},{10,11... | collective-permute-start | bytes 6291464 | tf_op jit(solution)/shard_map/ppermute | solution.py:425
  1.0 0.2 copy-done.2
  1.2 0.0 copy-start.4
  1.2 0.0 copy-start.1
  1.2 0.0 copy-start.5
  1.2 0.4 %forward_tables.1 = (bf16[384,1024]{1,0:T(8,128)(2,1)S(1)}, f32[2,16,512]{2,1,0:T(8,128)S(1)}) custom-call(s32[8,128]{1,0:T(8,128)S(1)} %bitcast.8, f32[8,128]{1,0:T(8,128)S(1)} %opening.1.after_ref), custom_call_target="tpu_custom_call" | custom-call | flops 2147483648 | bytes 1048576 | tf_op jit(solution)/shard_map/forward_tables/pallas_call | solution.py:430
  1.7 0.7 %inverse_tables.1 = (s32[128,128]{1,0:T(8,128)S(1)}, f32[2,8,8,128]{3,2,1,0:T(8,128)S(1)}, bf16[2,128,2048]{2,1,0:T(8,128)(2,1)S(1)}) custom-call(s32[8,128]{1,0:T(8,128)S(1)} %bitcast.9, f32[2,16,512]{2,1,0:T(8,128)S(1)} %get-tuple-element.12.after_ref.turn_ref), custom_call_target="tpu_custom_call" | custom-call | flops 268435456 | bytes 1048576 | tf_op jit(solution)/shard_map/inverse_tables/pallas_call | solution.py:440
  2.3 0.0 copy-done.4
  2.3 0.2 cycle_tables.1
  2.5 0.0 collective-permute-done.also_after_ref.other_love_ref
  2.5 0.0 collective-permute-done.1.refs_1_
  2.5 0.0 copy-done.1
  2.5 0.0 copy-done.5
  2.6 0.0 copy-start
  2.6 0.0 copy-start.3
  2.6 0.6 %analyse_grid.1 = f32[32,8,128]{2,1,0:T(8,128)S(1)} custom-call(bf16[256,128]{1,0:T(8,128)(2,1)S(1)} %get-tuple-element.16.after_ref.pick_ref, f32[2,2,256]{2,1,0:T(2,128)S(1)} %collective-permute-done.also_after_ref.other_love_ref, bf16[384,1024]{1,0:T(8,128)(2,1)S(1)} %get-tuple-element.18.right_ref, ...), custom_call_target="tpu_custom_call" | custom-call | flops 17179869184 | bytes 1048576 | tf_op jit(solution)/shard_map/analyse_grid/pallas_call | solution.py:461
  3.2 15.3 %all_to_all.10.parts_ref = f32[32,8,128]{2,1,0:T(8,128)S(1)} all-to-all(f32[32,8,128]{2,1,0:T(8,128)S(1)} %analyse_grid.1), channel_id=1, replica_groups=mesh['band'=8,'lon'=4] {'band','lon'}, dimensions={0} | all-to-all | bytes 262144 | tf_op jit(solution)/shard_map/all_to_all | solution.py:471
  18.6 0.0 collective-permute-done.2.other_table_hbm
  18.6 0.0 copy-done
  18.6 0.0 copy-done.3
  18.6 2.0 %spectral.1 = bf16[32,16,128]{2,1,0:T(8,128)(2,1)S(1)} custom-call(bf16[256,128]{1,0:T(8,128)(2,1)S(1)} %get-tuple-element.16.after_ref.pick_ref, bf16[2,128,256]{2,1,0:T(8,128)(2,1)S(1)} %get-tuple-element.17.put_ref, s32[128,128]{1,0:T(8,128)S(1)} %get-tuple-element.15.after_ref.rows_ref, bf16[2,8,8,128]{3,2,1,0:T(8,128)(2,1)S(1)} %add_points.1.folded_ref, ...), custom_call_target="tpu_custom_call" | custom-call | flops 2147483648 | bytes 1048576 | tf_op jit(solution)/shard_map/spectral/pallas_call | solution.py:479
  20.6 10.0 %all_to_all.11.values_ref = bf16[32,16,128]{2,1,0:T(8,128)(2,1)S(1)} all-to-all(bf16[32,16,128]{2,1,0:T(8,128)(2,1)S(1)} %spectral.1), channel_id=1, replica_groups=mesh['band'=8,'lon'=4] {'band','lon'}, dimensions={0} | all-to-all | bytes 262144 | tf_op jit(solution)/shard_map/all_to_all | solution.py:492
  30.5 1.4 %synthesise_grid.1 = f32[2,2,4,1024]{3,2,1,0:T(4,128)} custom-call(f32[2,8,8,128]{3,2,1,0:T(8,128)S(1)} %get-tuple-element.13.turn_ref, bf16[2,128,2048]{2,1,0:T(8,128)(2,1)S(1)} %get-tuple-element.14.basis_ref, bf16[32,16,128]{2,1,0:T(8,128)(2,1)S(1)} %all_to_all.11.values_ref), custom_call_target="tpu_custom_call" | custom-call | flops 2147483648 | bytes 1048576 | tf_op jit(solution)/shard_map/synthesise_grid/pallas_call | solution.py:494
  (2 shorter events, 0.0 us)
Async XLA Ops:
  0.0 2.5 %collective-permute-start = (f32[2,2,256]{2,1,0:T(2,128)}, f32[2,2,256]{2,1,0:T(2,128)S(1)}, u32[]{:S(2)}, u32[]{:S(2)}) collective-permute-start(f32[2,2,256]{2,1,0:T(2,128)} %own_love_ref.1), channel_id=1, source_target_pairs={{0,1},{1,0},{2,3},{3,2},{4,5},{5,4},{6,7},{7,6},{8,9},{9,8},{10,11... | collective-permute-start | bytes 12296 | tf_op jit(solution)/shard_map/ppermute | solution.py:426
  0.5 2.0 %collective-permute-start.1 = (f32[2,2,4,1024]{3,2,1,0:T(4,128)}, f32[2,2,4,1024]{3,2,1,0:T(4,128)S(1)}, u32[]{:S(2)}, u32[]{:S(2)}) collective-permute-start(f32[2,2,4,1024]{3,2,1,0:T(4,128)} %refs_0_.1), channel_id=1, source_target_pairs={{0,1},{1,0},{2,3},{3,2},{4,5},{5,4},{6,7},{7,6},{8,9},{9,8},{10,11... | collective-permute-start | bytes 196616 | tf_op jit(solution)/shard_map/ppermute | solution.py:424
  0.5 0.7 %copy-start.2 = (s32[1024]{0:T(1024)S(1)}, s32[1024]{0:T(1024)}, u32[]{:S(2)}) copy-start(s32[1024]{0:T(1024)} %param.10) | copy-start | bytes 12292
  0.5 18.1 %collective-permute-start.2 = (bf16[4096,256]{1,0:T(8,128)(2,1)}, bf16[4096,256]{1,0:T(8,128)(2,1)S(1)}, u32[]{:S(2)}, u32[]{:S(2)}) collective-permute-start(bf16[4096,256]{1,0:T(8,128)(2,1)} %bitcast.6), channel_id=1, source_target_pairs={{0,1},{1,0},{2,3},{3,2},{4,5},{5,4},{6,7},{7,6},{8,9},{9,8},{10,11... | collective-permute-start | bytes 6291464 | tf_op jit(solution)/shard_map/ppermute | solution.py:425
  1.2 1.1 %copy-start.4 = (s32[32]{0:T(128)S(1)}, s32[32]{0:T(128)}, u32[]{:S(2)}) copy-start(s32[32]{0:T(128)} %param.11) | copy-start | bytes 388
  1.2 1.3 %copy-start.1 = (f32[2,2,4,1024]{3,2,1,0:T(4,128)S(1)}, f32[2,2,4,1024]{3,2,1,0:T(4,128)}, u32[]{:S(2)}) copy-start(f32[2,2,4,1024]{3,2,1,0:T(4,128)} %refs_0_.1) | copy-start | bytes 196612
  1.2 1.3 %copy-start.5 = (f32[32]{0:T(128)S(1)}, f32[32]{0:T(128)}, u32[]{:S(2)}) copy-start(f32[32]{0:T(128)} %param.9) | copy-start | bytes 388
  2.6 16.0 %copy-start = (bf16[128,256,32]{1,2,0:T(8,128)(2,1)S(1)}, bf16[128,256,32]{1,2,0:T(8,128)(2,1)}, u32[]{:S(2)}) copy-start(bf16[128,256,32]{1,2,0:T(8,128)(2,1)} %param.7) | copy-start | bytes 6291460
  2.6 16.0 %copy-start.3 = (f32[2,2,256]{2,1,0:T(2,128)S(1)}, f32[2,2,256]{2,1,0:T(2,128)}, u32[]{:S(2)}) copy-start(f32[2,2,256]{2,1,0:T(2,128)} %own_love_ref.1) | copy-start | bytes 12292
